TPU v7x, 512 devices: a whole 4x8x8 slice. The times are simulated.
512 devices in a mesh: dp: 32 (over x, z), expert: 16 (over y, core).
Axes of the slice: x: 4, y: 8, z: 8, core: 2. Of those that a mesh axis runs over, the one named last changes fastest.
Arguments:
- step_inputs: bfloat16 [65536, 2048], P(('dp', 'expert')), may hold values from -6 to 6
- step_cotangent: bfloat16 [65536, 2048], P(('dp', 'expert')), may hold values from -6 to 6
- step_routes: int32 [65536, 1], P(('dp', 'expert')), may hold values from 0 to 3; in each aligned block of 128 rows (0 to 127, 128 to 255, ...) at most 40 rows name the same one
- step_gates: float32 [65536, 1], P(('dp', 'expert')), may hold values from 0.1 to 1
- next_inputs: bfloat16 [65536, 2048], P(('dp', 'expert')), may hold values from -6 to 6
- next_routes: int32 [65536, 1], P(('dp', 'expert')), may hold values from 0 to 3; in each aligned block of 128 rows (0 to 127, 128 to 255, ...) at most 40 rows name the same one
- next_gates: float32 [65536, 1], P(('dp', 'expert')), may hold values from 0.1 to 1
- master_weights: float32 [16, 2048, 864], P('expert', 'dp'), may hold values from -4 to 4
- first_moment: float32 [16, 2048, 864], P('expert', 'dp'), may hold values from -0.6 to 0.6
- second_moment: float32 [16, 2048, 864], P('expert', 'dp'), may hold values from 0.01 to 0.2
- owner_plan: int32 [16], replicated, may hold values from 0 to 15, as said below
Outputs:
- layer_output: bfloat16 [65536, 2048], P(('dp', 'expert'))
- moved_weights: float32 [16, 2048, 864], P('expert', 'dp')
- moved_first: float32 [16, 2048, 864], P('expert', 'dp')
- moved_second: float32 [16, 2048, 864], P('expert', 'dp')
Inputs may be any that keep to these rules, and one draw needn't show every extreme that they name: `step_routes`: among the 128 tokens of one device no expert is named more than 40 times. `next_routes`: among the 128 tokens of one device no expert is named more than 40 times. `owner_plan`: every index appears once.
All inputs are finite; a program needn't handle non-finite values.
Results may differ from a plain program's by a relative error of at most 0.025.
Values may be sent and summed in bfloat16 or wider, within the bound.
No kernel may reach another device: no remote copies, remote signals or barrier semaphores. Data moves between devices by JAX's collectives and lax.ppermute only.
A program may use at most 64 MiB of HBM per device.

v0:
```python
import jax
import jax.numpy as jnp
from jax import lax
from jax.sharding import Mesh
from jax.sharding import PartitionSpec as P

D = 2048
HID = 1152
EXPERTS = 4
CAP = 40
DP = ("dp_0", "dp_1")
DP_EXPERT = ("dp_0", "dp_1", "expert")


beta_one = 0.9
beta_two = 0.95
learn_rate = 0.2
decay_rate = 0.1
adam_step = 10.0
adam_eps = 1e-08


def in_one_piece(arrays, axis, split_dim, concat_dim, along):
    widths = [a.shape[along] for a in arrays]
    both = jnp.concatenate(arrays, axis=along)
    filled = lax.all_to_all(both, axis, split_axis=split_dim, concat_axis=concat_dim, tiled=True)
    return tuple(jnp.split(filled, [sum(widths[:k]) for k in range(1, len(widths))], axis=along))


def laid_out(parts, dim):
    parts = jnp.moveaxis(parts, 0, dim)
    shape = parts.shape
    return parts.reshape(*shape[:dim], shape[dim] * shape[dim + 1], *shape[dim + 2 :])


def gather_in_order(value, axes, sequence):
    parts = value[None]
    for k in sequence:
        parts = lax.all_gather(parts, axes[k], axis=0, tiled=True)
    carried = [lax.axis_size(axes[k]) for k in reversed(sequence)]
    parts = parts.reshape(*carried, *value.shape)
    turned = sorted(range(len(sequence)), key=lambda place: sequence[len(sequence) - 1 - place])
    return parts.transpose(*turned, *range(len(sequence), parts.ndim)).reshape(-1, *value.shape)


def gather_axes(value, axes, sequence, dim):
    return laid_out(gather_in_order(value, axes, sequence), dim)


def own_rows(terms, axes):
    so_far = terms.astype(jnp.bfloat16)
    for axis in axes:
        so_far = lax.psum_scatter(so_far, axis, scatter_dimension=0, tiled=True)
    return so_far.astype(jnp.float32)


def slot_targets(routes, capacity):
    pair_ids = routes.reshape(-1)
    one_hot = (pair_ids[:, None] == jnp.arange(EXPERTS, dtype=jnp.int32)[None, :]).astype(jnp.int32)
    earlier = jnp.cumsum(one_hot, axis=0) - one_hot
    slot_ids = jnp.sum(earlier * one_hot, axis=1)
    return pair_ids * capacity + slot_ids


def dispatch_pairs(targets, payload, capacity):
    selector = (
        lax.broadcasted_iota(jnp.int32, (EXPERTS * capacity, targets.shape[0]), 0)
        == targets[None, :]
    ).astype(jnp.bfloat16)
    filled = jnp.dot(selector, payload, preferred_element_type=jnp.float32).astype(jnp.bfloat16)
    return filled.reshape(EXPERTS, capacity, payload.shape[1])


def shards(
    step_inputs,
    step_cotangent,
    step_routes,
    step_gates,
    next_inputs,
    next_routes,
    next_gates,
    master_weights,
    first_moment,
    second_moment,
    owner_plan,
):
    groups = lax.axis_size("expert")
    split = groups // EXPERTS
    width = master_weights.shape[2] // 3
    in_scale = D ** (-0.5)
    out_scale = HID ** (-0.5)
    topk_count = step_routes.shape[1]
    step_targets = slot_targets(step_routes, CAP)
    input_pairs = jnp.repeat(step_inputs, topk_count, axis=0)
    scaled_pairs = (
        jnp.repeat(step_cotangent, topk_count, axis=0).astype(jnp.float32) * step_gates
    ).astype(jnp.bfloat16)
    send_inputs = jnp.repeat(dispatch_pairs(step_targets, input_pairs, CAP), split, axis=0)
    send_scaled = jnp.repeat(dispatch_pairs(step_targets, scaled_pairs, CAP), split, axis=0)
    got_inputs, got_scaled = in_one_piece((send_inputs, send_scaled), "expert", 0, 0, 1)
    flat_inputs = got_inputs.reshape(-1, D)
    flat_scaled = got_scaled.reshape(-1, D)
    old_weights = master_weights[0]
    piece = gather_axes(old_weights.astype(jnp.bfloat16), DP, (0, 1), 0)
    inputs_part = flat_inputs
    scaled_part = flat_scaled
    gate_sum = jnp.dot(inputs_part, piece[:, :width], preferred_element_type=jnp.float32)
    up_sum = jnp.dot(inputs_part, piece[:, width : 2 * width], preferred_element_type=jnp.float32)
    down_sum = jnp.dot(scaled_part, piece[:, 2 * width :], preferred_element_type=jnp.float32)
    gate_sum, up_sum, down_sum = (gate_sum, up_sum, down_sum)
    gate_pre = gate_sum * in_scale
    up_pre = up_sum * in_scale
    down_back = down_sum * out_scale
    sigmoid_gate = jax.nn.sigmoid(gate_pre)
    silu_gate = gate_pre * sigmoid_gate
    activation = (silu_gate * up_pre).astype(jnp.bfloat16)
    gate_grad = (
        down_back * up_pre * sigmoid_gate * (1.0 + gate_pre * (1.0 - sigmoid_gate))
    ).astype(jnp.bfloat16)
    up_grad = (down_back * silu_gate).astype(jnp.bfloat16)
    inputs_part = flat_inputs
    scaled_part = flat_scaled
    contract = (((0,), (0,)), ((), ()))
    gate_part = (
        lax.dot_general(inputs_part, gate_grad, contract, preferred_element_type=jnp.float32)
        * in_scale
    )
    up_part = (
        lax.dot_general(inputs_part, up_grad, contract, preferred_element_type=jnp.float32)
        * in_scale
    )
    down_part = (
        lax.dot_general(scaled_part, activation, contract, preferred_element_type=jnp.float32)
        * out_scale
    )
    gradient = own_rows(jnp.concatenate([gate_part, up_part, down_part], axis=1), DP)
    first_new = beta_one * first_moment[0] + (1.0 - beta_one) * gradient
    second_new = beta_two * second_moment[0] + (1.0 - beta_two) * gradient * gradient
    first_hat = first_new / (1.0 - beta_one**adam_step)
    second_hat = second_new / (1.0 - beta_two**adam_step)
    new_weights = old_weights - learn_rate * (
        first_hat / (jnp.sqrt(second_hat) + adam_eps) + decay_rate * old_weights
    )
    positions = jnp.arange(groups, dtype=jnp.int32)
    holder = jnp.sum(
        jnp.where(owner_plan[:, None] == positions[None, :], positions[:, None], 0), axis=0
    )
    stacked = jnp.stack([new_weights, first_new, second_new])
    rows_here = stacked.shape[1]
    pieces = stacked.reshape(3, groups, rows_here // groups, stacked.shape[2])
    spread = lax.all_to_all(
        pieces.astype(jnp.bfloat16), "expert", split_axis=1, concat_axis=1, tiled=True
    ).astype(pieces.dtype)
    ordered = jnp.take(spread, holder, axis=1)
    collected = lax.all_to_all(
        ordered.astype(jnp.bfloat16), "expert", split_axis=1, concat_axis=1, tiled=True
    ).astype(ordered.dtype)
    relocated = collected.reshape(3, rows_here, stacked.shape[2])
    serve_expert = positions // split
    serve_full = lax.all_gather(new_weights.astype(jnp.bfloat16), DP, axis=0, tiled=True)
    next_targets = slot_targets(next_routes, CAP)
    next_pairs = jnp.repeat(next_inputs, topk_count, axis=0)
    send_next = jnp.take(dispatch_pairs(next_targets, next_pairs, CAP), serve_expert, axis=0)
    received = lax.all_to_all(send_next, "expert", split_axis=0, concat_axis=0, tiled=True)
    flat_rows = received.reshape(-1, D)
    gate_next = (
        jnp.dot(flat_rows, serve_full[:, :width], preferred_element_type=jnp.float32) * in_scale
    )
    up_next = (
        jnp.dot(flat_rows, serve_full[:, width : 2 * width], preferred_element_type=jnp.float32)
        * in_scale
    )
    next_activation = (gate_next * jax.nn.sigmoid(gate_next) * up_next).astype(jnp.bfloat16)
    slab_partial = (
        lax.dot_general(
            next_activation,
            serve_full[:, 2 * width :],
            (((1,), (1,)), ((), ())),
            preferred_element_type=jnp.float32,
        )
        * out_scale
    )
    partials = slab_partial.astype(jnp.bfloat16).reshape(received.shape[0], received.shape[1], D)
    returned = lax.all_to_all(partials, "expert", split_axis=0, concat_axis=0, tiled=True)
    selector = (serve_expert[None, :] == jnp.arange(EXPERTS, dtype=jnp.int32)[:, None]).astype(
        jnp.bfloat16
    )
    expert_sums = jnp.dot(
        selector, returned.reshape(groups, -1), preferred_element_type=jnp.float32
    ).reshape(EXPERTS * CAP, D)
    pair_sums = jnp.take(expert_sums, next_targets, axis=0)
    weighted = pair_sums * next_gates
    layer_output = jnp.sum(weighted.reshape(-1, topk_count, D), axis=1).astype(jnp.bfloat16)
    return (layer_output, relocated[0][None], relocated[1][None], relocated[2][None])


def solution(mesh):
    torus = Mesh(mesh.devices.reshape(4, 8, mesh.shape["expert"]), ("dp_0", "dp_1", "expert"))
    return jax.shard_map(
        shards,
        mesh=torus,
        in_specs=(
            P(DP_EXPERT, None),
            P(DP_EXPERT, None),
            P(DP_EXPERT, None),
            P(DP_EXPERT, None),
            P(DP_EXPERT, None),
            P(DP_EXPERT, None),
            P(DP_EXPERT, None),
            P("expert", DP, None),
            P("expert", DP, None),
            P("expert", DP, None),
            P(),
        ),
        out_specs=(
            P(DP_EXPERT, None),
            P("expert", DP, None),
            P("expert", DP, None),
            P("expert", DP, None),
        ),
        check_vma=False,
    )
```

profile of v0, /device:TPU:1, one launch (start us, length us, event | category | flops | bytes accessed | tf_op | source)
XLA Modules:
  0.0 430.1 jit_solution(923585114164103687)
XLA Ops:
  7.2 0.8 fusion.57
  8.2 0.8 select_reduce_fusion
  9.0 0.7 multiply_add_fusion
  10.0 1.4 convolution_convert_fusion
  12.1 2.8 pad_maximum_fusion
  14.9 11.3 %all-to-all-start.1 = ((bf16[16,80,2048]{2,1,0:T(8,128)(2,1)}), bf16[16,80,2048]{2,1,0:T(8,128)(2,1)}, u32[]{:S(2)}, u32[]{:S(2)}) async-start(bf16[16,80,2048]{2,1,0:T(8,128)(2,1)} %pad_maximum_fusion), calls=%async_computation.1 | async-start | bytes 10485760 | tf_op jit(solution)/shard_map/all_to_all | solution.py:26
  26.2 11.1 %all_gather.9 = bf16[4,64,864]{2,1,0:T(8,128)(2,1)} all-gather(bf16[1,64,864]{2,1,0:T(8,128)(2,1)S(1)} %convert_element_type.71), channel_id=1, replica_groups=mesh['dp_0'=4,'dp_1'=8,'expert'=16] {'dp_0'}, dimensions={0}, use_global_device_ids=true | all-gather | bytes 552960 | tf_op jit(solution)/shard_map/all_gather | solution.py:39
  37.4 56.8 %all-gather.3.cloned.1.call-done = bf16[32,64,864]{2,1,0:T(8,128)(2,1)} async-done(((bf16[4,64,864]{2,1,0:T(8,128)(2,1)}), bf16[32,64,864]{2,1,0:T(8,128)(2,1)}) %all-gather.3.cloned.1.call-update) | async-done | bytes 3538960 | tf_op jit(solution)/shard_map/all_gather | solution.py:39
  94.2 4.3 %copy.48 = bf16[8,4,64,864]{3,2,0,1:T(8,128)(2,1)} copy(bf16[8,4,64,864]{3,2,1,0:T(8,128)(2,1)} %bitcast.86) | data formatting | bytes 7077888 | tf_op jit(solution)/shard_map/reshape | solution.py:41
  98.5 43.6 %all-to-all-done.1 = bf16[16,80,2048]{2,1,0:T(8,128)(2,1)} async-done(((bf16[16,80,2048]{2,1,0:T(8,128)(2,1)}), bf16[16,80,2048]{2,1,0:T(8,128)(2,1)}, u32[]{:S(2)}, u32[]{:S(2)}) %all-to-all-start.1) | async-done | bytes 5242912 | tf_op jit(solution)/shard_map/all_to_all | solution.py:26
  142.2 3.4 fusion.71
  145.8 1.7 fusion.17
  147.5 1.2 fusion.20
  148.6 1.7 fusion.14
  150.3 1.1 fusion.2
  151.5 1.1 fusion.1
  152.6 1.2 fusion
  153.8 2.0 pad_maximum_fusion.1
  155.9 46.6 %reduce-scatter.5.cloned.1.call-done = bf16[512,864]{0,1:T(8,128)(2,1)} async-done(((bf16[2048,864]{0,1:T(8,128)(2,1)}), bf16[512,864]{0,1:T(8,128)(2,1)}) %reduce-scatter.5.cloned.1.call-update) | async-done | bytes 884752 | tf_op jit(solution)/shard_map/reduce_scatter | solution.py:53
  202.5 2.2 copy.53
  205.0 37.9 %reduce-scatter.7.cloned.1.call-done = bf16[64,864]{1,0:T(8,128)(2,1)} async-done(((bf16[512,864]{1,0:T(8,128)(2,1)}), bf16[64,864]{1,0:T(8,128)(2,1)}) %reduce-scatter.7.cloned.1.call-update) | async-done | bytes 110608 | tf_op jit(solution)/shard_map/reduce_scatter | solution.py:53
  242.9 1.7 fusion.53
  245.2 0.3 convolution_convert_fusion.2
  245.5 0.9 stack.12
  246.8 0.8 copy.50
  247.6 11.9 %all-to-all-start.3 = ((bf16[3,16,4,864]{3,2,0,1:T(4,128)(2,1)}), bf16[3,16,4,864]{3,2,0,1:T(4,128)(2,1)S(1)}, u32[]{:S(2)}, u32[]{:S(2)}) async-start(bf16[3,16,4,864]{3,2,0,1:T(4,128)(2,1)} %copy.50), calls=%async_computation.4 | async-start | bytes 688128 | tf_op jit(solution)/shard_map/all_to_all | solution.py:151
  259.5 2.2 gather_fusion
  261.7 3.6 broadcast_select_fusion
  265.3 7.6 %all-to-all-done.3 = bf16[3,16,4,864]{3,2,0,1:T(4,128)(2,1)S(1)} async-done(((bf16[3,16,4,864]{3,2,0,1:T(4,128)(2,1)}), bf16[3,16,4,864]{3,2,0,1:T(4,128)(2,1)S(1)}, u32[]{:S(2)}, u32[]{:S(2)}) %all-to-all-start.3) | async-done | bytes 331808 | tf_op jit(solution)/shard_map/all_to_all | solution.py:151
  272.9 3.6 all-to-all-start
  276.8 0.9 gather_fusion.2
  277.7 0.9 fusion.47
  278.6 56.9 %all-to-all-done = bf16[16,40,2048]{2,1,0:T(8,128)(2,1)S(1)} async-done(((bf16[16,40,2048]{2,1,0:T(8,128)(2,1)}), bf16[16,40,2048]{2,1,0:T(8,128)(2,1)S(1)}, u32[]{:S(2)}, u32[]{:S(2)}) %all-to-all-start) | async-done | bytes 2621472 | tf_op jit(solution)/shard_map/all_to_all | solution.py:164
  335.5 5.5 %all-to-all-start.4 = ((bf16[3,16,4,864]{3,2,0,1:T(4,128)(2,1)}), bf16[3,16,4,864]{3,2,0,1:T(4,128)(2,1)S(1)}, u32[]{:S(2)}, u32[]{:S(2)}) async-start(bf16[3,16,4,864]{3,2,0,1:T(4,128)(2,1)} %fusion.47), calls=%async_computation.5 | async-start | bytes 688128 | tf_op jit(solution)/shard_map/all_to_all | solution.py:155
  341.0 3.4 fusion.23
  344.4 7.5 %multiply_convert_fusion = bf16[640,2048]{1,0:T(8,128)(2,1)} fusion(bf16[2048,864]{1,0:T(8,128)(2,1)} %all-gather.5.cloned.1.call-done, bf16[640,2048]{1,0:T(8,128)(2,1)S(1)} %bitcast.94, f32[640,288]{0,1:T(8,128)} %fusion.23), kind=kOutput, calls=%fused_computation.4 | convolution fusion | flops 1513861120 | bytes 9125888 | tf_op jit(solution)/shard_map/dot_general | solution.py:175
  351.9 2.5 all-to-all-done.4
  354.4 4.8 %all-to-all-start.2 = ((bf16[16,40,2048]{2,1,0:T(8,128)(2,1)}), bf16[16,40,2048]{2,1,0:T(8,128)(2,1)S(1)}, u32[]{:S(2)}, u32[]{:S(2)}) async-start(bf16[16,40,2048]{2,1,0:T(8,128)(2,1)} %bitcast.95), calls=%async_computation.3 | async-start | bytes 5242880 | tf_op jit(solution)/shard_map/all_to_all | solution.py:184
  359.2 0.8 fusion.72
  360.0 1.7 slice.43
  361.7 1.7 slice.45
  363.4 0.8 slice.47
  364.2 54.6 %all-to-all-done.2 = bf16[16,40,2048]{2,1,0:T(8,128)(2,1)S(1)} async-done(((bf16[16,40,2048]{2,1,0:T(8,128)(2,1)}), bf16[16,40,2048]{2,1,0:T(8,128)(2,1)S(1)}, u32[]{:S(2)}, u32[]{:S(2)}) %all-to-all-start.2) | async-done | bytes 2621472 | tf_op jit(solution)/shard_map/all_to_all | solution.py:184
  418.7 1.4 copy.55
  420.2 0.5 fusion.62
  420.7 0.9 reshape.195
  421.6 1.0 gather_fusion.1
  422.6 1.0 multiply_convert_fusion.1
  (53 shorter events, 3.0 us)
Async XLA Ops:
  7.2 2.5 copy-start
  14.9 11.3 %copy-start.3 = (f32[1,64,864]{2,1,0:T(8,128)S(1)}, f32[1,64,864]{2,1,0:T(8,128)}, u32[]{:S(2)}) copy-start(f32[1,64,864]{2,1,0:T(8,128)} %param.18) | copy-start | bytes 663556
  14.9 127.3 %all-to-all-start.1 = ((bf16[16,80,2048]{2,1,0:T(8,128)(2,1)}), bf16[16,80,2048]{2,1,0:T(8,128)(2,1)}, u32[]{:S(2)}, u32[]{:S(2)}) async-start(bf16[16,80,2048]{2,1,0:T(8,128)(2,1)} %pad_maximum_fusion), calls=%async_computation.1 | async-start | bytes 10485760 | tf_op jit(solution)/shard_map/all_to_all | solution.py:26
  26.2 68.0 %all-gather.3.cloned.1.call-start = ((), (), s32[]{:S(2)}) async-start(), calls=%async_computation.7 | async-start | bytes 4128768 | tf_op jit(solution)/shard_map/all_gather | solution.py:39
  37.4 165.2 %reduce-scatter.5.cloned.1.call-start = ((), (), s32[]{:S(2)}) async-start(), calls=%async_computation.8 | async-start | bytes 4423680 | tf_op jit(solution)/shard_map/reduce_scatter | solution.py:53
  142.2 3.6 copy-start.2
  155.8 87.1 %copy-start.5 = (f32[1,64,864]{2,1,0:T(8,128)S(1)}, f32[1,64,864]{2,1,0:T(8,128)}, u32[]{:S(2)}) copy-start(f32[1,64,864]{2,1,0:T(8,128)} %param.19) | copy-start | bytes 663556
  155.8 87.1 %copy-start.6 = (f32[1,64,864]{2,1,0:T(8,128)S(1)}, f32[1,64,864]{2,1,0:T(8,128)}, u32[]{:S(2)}) copy-start(f32[1,64,864]{2,1,0:T(8,128)} %param.20) | copy-start | bytes 663556
  155.8 88.8 %copy-start.7 = (s32[128,1]{0,1:T(1,128)S(1)}, s32[128,1]{0,1:T(1,128)}, u32[]{:S(2)}) copy-start(s32[128,1]{0,1:T(1,128)} %param.16) | copy-start | bytes 1540
  155.8 89.3 %copy-start.4 = (bf16[128,2048]{1,0:T(8,128)(2,1)S(1)}, bf16[128,2048]{1,0:T(8,128)(2,1)}, u32[]{:S(2)}) copy-start(bf16[128,2048]{1,0:T(8,128)(2,1)} %param.15) | copy-start | bytes 1572868
  155.8 87.0 %reduce-scatter.7.cloned.1.call-start = ((), (), s32[]{:S(2)}) async-start(), calls=%async_computation.10 | async-start | bytes 1032192 | tf_op jit(solution)/shard_map/reduce_scatter | solution.py:53
  204.8 136.2 %all-gather.5.cloned.1.call-start = ((), (), s32[]{:S(2)}) async-start(), calls=%async_computation.9 | async-start | bytes 3784704 | tf_op jit(solution)/shard_map/all_gather | solution.py:160
  247.6 25.2 %all-to-all-start.3 = ((bf16[3,16,4,864]{3,2,0,1:T(4,128)(2,1)}), bf16[3,16,4,864]{3,2,0,1:T(4,128)(2,1)S(1)}, u32[]{:S(2)}, u32[]{:S(2)}) async-start(bf16[3,16,4,864]{3,2,0,1:T(4,128)(2,1)} %copy.50), calls=%async_computation.4 | async-start | bytes 688128 | tf_op jit(solution)/shard_map/all_to_all | solution.py:151
  265.3 11.2 %copy-start.9 = (s32[16]{0:T(128)S(1)}, s32[16]{0:T(128)}, u32[]{:S(2)}) copy-start(s32[16]{0:T(128)} %param.21) | copy-start | bytes 196
  272.9 62.7 %all-to-all-start = ((bf16[16,40,2048]{2,1,0:T(8,128)(2,1)}), bf16[16,40,2048]{2,1,0:T(8,128)(2,1)S(1)}, u32[]{:S(2)}, u32[]{:S(2)}) async-start(bf16[16,40,2048]{2,1,0:T(8,128)(2,1)} %broadcast_select_fusion), calls=%async_computation | async-start | bytes 5242880 | tf_op jit(solution)/shard_map/all_to_all | solution.py:164
  335.5 18.8 %all-to-all-start.4 = ((bf16[3,16,4,864]{3,2,0,1:T(4,128)(2,1)}), bf16[3,16,4,864]{3,2,0,1:T(4,128)(2,1)S(1)}, u32[]{:S(2)}, u32[]{:S(2)}) async-start(bf16[3,16,4,864]{3,2,0,1:T(4,128)(2,1)} %fusion.47), calls=%async_computation.5 | async-start | bytes 688128 | tf_op jit(solution)/shard_map/all_to_all | solution.py:155
  354.4 64.4 %all-to-all-start.2 = ((bf16[16,40,2048]{2,1,0:T(8,128)(2,1)}), bf16[16,40,2048]{2,1,0:T(8,128)(2,1)S(1)}, u32[]{:S(2)}, u32[]{:S(2)}) async-start(bf16[16,40,2048]{2,1,0:T(8,128)(2,1)} %bitcast.95), calls=%async_computation.3 | async-start | bytes 5242880 | tf_op jit(solution)/shard_map/all_to_all | solution.py:184
  421.6 1.0 copy-start.8
  421.6 2.0 copy-start.1
Sparse Core Ops, SparseCore 0:
  37.5 56.6 all-gather.2
  155.9 46.5 reduce-scatter.4
  205.4 37.4 reduce-scatter.6
  246.5 85.5 all-gather.4
where the time goes:
time: 431 us; the launch traced here: 430 us
  waiting for transfers between devices  307 us (71%)
  starting transfers between devices  37.3 us (9%)
  local copies, waits for them, and re-layouts  24.2 us (6%)
  matrix products  21.5 us (5%)
  other arithmetic  15.3 us (4%)
  between operations  14.1 us (3%)
  blocking collectives  11.1 us (3%)
    reduce_scatter x2, waiting for transfers between devices, own_rows(): so_far = lax.psum_scatter(so_far, axis, scatter_dimension=0, tiled=True)  84.5 us
    all_to_all x1, waiting for transfers between devices, shards(): lax.all_to_all(send_next, 'expert', split_axis=0, concat_axis=0, tiled=True)  56.9 us
    all_gather x1, waiting for transfers between devices, gather_in_order(): parts = lax.all_gather(parts, axes[k], axis=0, tiled=True)  56.8 us
    all_to_all x1, waiting for transfers between devices, shards(): lax.all_to_all(partials, 'expert', split_axis=0, concat_axis=0, tiled=True)  54.6 us
    all_to_all x1, waiting for transfers between devices, in_one_piece(): lax.all_to_all(both, axis, split_axis=split_dim, concat_axis=concat_dim,...  43.6 us
    all_to_all x1, starting transfers between devices, shards(): lax.all_to_all(pieces.astype(jnp.bfloat16), 'expert', split_axis=1, conca...  11.9 us
    all_to_all x1, starting transfers between devices, in_one_piece(): lax.all_to_all(both, axis, split_axis=split_dim, concat_axis=concat_dim,...  11.3 us
    all_gather x1, blocking collectives, gather_in_order(): parts = lax.all_gather(parts, axes[k], axis=0, tiled=True)  11.1 us
  transfers between devices with their start and end apart: 9, of which 8 were waited for; matrix products, arithmetic and copies ran while one was open for 7% of the time, Pallas kernels for 0%

commit v1 on v0

v1 whole, which is shorter than its diff:
```python
import jax
import jax.numpy as jnp
from jax import lax
from jax.sharding import Mesh
from jax.sharding import PartitionSpec as P

D = 2048
HID = 1152
EXPERTS = 4
CAP = 40
SLOTS = EXPERTS * CAP
DP = ("x", "z")
EXPERT = ("y", "core")
ALL = DP + EXPERT
FIRST = 640


beta_one = 0.9
beta_two = 0.95
learn_rate = 0.2
decay_rate = 0.1
adam_step = 10.0
adam_eps = 1e-08


def around(axis, by):
    size = lax.axis_size(axis)
    return [(k, (k + by) % size) for k in range(size)]


def pass_on(value, axis, by):
    return lax.ppermute(value, axis, around(axis, by))


def exchange(value, axis):
    return lax.all_to_all(value, axis, split_axis=0, concat_axis=0, tiled=True)


def slot_of(routes):
    ids = routes.reshape(-1)
    one_hot = ids[:, None] == jnp.arange(EXPERTS, dtype=jnp.int32)[None, :]
    count = ids.shape[0]
    before = lax.broadcasted_iota(jnp.int32, (count, count), 1) < lax.broadcasted_iota(
        jnp.int32, (count, count), 0
    )
    earlier = jnp.dot(
        before.astype(jnp.bfloat16),
        one_hot.astype(jnp.bfloat16),
        preferred_element_type=jnp.float32,
    )
    slots = jnp.sum(jnp.where(one_hot, earlier, 0.0), axis=1).astype(jnp.int32)
    return ids * CAP + slots


def to_slots(targets, payload):
    rows = lax.broadcasted_iota(jnp.int32, (SLOTS, targets.shape[0]), 0)
    selector = (rows == targets[None, :]).astype(jnp.bfloat16)
    filled = jnp.dot(selector, payload, preferred_element_type=jnp.float32)
    return filled.astype(jnp.bfloat16).reshape(EXPERTS, CAP, payload.shape[1])


def after(value, other):
    one = other[(0,) * other.ndim]
    return value + (one != one).astype(value.dtype)


def both_cores(rows):
    return jnp.concatenate([rows, pass_on(rows, "core", 1)], axis=0)


def to_chips(slots):
    chips = lax.axis_size("y")
    return exchange(jnp.repeat(slots, chips // EXPERTS, axis=0), "y")


def chunk_of(parts, offset):
    return lax.dynamic_index_in_dim(
        parts, lax.rem(lax.axis_index("x") + offset, 4), 0, keepdims=False
    )


def f32(value):
    return value.astype(jnp.float32)


def b16(value):
    return value.astype(jnp.bfloat16)


def sum_along_x(parts):
    far = chunk_of(parts, 2)
    half = far.shape[0] // 2
    top = pass_on(far[:half], "x", 1)
    bottom = pass_on(far[half:], "x", -1)
    after, before = chunk_of(parts, 1), chunk_of(parts, 3)
    after = jnp.concatenate([b16(f32(after[:half]) + f32(top)), after[half:]], axis=0)
    before = jnp.concatenate([before[:half], b16(f32(before[half:]) + f32(bottom))], axis=0)
    from_left = pass_on(after, "x", 1)
    from_right = pass_on(before, "x", -1)
    return f32(chunk_of(parts, 0)) + f32(from_left) + f32(from_right)


def sum_small_along_x(parts):
    total = f32(chunk_of(parts, 0))
    for by in (1, 2, 3):
        total = total + f32(pass_on(chunk_of(parts, by), "x", by))
    return total


def in_x_order(found):
    me = lax.axis_index("x")
    out = jnp.zeros((4,) + found[0].shape, found[0].dtype)
    for k, value in enumerate(found):
        out = lax.dynamic_update_index_in_dim(out, value, lax.rem(me + k, 4), 0)
    return out


def gather_along_x(value):
    half = value.shape[0] // 2
    left = pass_on(value, "x", 1)
    right = pass_on(value, "x", -1)
    top = pass_on(left[:half], "x", 1)
    bottom = pass_on(right[half:], "x", -1)
    return in_x_order([value, right, jnp.concatenate([top, bottom], axis=0), left])


def gather_small_along_x(value):
    return in_x_order([value] + [pass_on(value, "x", -by) for by in (1, 2, 3)])


def gather_along_z(value):
    size = lax.axis_size("z")
    return exchange(jnp.broadcast_to(value[None], (size,) + value.shape), "z")


def sum_along_z(value):
    got = exchange(value, "z")
    return jnp.sum(f32(got), axis=0)


def own_rows(first, second):
    size_x, size_z = lax.axis_size("x"), lax.axis_size("z")
    rows = first.shape[0] // (size_x * size_z)
    second = second.reshape(size_x, size_z, rows, -1).swapaxes(0, 1)
    half_second = b16(sum_along_z(second))
    half_first = b16(sum_along_x(first.reshape(size_x, size_z * rows, -1)))
    own_second = sum_small_along_x(half_second)
    own_first = sum_along_z(half_first.reshape(size_z, rows, -1))
    return jnp.concatenate([own_first, own_second], axis=1)


def all_rows(value):
    first, second = value[:, :FIRST], value[:, FIRST:]
    wide_first = gather_along_z(first)
    wide_second = gather_small_along_x(second)
    all_second = gather_along_z(wide_second).swapaxes(0, 1)
    all_first = gather_along_x(wide_first.reshape(-1, wide_first.shape[-1]))
    return (
        all_first.reshape(-1, first.shape[1]),
        all_second.reshape(-1, second.shape[1]),
    )


def whole_step(
    step_inputs,
    step_cotangent,
    step_routes,
    step_gates,
    next_inputs,
    next_routes,
    next_gates,
    master_weights,
    first_moment,
    second_moment,
    owner_plan,
):
    groups = lax.axis_size(EXPERT)
    width = master_weights.shape[2] // 3
    in_scale = D ** (-0.5)
    out_scale = HID ** (-0.5)
    old_weights = master_weights[0]
    step_targets = slot_of(step_routes)
    scaled = b16(f32(step_cotangent) * step_gates)
    sent_inputs = to_slots(step_targets, step_inputs)
    parts = lax.all_gather(b16(old_weights), "x", axis=0)
    parts = lax.all_gather(parts, "z", axis=0)
    weights = parts.swapaxes(0, 1).reshape(D, 3 * width)
    got_inputs = to_chips(sent_inputs)
    got_scaled = to_chips(to_slots(step_targets, scaled))
    flat_inputs = both_cores(got_inputs).reshape(-1, D)
    flat_scaled = both_cores(got_scaled).reshape(-1, D)

    def times(rows, block):
        return jnp.dot(rows, block, preferred_element_type=jnp.float32)

    gate_pre = times(flat_inputs, weights[:, :width]) * in_scale
    up_pre = times(flat_inputs, weights[:, width : 2 * width]) * in_scale
    down_back = times(flat_scaled, weights[:, 2 * width :]) * out_scale
    sigmoid_gate = jax.nn.sigmoid(gate_pre)
    silu_gate = gate_pre * sigmoid_gate
    activation = b16(silu_gate * up_pre)
    gate_grad = b16(down_back * up_pre * sigmoid_gate * (1.0 + gate_pre * (1.0 - sigmoid_gate)))
    up_grad = b16(down_back * silu_gate)
    contract = (((0,), (0,)), ((), ()))

    def gradient_of(rows, grads, scale):
        return b16(
            lax.dot_general(rows, grads, contract, preferred_element_type=jnp.float32) * scale
        )

    gate_part = gradient_of(flat_inputs, gate_grad, in_scale)
    up_part = gradient_of(flat_inputs, up_grad, in_scale)
    down_part = gradient_of(flat_scaled, activation, out_scale)
    cut = FIRST - 2 * width
    gradient = own_rows(
        jnp.concatenate([gate_part, up_part, down_part[:, :cut]], axis=1), down_part[:, cut:]
    )
    first_new = beta_one * first_moment[0] + (1.0 - beta_one) * gradient
    second_new = beta_two * second_moment[0] + (1.0 - beta_two) * gradient * gradient
    first_hat = first_new / (1.0 - beta_one**adam_step)
    second_hat = second_new / (1.0 - beta_two**adam_step)
    new_weights = old_weights - learn_rate * (
        first_hat / (jnp.sqrt(second_hat) + adam_eps) + decay_rate * old_weights
    )
    serve_first, serve_second = all_rows(b16(new_weights))

    positions = jnp.arange(groups, dtype=jnp.int32)
    me = lax.axis_index(EXPERT)
    holder = jnp.sum(jnp.where(owner_plan == me, positions, 0))
    stacked = jnp.concatenate([b16(new_weights), b16(first_new), b16(second_new)], axis=0)
    everywhere = lax.all_gather(stacked, EXPERT, axis=0)
    relocated = lax.dynamic_index_in_dim(everywhere, holder, 0, keepdims=False)
    relocated = f32(relocated).reshape(3, 1, new_weights.shape[0], new_weights.shape[1])

    next_targets = slot_of(next_routes)
    next_slots = to_slots(after(next_targets, got_scaled), next_inputs)
    column = lax.all_gather(next_slots, "y", axis=0)
    chips_each = lax.axis_size("y") // EXPERTS
    here = lax.axis_index("y") // chips_each
    own_next = lax.dynamic_index_in_dim(column, here, 1, keepdims=False).reshape(-1, D)
    other_next = pass_on(own_next, "core", 1)
    down = jnp.concatenate([serve_first[:, 2 * width :], serve_second], axis=1)

    def partial_of(rows):
        gate_next = times(rows, serve_first[:, :width]) * in_scale
        up_next = times(rows, serve_first[:, width : 2 * width]) * in_scale
        next_activation = b16(gate_next * jax.nn.sigmoid(gate_next) * up_next)
        return (
            lax.dot_general(
                next_activation, down, (((1,), (1,)), ((), ())), preferred_element_type=jnp.float32
            )
            * out_scale
        )

    met = pass_on(b16(partial_of(other_next)), "core", 1)
    partials = b16(partial_of(own_next) + f32(met))
    returned = exchange(partials, "y")
    chip_rows = returned.shape[0]
    slot = lax.broadcasted_iota(jnp.int32, (next_targets.shape[0], chip_rows), 1)
    expert_slot = (slot // (chips_each * CAP)) * CAP + lax.rem(slot, CAP)
    picks = (next_targets[:, None] == expert_slot).astype(jnp.bfloat16)
    pair_sums = jnp.dot(picks, returned, preferred_element_type=jnp.float32)
    layer_output = b16(pair_sums * next_gates)
    return (layer_output, relocated[0], relocated[1], relocated[2])


def solution(mesh):
    chips = mesh.devices.reshape(4, -1, mesh.shape["expert"] // 2, 2)
    tokens = P(ALL, None)
    slabs = P(EXPERT, DP, None)
    return jax.shard_map(
        whole_step,
        mesh=Mesh(chips, ALL),
        in_specs=(tokens,) * 7 + (slabs,) * 3 + (P(),),
        out_specs=(tokens,) + (slabs,) * 3,
        check_vma=False,
    )
```

time: 431 us -> 354 us (0.82)
  waiting for transfers between devices: 307 us -> 139 us
  starting transfers between devices: 37.3 us -> 103 us
  matrix products: 21.5 us -> 30.3 us
  other arithmetic: 15.3 us -> 21.3 us
  local copies, waits for them, and re-layouts: 24.2 us -> 29 us
    reduce_scatter x2 -> x0, waiting for transfers between devices: 84.5 us -> none  [own_rows(): so_far = lax.psum_scatter(so_far, axis, scatter_dimension=0, tiled=True)]
    ppermute x0 -> x18, starting transfers between devices: none -> 57.9 us  [pass_on(): return lax.ppermute(value, axis, around(axis, by))]
    all_gather x2 -> x3, waiting for transfers between devices: 56.8 us -> 0.02 us  [the longest x1 0.02 us: whole_step(): column = lax.all_gather(next_slots, 'y', axis=0)]
    all_to_all x5 -> x7, waiting for transfers between devices: 165 us -> 112 us  [exchange(): return lax.all_to_all(value, axis, split_axis=0, concat_axis=0, tiled=True)]
    ppermute x0 -> x18, waiting for transfers between devices: none -> 27.2 us  [pass_on(): return lax.ppermute(value, axis, around(axis, by))]
    dot_general x12 -> x16, matrix products: 21.5 us -> 30.3 us  [the longest x2 11.6 us: partial_of(): lax.dot_general(next_activation, down, (((1,), (1,)), ((), ())), preferre...]
    all_to_all x5 -> x7, starting transfers between devices: 37 us -> 44.8 us  [exchange(): return lax.all_to_all(value, axis, split_axis=0, concat_axis=0, tiled=True)]
    concatenate x2 -> x6, other arithmetic: 4.78 us -> 10.6 us  [the longest x2 6.14 us: both_cores(): return jnp.concatenate([rows, pass_on(rows, 'core', 1)], axis=0)]
  transfers between devices with their start and end apart: 9 -> 28, of which waited for: 8 -> 15; matrix products, arithmetic and copies ran while one was open for 7% -> 22% of each run, Pallas kernels for 0% -> 0%
where the time goes in v1:
time: 354 us; the launch traced here: 352 us
  waiting for transfers between devices  139 us (39%)
  starting transfers between devices  103 us (29%)
  matrix products  30.3 us (9%)
  local copies, waits for them, and re-layouts  29 us (8%)
  other arithmetic  21.3 us (6%)
  between operations  17.6 us (5%)
  blocking collectives  11.7 us (3%)
    all_to_all x7, waiting for transfers between devices, exchange(): return lax.all_to_all(value, axis, split_axis=0, concat_axis=0, tiled=True)  112 us
    ppermute x18, starting transfers between devices, pass_on(): return lax.ppermute(value, axis, around(axis, by))  57.9 us
    all_to_all x7, starting transfers between devices, exchange(): return lax.all_to_all(value, axis, split_axis=0, concat_axis=0, tiled=True)  44.8 us
    ppermute x18, waiting for transfers between devices, pass_on(): return lax.ppermute(value, axis, around(axis, by))  27.2 us
    all_gather x1, blocking collectives, whole_step(): parts = lax.all_gather(b16(old_weights), 'x', axis=0)  11.7 us
    dot_general x2, matrix products, partial_of(): lax.dot_general(next_activation, down, (((1,), (1,)), ((), ())), preferre...  11.6 us
    dot_general x5, matrix products, times(): return jnp.dot(rows, block, preferred_element_type=jnp.float32)  9.95 us
  transfers between devices with their start and end apart: 28, of which 15 were waited for; matrix products, arithmetic and copies ran while one was open for 22% of the time, Pallas kernels for 0%

profile of v1, /device:TPU:1, one launch (start us, length us, event | category | flops | bytes accessed | tf_op | source)
XLA Modules:
  0.0 351.7 jit_solution(12179046811351989986)
XLA Ops:
  8.2 11.7 %all_gather.20 = bf16[4,64,864]{2,1,0:T(8,128)(2,1)} all-gather(bf16[1,64,864]{2,1,0:T(8,128)(2,1)S(1)} %convert_element_type.176), channel_id=1, replica_groups=mesh['x'=4,'z'=8,'y'=8,'core'=2] {'x'}, dimensions={0}, use_global_device_ids=true | all-gather | bytes 552960 | tf_op jit(solution)/shard_map/all_gather | solution.py:185
  24.2 7.7 %all-to-all-start = ((bf16[8,40,2048]{2,1,0:T(8,128)(2,1)}), bf16[8,40,2048]{2,1,0:T(8,128)(2,1)S(1)}, u32[]{:S(2)}, u32[]{:S(2)}) async-start(bf16[8,40,2048]{2,1,0:T(8,128)(2,1)} %bitcast.6), calls=%async_computation | async-start | bytes 2621440 | tf_op jit(solution)/shard_map/all_to_all | solution.py:36
  32.3 31.4 %all-to-all-done = bf16[8,40,2048]{2,1,0:T(8,128)(2,1)S(1)} async-done(((bf16[8,40,2048]{2,1,0:T(8,128)(2,1)}), bf16[8,40,2048]{2,1,0:T(8,128)(2,1)S(1)}, u32[]{:S(2)}, u32[]{:S(2)}) %all-to-all-start) | async-done | bytes 1310752 | tf_op jit(solution)/shard_map/all_to_all | solution.py:36
  64.9 3.6 %all-to-all-start.1 = ((bf16[8,40,2048]{2,1,0:T(8,128)(2,1)}), bf16[8,40,2048]{2,1,0:T(8,128)(2,1)S(1)}, u32[]{:S(2)}, u32[]{:S(2)}) async-start(bf16[8,40,2048]{2,1,0:T(8,128)(2,1)} %bitcast.126), calls=%async_computation.1 | async-start | bytes 2621440 | tf_op jit(solution)/shard_map/all_to_all | solution.py:36
  71.8 29.2 %all-to-all-done.1 = bf16[8,40,2048]{2,1,0:T(8,128)(2,1)S(1)} async-done(((bf16[8,40,2048]{2,1,0:T(8,128)(2,1)}), bf16[8,40,2048]{2,1,0:T(8,128)(2,1)S(1)}, u32[]{:S(2)}, u32[]{:S(2)}) %all-to-all-start.1) | async-done | bytes 1310752 | tf_op jit(solution)/shard_map/all_to_all | solution.py:36
  101.0 4.9 %collective-permute-start = (bf16[8,40,2048]{2,1,0:T(8,128)(2,1)S(1)}, bf16[8,40,2048]{2,1,0:T(8,128)(2,1)}, u32[]{:S(2)}, u32[]{:S(2)}) collective-permute-start(bf16[8,40,2048]{2,1,0:T(8,128)(2,1)S(1)} %all-to-all-done.1), channel_id=1, source_target_pairs={{0,1},{1,0},{2,3},{3,2},{4,5},{5,4},{6,7},{7,6},{8,9},{9,8},{10,11... | collective-permute-start | bytes 3932168 | tf_op jit(solution)/shard_map/ppermute | solution.py:32
  105.9 1.9 collective-permute-start.1
  108.7 3.1 pad_maximum_fusion.1
  111.8 3.0 pad_maximum_fusion
  114.8 2.6 copy.25
  127.8 3.1 copy.33
  131.9 1.9 collective-permute-start.2
  133.8 4.6 %collective-permute-start.4 = (bf16[256,640]{1,0:T(8,128)(2,1)}, bf16[256,640]{1,0:T(8,128)(2,1)}, u32[]{:S(2)}, u32[]{:S(2)}) collective-permute-start(bf16[256,640]{1,0:T(8,128)(2,1)} %get-tuple-element.8), channel_id=1, source_target_pairs={{0,384},{128,0},{256,128},{384,256},{1,385},{129,1},{257,129},{385... | collective-permute-start | bytes 983048 | tf_op jit(solution)/shard_map/ppermute | solution.py:32
  139.4 2.3 copy.30
  141.7 2.3 copy.31
  144.0 19.2 %all-to-all-start.3 = ((bf16[8,4,64,224]{3,2,1,0:T(8,128)(2,1)}), bf16[8,4,64,224]{3,2,1,0:T(8,128)(2,1)}, u32[]{:S(2)}, u32[]{:S(2)}) async-start(bf16[8,4,64,224]{3,2,1,0:T(8,128)(2,1)} %copy.31), calls=%async_computation.3 | async-start | bytes 2097152 | tf_op jit(solution)/shard_map/all_to_all | solution.py:36
  168.2 4.7 %collective-permute-start.5 = (bf16[512,640]{1,0:T(8,128)(2,1)}, bf16[512,640]{1,0:T(8,128)(2,1)}, u32[]{:S(2)}, u32[]{:S(2)}) collective-permute-start(bf16[512,640]{1,0:T(8,128)(2,1)} %pad_maximum_fusion.7), channel_id=1, source_target_pairs={{0,384},{128,0},{256,128},{384,256},{1,385},{129,1},{257,129},{385... | collective-permute-start | bytes 1966088 | tf_op jit(solution)/shard_map/ppermute | solution.py:32
  172.9 10.9 %collective-permute-done.3 = bf16[512,640]{1,0:T(8,128)(2,1)} collective-permute-done((bf16[512,640]{1,0:T(8,128)(2,1)}, bf16[512,640]{1,0:T(8,128)(2,1)}, u32[]{:S(2)}, u32[]{:S(2)}) %collective-permute-start.3) | collective-permute-done | bytes 655392 | tf_op jit(solution)/shard_map/ppermute | solution.py:32
  185.7 2.4 fusion.20
  188.1 4.4 %all-to-all-done.3 = bf16[8,4,64,224]{3,2,1,0:T(8,128)(2,1)} async-done(((bf16[8,4,64,224]{3,2,1,0:T(8,128)(2,1)}), bf16[8,4,64,224]{3,2,1,0:T(8,128)(2,1)}, u32[]{:S(2)}, u32[]{:S(2)}) %all-to-all-start.3) | async-done | bytes 917536 | tf_op jit(solution)/shard_map/all_to_all | solution.py:36
  192.5 3.5 %all-to-all-start.2 = ((bf16[8,64,640]{2,1,0:T(8,128)(2,1)}), bf16[8,64,640]{2,1,0:T(8,128)(2,1)S(1)}, u32[]{:S(2)}, u32[]{:S(2)}) async-start(bf16[8,64,640]{2,1,0:T(8,128)(2,1)} %bitcast.143), calls=%async_computation.2 | async-start | bytes 1310720 | tf_op jit(solution)/shard_map/all_to_all | solution.py:36
  197.5 1.9 collective-permute-start.6
  199.4 5.0 %collective-permute-start.7 = (bf16[64,224]{1,0:T(8,128)(2,1)S(1)}, bf16[64,224]{1,0:T(8,128)(2,1)S(1)}, u32[]{:S(2)}, u32[]{:S(2)}) collective-permute-start(bf16[64,224]{1,0:T(8,128)(2,1)S(1)} %get-tuple-element.18), channel_id=1, source_target_pairs={{0,256},{128,384},{256,0},{384,128},{1,257},{129,385},{257,1},{385... | collective-permute-start | bytes 86024 | tf_op jit(solution)/shard_map/ppermute | solution.py:32
  204.5 1.9 collective-permute-start.8
  206.4 3.0 collective-permute-done.8
  209.4 6.3 %all-to-all-done.2 = bf16[8,64,640]{2,1,0:T(8,128)(2,1)S(1)} async-done(((bf16[8,64,640]{2,1,0:T(8,128)(2,1)}), bf16[8,64,640]{2,1,0:T(8,128)(2,1)S(1)}, u32[]{:S(2)}, u32[]{:S(2)}) %all-to-all-start.2) | async-done | bytes 655392 | tf_op jit(solution)/shard_map/all_to_all | solution.py:36
  217.8 3.5 %all-to-all-start.4 = ((bf16[8,64,640]{2,1,0:T(8,128)(2,1)}), bf16[8,64,640]{2,1,0:T(8,128)(2,1)S(1)}, u32[]{:S(2)}, u32[]{:S(2)}) async-start(bf16[8,64,640]{2,1,0:T(8,128)(2,1)} %broadcast_in_dim.69), calls=%async_computation.4 | async-start | bytes 1310720 | tf_op jit(solution)/shard_map/all_to_all | solution.py:36
  221.3 2.2 collective-permute-start.13
  223.5 2.0 collective-permute-start.14
  225.6 3.0 collective-permute-start.15
  230.0 2.6 collective-permute-done.15
  232.6 7.9 %all-to-all-done.4 = bf16[8,64,640]{2,1,0:T(8,128)(2,1)S(1)} async-done(((bf16[8,64,640]{2,1,0:T(8,128)(2,1)}), bf16[8,64,640]{2,1,0:T(8,128)(2,1)S(1)}, u32[]{:S(2)}, u32[]{:S(2)}) %all-to-all-start.4) | async-done | bytes 655392 | tf_op jit(solution)/shard_map/all_to_all | solution.py:36
  241.7 3.6 %all-to-all-start.5 = ((bf16[8,4,64,224]{3,2,1,0:T(8,128)(2,1)}), bf16[8,4,64,224]{3,2,1,0:T(8,128)(2,1)S(1)}, u32[]{:S(2)}, u32[]{:S(2)}) async-start(bf16[8,4,64,224]{3,2,1,0:T(8,128)(2,1)} %broadcast_in_dim.79), calls=%async_computation.5 | async-start | bytes 2097152 | tf_op jit(solution)/shard_map/all_to_all | solution.py:36
  245.3 1.9 collective-permute-start.9
  247.2 3.4 collective-permute-start.10
  250.6 2.6 constant_dynamic-slice_fusion
  253.2 4.4 %collective-permute-start.16 = (bf16[320,2048]{1,0:T(8,128)(2,1)}, bf16[320,2048]{1,0:T(8,128)(2,1)}, u32[]{:S(2)}, u32[]{:S(2)}) collective-permute-start(bf16[320,2048]{1,0:T(8,128)(2,1)} %bitcast.9), channel_id=1, source_target_pairs={{0,1},{1,0},{2,3},{3,2},{4,5},{5,4},{6,7},{7,6},{8,9},{9,8},{10,11... | collective-permute-start | bytes 3932168 | tf_op jit(solution)/shard_map/ppermute | solution.py:32
  257.6 6.4 %collective-permute-done.10 = bf16[512,640]{1,0:T(8,128)(2,1)S(1)} collective-permute-done((bf16[512,640]{1,0:T(8,128)(2,1)S(1)}, bf16[512,640]{1,0:T(8,128)(2,1)S(1)}, u32[]{:S(2)}, u32[]{:S(2)}) %collective-permute-start.10) | collective-permute-done | bytes 655392 | tf_op jit(solution)/shard_map/ppermute | solution.py:32
  264.1 2.5 collective-permute-start.11
  267.3 4.0 %collective-permute-start.12 = (bf16[256,640]{1,0:T(8,128)(2,1)}, bf16[256,640]{1,0:T(8,128)(2,1)}, u32[]{:S(2)}, u32[]{:S(2)}) collective-permute-start(bf16[256,640]{1,0:T(8,128)(2,1)} %slice.122), channel_id=1, source_target_pairs={{0,384},{128,0},{256,128},{384,256},{1,385},{129,1},{257,129},{385... | collective-permute-start | bytes 983048 | tf_op jit(solution)/shard_map/ppermute | solution.py:32
  276.3 2.0 fusion.45
  280.6 2.7 fusion.33
  283.3 5.8 %fusion = bf16[320,2048]{1,0:T(8,128)(2,1)} fusion(bf16[2048,224]{1,0:T(8,128)(2,1)S(1)} %bitcast.146, bf16[2048,64]{1,0:T(8,128)(2,1)S(1)} %slice.125, f32[320,288]{0,1:T(8,128)S(1)} %fusion.33, bf16[320,2048]{1,0:T(8,128)(2,1)} %collective-permute-done.16, bf16[2048,640]{1,0:T(8,128)(2,1)} %bitcast.40), kind=kOutput, calls=%fused_computation.5 | convolution fusion | flops 759289856 | bytes 5742592 | tf_op jit(solution)/shard_map/dot_general | solution.py:249
  289.1 5.7 %collective-permute-start.17 = (bf16[320,2048]{1,0:T(8,128)(2,1)}, bf16[320,2048]{1,0:T(8,128)(2,1)S(1)}, u32[]{:S(2)}, u32[]{:S(2)}) collective-permute-start(bf16[320,2048]{1,0:T(8,128)(2,1)} %fusion), channel_id=1, source_target_pairs={{0,1},{1,0},{2,3},{3,2},{4,5},{5,4},{6,7},{7,6},{8,9},{9,8},{10,11... | collective-permute-start | bytes 3932168 | tf_op jit(solution)/shard_map/ppermute | solution.py:32
  294.9 2.7 fusion.30
  297.7 5.8 %add_convert_fusion = bf16[320,2048]{1,0:T(8,128)(2,1)} fusion(bf16[320,2048]{1,0:T(8,128)(2,1)S(1)} %collective-permute-done.17, bf16[2048,224]{1,0:T(8,128)(2,1)S(1)} %bitcast.147, bf16[2048,64]{1,0:T(8,128)(2,1)S(1)} %slice.125, f32[320,288]{0,1:T(8,128)S(1)} %fusion.30, bf16[320,2048]{1,0:T(8,128)(2,1)} %bitcast.9, bf16[2048,640]{1,0:T(8,128)(2,1)} %bitcast.40), kind=kOutput, calls=%fused_computation.12 | convolution fusion | flops 760600576 | bytes 7053312 | tf_op jit(solution)/shard_map/dot_general | solution.py:249
  303.5 3.7 %all-to-all-start.6 = ((bf16[8,40,2048]{2,1,0:T(8,128)(2,1)}), bf16[8,40,2048]{2,1,0:T(8,128)(2,1)S(1)}, u32[]{:S(2)}, u32[]{:S(2)}) async-start(bf16[8,40,2048]{2,1,0:T(8,128)(2,1)} %bitcast.47), calls=%async_computation.6 | async-start | bytes 2621440 | tf_op jit(solution)/shard_map/all_to_all | solution.py:36
  309.9 32.1 %all-to-all-done.6 = bf16[8,40,2048]{2,1,0:T(8,128)(2,1)S(1)} async-done(((bf16[8,40,2048]{2,1,0:T(8,128)(2,1)}), bf16[8,40,2048]{2,1,0:T(8,128)(2,1)S(1)}, u32[]{:S(2)}, u32[]{:S(2)}) %all-to-all-start.6) | async-done | bytes 1310752 | tf_op jit(solution)/shard_map/all_to_all | solution.py:36
  (109 shorter events, 46.8 us)
Async XLA Ops:
  7.2 24.7 %copy-start = (bf16[128,2048]{1,0:T(8,128)(2,1)S(1)}, bf16[128,2048]{1,0:T(8,128)(2,1)}, u32[]{:S(2)}) copy-start(bf16[128,2048]{1,0:T(8,128)(2,1)} %param.11) | copy-start | bytes 1572868
  7.2 107.6 %all-gather.8.cloned.1.call-start = ((), (), s32[]{:S(2)}) async-start(), calls=%async_computation.8 | async-start | bytes 4128768 | tf_op jit(solution)/shard_map/all_gather | solution.py:186
  24.2 39.5 %all-to-all-start = ((bf16[8,40,2048]{2,1,0:T(8,128)(2,1)}), bf16[8,40,2048]{2,1,0:T(8,128)(2,1)S(1)}, u32[]{:S(2)}, u32[]{:S(2)}) async-start(bf16[8,40,2048]{2,1,0:T(8,128)(2,1)} %bitcast.6), calls=%async_computation | async-start | bytes 2621440 | tf_op jit(solution)/shard_map/all_to_all | solution.py:36
  32.2 36.3 %copy-start.12 = (s32[128,1]{0,1:T(1,128)S(1)}, s32[128,1]{0,1:T(1,128)}, u32[]{:S(2)}) copy-start(s32[128,1]{0,1:T(1,128)} %param.16) | copy-start | bytes 1540
  32.3 38.3 %copy-start.8 = (bf16[128,2048]{1,0:T(8,128)(2,1)S(1)}, bf16[128,2048]{1,0:T(8,128)(2,1)}, u32[]{:S(2)}) copy-start(bf16[128,2048]{1,0:T(8,128)(2,1)} %param.15) | copy-start | bytes 1572868
  64.9 36.1 %all-to-all-start.1 = ((bf16[8,40,2048]{2,1,0:T(8,128)(2,1)}), bf16[8,40,2048]{2,1,0:T(8,128)(2,1)S(1)}, u32[]{:S(2)}, u32[]{:S(2)}) async-start(bf16[8,40,2048]{2,1,0:T(8,128)(2,1)} %bitcast.126), calls=%async_computation.1 | async-start | bytes 2621440 | tf_op jit(solution)/shard_map/all_to_all | solution.py:36
  68.5 182.1 %all-gather.6.cloned.1.call-start = ((), (), s32[]{:S(2)}) async-start(), calls=%async_computation.7 | async-start | bytes 5898240 | tf_op jit(solution)/shard_map/all_gather | solution.py:237
  101.0 7.7 %collective-permute-start = (bf16[8,40,2048]{2,1,0:T(8,128)(2,1)S(1)}, bf16[8,40,2048]{2,1,0:T(8,128)(2,1)}, u32[]{:S(2)}, u32[]{:S(2)}) collective-permute-start(bf16[8,40,2048]{2,1,0:T(8,128)(2,1)S(1)} %all-to-all-done.1), channel_id=1, source_target_pairs={{0,1},{1,0},{2,3},{3,2},{4,5},{5,4},{6,7},{7,6},{8,9},{9,8},{10,11... | collective-permute-start | bytes 3932168 | tf_op jit(solution)/shard_map/ppermute | solution.py:32
  105.9 5.9 %collective-permute-start.1 = (bf16[8,40,2048]{2,1,0:T(8,128)(2,1)S(1)}, bf16[8,40,2048]{2,1,0:T(8,128)(2,1)}, u32[]{:S(2)}, u32[]{:S(2)}) collective-permute-start(bf16[8,40,2048]{2,1,0:T(8,128)(2,1)S(1)} %all-to-all-done), channel_id=1, source_target_pairs={{0,1},{1,0},{2,3},{3,2},{4,5},{5,4},{6,7},{7,6},{8,9},{9,8},{10,11... | collective-permute-start | bytes 3932168 | tf_op jit(solution)/shard_map/ppermute | solution.py:32
  114.8 2.9 copy-start.2
  118.9 1.8 copy-start.3
  121.8 1.7 copy-start.4
  124.7 1.2 slice-start
  130.9 7.5 %copy-start.5 = (bf16[2048,288]{0,1:T(8,128)(2,1)S(1)}, bf16[2048,288]{0,1:T(8,128)(2,1)}, u32[]{:S(2)}) copy-start(bf16[2048,288]{0,1:T(8,128)(2,1)} %copy-done.4) | copy-start | bytes 3538948
  131.9 31.3 %collective-permute-start.2 = (bf16[256,640]{1,0:T(8,128)(2,1)}, bf16[256,640]{1,0:T(8,128)(2,1)}, u32[]{:S(2)}, u32[]{:S(2)}) collective-permute-start(bf16[256,640]{1,0:T(8,128)(2,1)} %get-tuple-element.6), channel_id=1, source_target_pairs={{0,128},{128,256},{256,384},{384,0},{1,129},{129,257},{257,385},{3... | collective-permute-start | bytes 983048 | tf_op jit(solution)/shard_map/ppermute | solution.py:32
  133.8 29.4 %collective-permute-start.4 = (bf16[256,640]{1,0:T(8,128)(2,1)}, bf16[256,640]{1,0:T(8,128)(2,1)}, u32[]{:S(2)}, u32[]{:S(2)}) collective-permute-start(bf16[256,640]{1,0:T(8,128)(2,1)} %get-tuple-element.8), channel_id=1, source_target_pairs={{0,384},{128,0},{256,128},{384,256},{1,385},{129,1},{257,129},{385... | collective-permute-start | bytes 983048 | tf_op jit(solution)/shard_map/ppermute | solution.py:32
  144.0 48.5 %all-to-all-start.3 = ((bf16[8,4,64,224]{3,2,1,0:T(8,128)(2,1)}), bf16[8,4,64,224]{3,2,1,0:T(8,128)(2,1)}, u32[]{:S(2)}, u32[]{:S(2)}) async-start(bf16[8,4,64,224]{3,2,1,0:T(8,128)(2,1)} %copy.31), calls=%async_computation.3 | async-start | bytes 2097152 | tf_op jit(solution)/shard_map/all_to_all | solution.py:36
  165.4 18.5 %collective-permute-start.3 = (bf16[512,640]{1,0:T(8,128)(2,1)}, bf16[512,640]{1,0:T(8,128)(2,1)}, u32[]{:S(2)}, u32[]{:S(2)}) collective-permute-start(bf16[512,640]{1,0:T(8,128)(2,1)} %pad_maximum_fusion.6), channel_id=1, source_target_pairs={{0,128},{128,256},{256,384},{384,0},{1,129},{129,257},{257,385},{3... | collective-permute-start | bytes 1966088 | tf_op jit(solution)/shard_map/ppermute | solution.py:32
  168.2 17.5 %collective-permute-start.5 = (bf16[512,640]{1,0:T(8,128)(2,1)}, bf16[512,640]{1,0:T(8,128)(2,1)}, u32[]{:S(2)}, u32[]{:S(2)}) collective-permute-start(bf16[512,640]{1,0:T(8,128)(2,1)} %pad_maximum_fusion.7), channel_id=1, source_target_pairs={{0,384},{128,0},{256,128},{384,256},{1,385},{129,1},{257,129},{385... | collective-permute-start | bytes 1966088 | tf_op jit(solution)/shard_map/ppermute | solution.py:32
  188.0 27.7 %copy-start.7 = (f32[1,64,864]{2,1,0:T(8,128)S(1)}, f32[1,64,864]{2,1,0:T(8,128)}, u32[]{:S(2)}) copy-start(f32[1,64,864]{2,1,0:T(8,128)} %param.18) | copy-start | bytes 663556
  188.0 27.8 %copy-start.9 = (f32[1,64,864]{2,1,0:T(8,128)S(1)}, f32[1,64,864]{2,1,0:T(8,128)}, u32[]{:S(2)}) copy-start(f32[1,64,864]{2,1,0:T(8,128)} %param.19) | copy-start | bytes 663556
  188.0 27.8 %copy-start.10 = (f32[1,64,864]{2,1,0:T(8,128)S(1)}, f32[1,64,864]{2,1,0:T(8,128)}, u32[]{:S(2)}) copy-start(f32[1,64,864]{2,1,0:T(8,128)} %param.20) | copy-start | bytes 663556
  192.5 23.2 %all-to-all-start.2 = ((bf16[8,64,640]{2,1,0:T(8,128)(2,1)}), bf16[8,64,640]{2,1,0:T(8,128)(2,1)S(1)}, u32[]{:S(2)}, u32[]{:S(2)}) async-start(bf16[8,64,640]{2,1,0:T(8,128)(2,1)} %bitcast.143), calls=%async_computation.2 | async-start | bytes 1310720 | tf_op jit(solution)/shard_map/all_to_all | solution.py:36
  196.0 147.2 %all-gather.10.cloned.1.call-start = ((), (), s32[]{:S(2)}) async-start(), calls=%async_computation.9 | async-start | bytes 5849088 | tf_op jit(solution)/shard_map/all_gather | solution.py:231
  197.5 8.9 %collective-permute-start.6 = (bf16[64,224]{1,0:T(8,128)(2,1)S(1)}, bf16[64,224]{1,0:T(8,128)(2,1)S(1)}, u32[]{:S(2)}, u32[]{:S(2)}) collective-permute-start(bf16[64,224]{1,0:T(8,128)(2,1)S(1)} %get-tuple-element.16), channel_id=1, source_target_pairs={{0,128},{128,256},{256,384},{384,0},{1,129},{129,257},{257,385},{3... | collective-permute-start | bytes 86024 | tf_op jit(solution)/shard_map/ppermute | solution.py:32
  199.4 7.0 %collective-permute-start.7 = (bf16[64,224]{1,0:T(8,128)(2,1)S(1)}, bf16[64,224]{1,0:T(8,128)(2,1)S(1)}, u32[]{:S(2)}, u32[]{:S(2)}) collective-permute-start(bf16[64,224]{1,0:T(8,128)(2,1)S(1)} %get-tuple-element.18), channel_id=1, source_target_pairs={{0,256},{128,384},{256,0},{384,128},{1,257},{129,385},{257,1},{385... | collective-permute-start | bytes 86024 | tf_op jit(solution)/shard_map/ppermute | solution.py:32
  204.5 5.0 %collective-permute-start.8 = (bf16[64,224]{1,0:T(8,128)(2,1)S(1)}, bf16[64,224]{1,0:T(8,128)(2,1)S(1)}, u32[]{:S(2)}, u32[]{:S(2)}) collective-permute-start(bf16[64,224]{1,0:T(8,128)(2,1)S(1)} %get-tuple-element.17), channel_id=1, source_target_pairs={{0,384},{128,0},{256,128},{384,256},{1,385},{129,1},{257,129},{385... | collective-permute-start | bytes 86024 | tf_op jit(solution)/shard_map/ppermute | solution.py:32
  217.8 22.8 %all-to-all-start.4 = ((bf16[8,64,640]{2,1,0:T(8,128)(2,1)}), bf16[8,64,640]{2,1,0:T(8,128)(2,1)S(1)}, u32[]{:S(2)}, u32[]{:S(2)}) async-start(bf16[8,64,640]{2,1,0:T(8,128)(2,1)} %broadcast_in_dim.69), calls=%async_computation.4 | async-start | bytes 1310720 | tf_op jit(solution)/shard_map/all_to_all | solution.py:36
  221.3 7.3 %collective-permute-start.13 = (bf16[64,224]{1,0:T(8,128)(2,1)S(1)}, bf16[64,224]{1,0:T(8,128)(2,1)S(1)}, u32[]{:S(2)}, u32[]{:S(2)}) collective-permute-start(bf16[64,224]{1,0:T(8,128)(2,1)S(1)} %slice.126), channel_id=1, source_target_pairs={{0,384},{128,0},{256,128},{384,256},{1,385},{129,1},{257,129},{385... | collective-permute-start | bytes 86024 | tf_op jit(solution)/shard_map/ppermute | solution.py:32
  223.5 6.5 %collective-permute-start.14 = (bf16[64,224]{1,0:T(8,128)(2,1)S(1)}, bf16[64,224]{1,0:T(8,128)(2,1)S(1)}, u32[]{:S(2)}, u32[]{:S(2)}) collective-permute-start(bf16[64,224]{1,0:T(8,128)(2,1)S(1)} %slice.126), channel_id=1, source_target_pairs={{0,256},{128,384},{256,0},{384,128},{1,257},{129,385},{257,1},{385... | collective-permute-start | bytes 86024 | tf_op jit(solution)/shard_map/ppermute | solution.py:32
  225.6 7.0 %collective-permute-start.15 = (bf16[64,224]{1,0:T(8,128)(2,1)S(1)}, bf16[64,224]{1,0:T(8,128)(2,1)S(1)}, u32[]{:S(2)}, u32[]{:S(2)}) collective-permute-start(bf16[64,224]{1,0:T(8,128)(2,1)S(1)} %slice.126), channel_id=1, source_target_pairs={{0,128},{128,256},{256,384},{384,0},{1,129},{129,257},{257,385},{3... | collective-permute-start | bytes 86024 | tf_op jit(solution)/shard_map/ppermute | solution.py:32
  241.7 32.7 %all-to-all-start.5 = ((bf16[8,4,64,224]{3,2,1,0:T(8,128)(2,1)}), bf16[8,4,64,224]{3,2,1,0:T(8,128)(2,1)S(1)}, u32[]{:S(2)}, u32[]{:S(2)}) async-start(bf16[8,4,64,224]{3,2,1,0:T(8,128)(2,1)} %broadcast_in_dim.79), calls=%async_computation.5 | async-start | bytes 2097152 | tf_op jit(solution)/shard_map/all_to_all | solution.py:36
  245.3 21.3 %collective-permute-start.9 = (bf16[512,640]{1,0:T(8,128)(2,1)S(1)}, bf16[512,640]{1,0:T(8,128)(2,1)S(1)}, u32[]{:S(2)}, u32[]{:S(2)}) collective-permute-start(bf16[512,640]{1,0:T(8,128)(2,1)S(1)} %bitcast.140), channel_id=1, source_target_pairs={{0,384},{128,0},{256,128},{384,256},{1,385},{129,1},{257,129},{385... | collective-permute-start | bytes 1966088 | tf_op jit(solution)/shard_map/ppermute | solution.py:32
  247.2 16.8 %collective-permute-start.10 = (bf16[512,640]{1,0:T(8,128)(2,1)S(1)}, bf16[512,640]{1,0:T(8,128)(2,1)S(1)}, u32[]{:S(2)}, u32[]{:S(2)}) collective-permute-start(bf16[512,640]{1,0:T(8,128)(2,1)S(1)} %bitcast.141), channel_id=1, source_target_pairs={{0,128},{128,256},{256,384},{384,0},{1,129},{129,257},{257,385},{3... | collective-permute-start | bytes 1966088 | tf_op jit(solution)/shard_map/ppermute | solution.py:32
  253.2 27.4 %collective-permute-start.16 = (bf16[320,2048]{1,0:T(8,128)(2,1)}, bf16[320,2048]{1,0:T(8,128)(2,1)}, u32[]{:S(2)}, u32[]{:S(2)}) collective-permute-start(bf16[320,2048]{1,0:T(8,128)(2,1)} %bitcast.9), channel_id=1, source_target_pairs={{0,1},{1,0},{2,3},{3,2},{4,5},{5,4},{6,7},{7,6},{8,9},{9,8},{10,11... | collective-permute-start | bytes 3932168 | tf_op jit(solution)/shard_map/ppermute | solution.py:32
  264.1 12.3 %collective-permute-start.11 = (bf16[256,640]{1,0:T(8,128)(2,1)S(1)}, bf16[256,640]{1,0:T(8,128)(2,1)}, u32[]{:S(2)}, u32[]{:S(2)}) collective-permute-start(bf16[256,640]{1,0:T(8,128)(2,1)S(1)} %slice.121), channel_id=1, source_target_pairs={{0,128},{128,256},{256,384},{384,0},{1,129},{129,257},{257,385},{3... | collective-permute-start | bytes 983048 | tf_op jit(solution)/shard_map/ppermute | solution.py:32
  267.3 9.0 %collective-permute-start.12 = (bf16[256,640]{1,0:T(8,128)(2,1)}, bf16[256,640]{1,0:T(8,128)(2,1)}, u32[]{:S(2)}, u32[]{:S(2)}) collective-permute-start(bf16[256,640]{1,0:T(8,128)(2,1)} %slice.122), channel_id=1, source_target_pairs={{0,384},{128,0},{256,128},{384,256},{1,385},{129,1},{257,129},{385... | collective-permute-start | bytes 983048 | tf_op jit(solution)/shard_map/ppermute | solution.py:32
  279.2 4.0 %copy-start.6 = (bf16[4,8,64,224]{3,2,1,0:T(8,128)(2,1)S(1)}, bf16[4,8,64,224]{3,2,1,0:T(8,128)(2,1)}, u32[]{:S(2)}) copy-start(bf16[4,8,64,224]{3,2,1,0:T(8,128)(2,1)} %copy.32) | copy-start | bytes 2752516
  289.1 8.6 %collective-permute-start.17 = (bf16[320,2048]{1,0:T(8,128)(2,1)}, bf16[320,2048]{1,0:T(8,128)(2,1)S(1)}, u32[]{:S(2)}, u32[]{:S(2)}) collective-permute-start(bf16[320,2048]{1,0:T(8,128)(2,1)} %fusion), channel_id=1, source_target_pairs={{0,1},{1,0},{2,3},{3,2},{4,5},{5,4},{6,7},{7,6},{8,9},{9,8},{10,11... | collective-permute-start | bytes 3932168 | tf_op jit(solution)/shard_map/ppermute | solution.py:32
  303.5 3.7 %copy-start.13 = (s32[16]{0:T(128)S(1)}, s32[16]{0:T(128)}, u32[]{:S(2)}) copy-start(s32[16]{0:T(128)} %param.21) | copy-start | bytes 196
  303.5 38.5 %copy-start.11 = (f32[128,1]{0,1:T(1,128)S(1)}, f32[128,1]{0,1:T(1,128)}, u32[]{:S(2)}) copy-start(f32[128,1]{0,1:T(1,128)} %param.17) | copy-start | bytes 1540
  303.5 38.4 %all-to-all-start.6 = ((bf16[8,40,2048]{2,1,0:T(8,128)(2,1)}), bf16[8,40,2048]{2,1,0:T(8,128)(2,1)S(1)}, u32[]{:S(2)}, u32[]{:S(2)}) async-start(bf16[8,40,2048]{2,1,0:T(8,128)(2,1)} %bitcast.47), calls=%async_computation.6 | async-start | bytes 2621440 | tf_op jit(solution)/shard_map/all_to_all | solution.py:36
  307.2 37.9 %copy-start.1 = (bf16[128,2048]{1,0:T(8,128)(2,1)S(1)}, bf16[128,2048]{1,0:T(8,128)(2,1)}, u32[]{:S(2)}) copy-start(bf16[128,2048]{1,0:T(8,128)(2,1)} %param.11) | copy-start | bytes 1572868
Sparse Core Ops, SparseCore 0:
  20.0 60.6 all-gather.7
  82.8 68.3 all-gather.5
  216.9 38.6 all-gather.9

commit v2 on v1

v2 whole, which is shorter than its diff:
```python
import jax
import jax.numpy as jnp
from jax import lax
from jax.experimental import pallas as pl
from jax.experimental.pallas import tpu as pltpu
from jax.sharding import Mesh
from jax.sharding import PartitionSpec as P

D = 2048
HID = 1152
EXPERTS = 4
CAP = 40
SLOTS = EXPERTS * CAP
DP = ("x", "z")
EXPERT = ("y", "core")
ALL = DP + EXPERT
WIDTH = 288
MAIN = 256
TAIL = WIDTH - MAIN
FIRST = 2 * MAIN + 128
IN_SCALE = 2048 ** (-0.5)
OUT_SCALE = HID ** (-0.5)
TEST = False


beta_one = 0.9
beta_two = 0.95
learn_rate = 0.2
decay_rate = 0.1
adam_step = 10.0
adam_eps = 1e-08


def around(axis, by):
    size = lax.axis_size(axis)
    return [(k, (k + by) % size) for k in range(size)]


def pass_on(value, axis, by):
    return lax.ppermute(value, axis, around(axis, by))


def exchange(value, axis):
    return lax.all_to_all(value, axis, split_axis=0, concat_axis=0, tiled=True)


def slot_of(routes):
    ids = routes.reshape(-1)
    one_hot = ids[:, None] == jnp.arange(EXPERTS, dtype=jnp.int32)[None, :]
    count = ids.shape[0]
    before = lax.broadcasted_iota(jnp.int32, (count, count), 1) < lax.broadcasted_iota(
        jnp.int32, (count, count), 0
    )
    earlier = jnp.dot(
        before.astype(jnp.bfloat16),
        one_hot.astype(jnp.bfloat16),
        preferred_element_type=jnp.float32,
    )
    slots = jnp.sum(jnp.where(one_hot, earlier, 0.0), axis=1).astype(jnp.int32)
    return ids * CAP + slots


def to_slots(targets, payload):
    rows = lax.broadcasted_iota(jnp.int32, (SLOTS, targets.shape[0]), 0)
    selector = (rows == targets[None, :]).astype(jnp.bfloat16)
    filled = jnp.dot(selector, payload, preferred_element_type=jnp.float32)
    return filled.astype(jnp.bfloat16).reshape(EXPERTS, CAP, payload.shape[1])


def after(value, other):
    one = other[(0,) * other.ndim]
    return value + (one != one).astype(value.dtype)


def to_chips(slots):
    chips = lax.axis_size("y")
    return exchange(jnp.repeat(slots, chips // EXPERTS, axis=0), "y")


def chunk_of(parts, offset):
    return lax.dynamic_index_in_dim(
        parts, lax.rem(lax.axis_index("x") + offset, 4), 0, keepdims=False
    )


def f32(value):
    return value.astype(jnp.float32)


def b16(value):
    return value.astype(jnp.bfloat16)


def sum_along_x(parts):
    far = chunk_of(parts, 2)
    half = far.shape[0] // 2
    top = pass_on(far[:half], "x", 1)
    bottom = pass_on(far[half:], "x", -1)
    after, before = chunk_of(parts, 1), chunk_of(parts, 3)
    after = jnp.concatenate([b16(f32(after[:half]) + f32(top)), after[half:]], axis=0)
    before = jnp.concatenate([before[:half], b16(f32(before[half:]) + f32(bottom))], axis=0)
    from_left = pass_on(after, "x", 1)
    from_right = pass_on(before, "x", -1)
    return f32(chunk_of(parts, 0)) + f32(from_left) + f32(from_right)


def sum_small_along_x(parts):
    total = f32(chunk_of(parts, 0))
    for by in (1, 2, 3):
        total = total + f32(pass_on(chunk_of(parts, by), "x", by))
    return total


def in_x_order(found):
    me = lax.axis_index("x")
    out = jnp.zeros((4,) + found[0].shape, found[0].dtype)
    for k, value in enumerate(found):
        out = lax.dynamic_update_index_in_dim(out, value, lax.rem(me + k, 4), 0)
    return out


def gather_small_along_x(value):
    return in_x_order([value] + [pass_on(value, "x", -by) for by in (1, 2, 3)])


def gather_along_z(value):
    size = lax.axis_size("z")
    return exchange(jnp.broadcast_to(value[None], (size,) + value.shape), "z")


def sum_along_z(value):
    got = exchange(value, "z")
    return jnp.sum(f32(got), axis=0)


def arranged(value):
    gate, up, down = (value[:, k * WIDTH : (k + 1) * WIDTH] for k in range(3))
    spare = jnp.zeros((value.shape[0], 128 - 3 * TAIL), value.dtype)
    tails = [gate[:, MAIN:], up[:, MAIN:], down[:, MAIN:], spare]
    return jnp.concatenate([gate[:, :MAIN], up[:, :MAIN]] + tails, axis=1), down[:, :MAIN]


def in_place(first, second):
    tails = [first[:, 2 * MAIN + k * TAIL : 2 * MAIN + (k + 1) * TAIL] for k in range(3)]
    mains = [first[:, :MAIN], first[:, MAIN : 2 * MAIN], second]
    return jnp.concatenate([mains[0], tails[0], mains[1], tails[1], mains[2], tails[2]], axis=1)


def own_rows(first, second):
    size_z, rows = second.shape[0], second.shape[2]
    half_second = b16(sum_along_z(second))
    half_first = b16(sum_along_x(first))
    own_second = sum_small_along_x(half_second)
    own_first = sum_along_z(half_first.reshape(size_z, rows, -1))
    return in_place(own_first, own_second)


def all_rows(value):
    first, second = arranged(value)
    wide_first = gather_along_z(first)
    wide_second = gather_small_along_x(second)
    all_second = gather_along_z(wide_second)
    return found_along_x(wide_first.reshape(-1, wide_first.shape[-1])), all_second


def found_along_x(value):
    half = value.shape[0] // 2
    left = pass_on(value, "x", 1)
    right = pass_on(value, "x", -1)
    top = pass_on(left[:half], "x", 1)
    bottom = pass_on(right[half:], "x", -1)
    return value, right, top, bottom, left


def dot(a, b, dims=((1,), (0,))):
    return lax.dot_general(a, b, (dims, ((), ())), preferred_element_type=jnp.float32)


def lanes(shape):
    return lax.broadcasted_iota(jnp.int32, shape, 1)


def back_terms(gate, up, down_back):
    sigmoid_gate = jax.nn.sigmoid(gate)
    silu_gate = gate * sigmoid_gate
    return (
        silu_gate * up,
        down_back * up * sigmoid_gate * (1.0 + gate * (1.0 - sigmoid_gate)),
        down_back * silu_gate,
    )


def step_body(own_in, other_in, own_sc, other_sc, w, out_a, out_b, wn, pre, dn, g_in, g_sc):
    size_z, size_x, rows = w.shape[:3]
    wide = size_z * rows
    count = own_in.shape[0]
    for k in range(size_x):
        wn[k * wide : (k + 1) * wide, :] = w[:, k].reshape(wide, w.shape[3])
    for half, (taken, scaled) in enumerate(((own_in, own_sc), (other_in, other_sc))):
        span = slice(half * count, (half + 1) * count)
        pre[span, :] = dot(taken[...], wn[:, :FIRST]) * IN_SCALE
        dn[span, :] = dot(scaled[...], wn[:, 2 * MAIN :]) * OUT_SCALE

    def chunk(i, carry):
        at = pl.ds(pl.multiple_of(i * 64, 64), 64)
        act, gate_grad, up_grad = back_terms(
            pre[at, :MAIN], pre[at, MAIN : 2 * MAIN], dn[at, 128:]
        )
        tail, down_tail = pre[at, 2 * MAIN :], dn[at, :128]
        lane = lanes(tail.shape)
        act_t, gate_t, up_t = back_terms(
            tail, pltpu.roll(tail, 128 - TAIL, 1), pltpu.roll(down_tail, 128 - 2 * TAIL, 1)
        )
        tail_in = jnp.where(
            lane < TAIL, gate_t, jnp.where(lane < 2 * TAIL, pltpu.roll(up_t, TAIL, 1), 0.0)
        )
        here = (lane >= 2 * TAIL) & (lane < 3 * TAIL)
        tail_sc = jnp.where(here, pltpu.roll(act_t, 2 * TAIL, 1), 0.0)
        g_in[at, :MAIN] = b16(gate_grad)
        g_in[at, MAIN : 2 * MAIN] = b16(up_grad)
        g_in[at, 2 * MAIN :] = b16(tail_in)
        g_sc[at, :128] = b16(tail_sc)
        g_sc[at, 128:] = b16(act)
        return carry

    lax.fori_loop(0, 2 * count // 64, chunk, 0)
    over_rows = ((0,), (0,))
    for k in range(size_x):
        cols = slice(k * wide, (k + 1) * wide)
        a = dot(own_in[:, cols], g_in[:count, :], over_rows)
        a = (a + dot(other_in[:, cols], g_in[count:, :], over_rows)) * IN_SCALE
        b = dot(own_sc[:, cols], g_sc[:count, :], over_rows)
        b = (b + dot(other_sc[:, cols], g_sc[count:, :], over_rows)) * OUT_SCALE
        out_a[k, :, : 2 * MAIN] = b16(a[:, : 2 * MAIN])
        out_a[k, :, 2 * MAIN :] = b16(a[:, 2 * MAIN :] + b[:, :128])
        out_b[:, k] = b16(b[:, 128:]).reshape(size_z, rows, MAIN)


def step_gradients(own_in, other_in, own_sc, other_sc, w):
    size_z, size_x, rows, columns = w.shape
    count = own_in.shape[0]
    return pl.pallas_call(
        step_body,
        out_shape=(
            jax.ShapeDtypeStruct((size_x, size_z * rows, FIRST), jnp.bfloat16),
            jax.ShapeDtypeStruct((size_z, size_x, rows, MAIN), jnp.bfloat16),
        ),
        scratch_shapes=[
            pltpu.VMEM((D, columns), jnp.bfloat16),
            pltpu.VMEM((2 * count, FIRST), jnp.float32),
            pltpu.VMEM((2 * count, 128 + MAIN), jnp.float32),
            pltpu.VMEM((2 * count, FIRST), jnp.bfloat16),
            pltpu.VMEM((2 * count, 128 + MAIN), jnp.bfloat16),
        ],
        interpret=TEST,
        name="step_gradients",
    )(own_in, other_in, own_sc, other_sc, w)


def serve_body(me, taken, own, right, top, bottom, left, second, out, wn, pre, act):
    size_z, size_x, rows = second.shape[:3]
    wide = size_z * rows
    half = wide // 2

    def start_of(offset):
        return pl.multiple_of(lax.rem(me[0] + offset, size_x) * wide, wide)

    wn[pl.ds(start_of(0), wide), :] = own[...]
    wn[pl.ds(start_of(1), wide), :] = right[...]
    wn[pl.ds(start_of(2), half), :] = top[...]
    wn[pl.ds(pl.multiple_of(start_of(2) + half, half), half), :] = bottom[...]
    wn[pl.ds(start_of(3), wide), :] = left[...]
    pre[...] = dot(taken[...], wn[...]) * IN_SCALE

    def chunk(i, carry):
        at = pl.ds(pl.multiple_of(i * 64, 64), 64)
        gate, up = pre[at, :MAIN], pre[at, MAIN : 2 * MAIN]
        tail = pre[at, 2 * MAIN :]
        lane = lanes(tail.shape)
        act_t = tail * jax.nn.sigmoid(tail) * pltpu.roll(tail, 128 - TAIL, 1)
        here = (lane >= 2 * TAIL) & (lane < 3 * TAIL)
        act[at, :128] = b16(jnp.where(here, pltpu.roll(act_t, 2 * TAIL, 1), 0.0))
        act[at, 128:] = b16(gate * jax.nn.sigmoid(gate) * up)
        return carry

    lax.fori_loop(0, taken.shape[0] // 64, chunk, 0)
    for k in range(size_x):
        cols = slice(k * wide, (k + 1) * wide)
        total = dot(act[:, :128], wn[cols, 2 * MAIN :], ((1,), (1,)))
        total = total + dot(act[:, 128:], second[:, k].reshape(wide, MAIN), ((1,), (1,)))
        out[:, cols] = b16(total * OUT_SCALE)


def serve(taken, pieces, second):
    me = lax.axis_index("x").astype(jnp.int32).reshape(1)
    return pl.pallas_call(
        serve_body,
        out_shape=jax.ShapeDtypeStruct(taken.shape, jnp.bfloat16),
        in_specs=[pl.BlockSpec(memory_space=pltpu.SMEM)]
        + [pl.BlockSpec(memory_space=pltpu.VMEM)] * 7,
        scratch_shapes=[
            pltpu.VMEM((D, FIRST), jnp.bfloat16),
            pltpu.VMEM((taken.shape[0], FIRST), jnp.float32),
            pltpu.VMEM((taken.shape[0], 128 + MAIN), jnp.bfloat16),
        ],
        interpret=TEST,
        name="serve",
    )(me, taken, *pieces, second)


def whole_step(
    step_inputs,
    step_cotangent,
    step_routes,
    step_gates,
    next_inputs,
    next_routes,
    next_gates,
    master_weights,
    first_moment,
    second_moment,
    owner_plan,
):
    groups = lax.axis_size(EXPERT)
    old_weights = master_weights[0]
    step_targets = slot_of(step_routes)
    scaled = b16(f32(step_cotangent) * step_gates)
    sent_inputs = to_slots(step_targets, step_inputs)
    parts = lax.all_gather(
        jnp.concatenate(arranged(b16(old_weights)), axis=1), "x", axis=0
    )
    weights = lax.all_gather(parts, "z", axis=0)
    got_inputs = to_chips(sent_inputs)
    got_scaled = to_chips(to_slots(step_targets, scaled))
    other_inputs = pass_on(got_inputs, "core", 1)
    other_scaled = pass_on(got_scaled, "core", 1)
    rows_in_scaled = [
        rows.reshape(-1, D) for rows in (got_inputs, other_inputs, got_scaled, other_scaled)
    ]
    gradient = own_rows(*step_gradients(*rows_in_scaled, weights))
    first_new = beta_one * first_moment[0] + (1.0 - beta_one) * gradient
    second_new = beta_two * second_moment[0] + (1.0 - beta_two) * gradient * gradient
    first_hat = first_new / (1.0 - beta_one**adam_step)
    second_hat = second_new / (1.0 - beta_two**adam_step)
    new_weights = old_weights - learn_rate * (
        first_hat / (jnp.sqrt(second_hat) + adam_eps) + decay_rate * old_weights
    )
    pieces, second = all_rows(b16(new_weights))

    positions = jnp.arange(groups, dtype=jnp.int32)
    me = lax.axis_index(EXPERT)
    holder = jnp.sum(jnp.where(owner_plan == me, positions, 0))
    stacked = jnp.concatenate([b16(new_weights), b16(first_new), b16(second_new)], axis=0)
    everywhere = lax.all_gather(stacked, EXPERT, axis=0)
    relocated = lax.dynamic_index_in_dim(everywhere, holder, 0, keepdims=False)
    relocated = f32(relocated).reshape(3, 1, new_weights.shape[0], new_weights.shape[1])

    next_targets = slot_of(next_routes)
    next_slots = to_slots(after(next_targets, other_inputs), next_inputs)
    column = lax.all_gather(next_slots, "y", axis=0)
    chips_each = lax.axis_size("y") // EXPERTS
    here = lax.axis_index("y") // chips_each
    own_next = lax.dynamic_index_in_dim(column, here, 1, keepdims=False).reshape(-1, D)
    other_next = pass_on(own_next, "core", 1)
    met = pass_on(serve(other_next, pieces, second), "core", 1)
    partials = b16(f32(serve(own_next, pieces, second)) + f32(met))
    partials = partials.reshape(-1, CAP, D)
    returned = exchange(partials, "y")
    returned = returned.reshape(-1, D)
    chip_rows = returned.shape[0]
    slot = lax.broadcasted_iota(jnp.int32, (next_targets.shape[0], chip_rows), 1)
    expert_slot = (slot // (chips_each * CAP)) * CAP + lax.rem(slot, CAP)
    picks = (next_targets[:, None] == expert_slot).astype(jnp.bfloat16)
    pair_sums = jnp.dot(picks, returned, preferred_element_type=jnp.float32)
    layer_output = b16(pair_sums * next_gates)
    return (layer_output, relocated[0], relocated[1], relocated[2])


def solution(mesh):
    chips = mesh.devices.reshape(4, -1, mesh.shape["expert"] // 2, 2)
    tokens = P(ALL, None)
    slabs = P(EXPERT, DP, None)
    return jax.shard_map(
        whole_step,
        mesh=Mesh(chips, ALL),
        in_specs=(tokens,) * 7 + (slabs,) * 3 + (P(),),
        out_specs=(tokens,) + (slabs,) * 3,
        check_vma=False,
    )
```

time: 354 us -> 353 us (level)
  blocking collectives: 11.7 us -> 90.8 us
  waiting for transfers between devices: 139 us -> 88.4 us
  Pallas kernels: 0 us -> 30.1 us
  matrix products: 30.3 us -> 4.53 us
  local copies, waits for them, and re-layouts: 29 us -> 11.1 us
  other arithmetic: 21.3 us -> 10.5 us
  starting transfers between devices: 103 us -> 98 us
    all_to_all x0 -> x2, blocking collectives: none -> 79.1 us  [exchange(): return lax.all_to_all(value, axis, split_axis=0, concat_axis=0, tiled=True)]
    all_to_all x7 -> x5, waiting for transfers between devices: 112 us -> 39.6 us  [exchange(): return lax.all_to_all(value, axis, split_axis=0, concat_axis=0, tiled=True)]
    pallas_call x0 -> x3, Pallas kernels: none -> 30.1 us  [the longest x1 15.8 us: step_gradients(): pl.pallas_call(step_body, out_shape=(jax.ShapeDtypeStruct((size_x, size_z...]
    dot_general x10 -> x0, matrix products: 25.1 us -> none  [the longest x2 11.6 us: partial_of(): lax.dot_general(next_activation, down, (((1,), (1,)), ((), ())), preferre...]
    ppermute x18, waiting for transfers between devices: 27.2 us -> 48.7 us  [pass_on(): return lax.ppermute(value, axis, around(axis, by))]
    all_to_all x7 -> x5, starting transfers between devices: 44.8 us -> 29.4 us  [exchange(): return lax.all_to_all(value, axis, split_axis=0, concat_axis=0, tiled=True)]
    ppermute x18, starting transfers between devices: 57.9 us -> 68.3 us  [pass_on(): return lax.ppermute(value, axis, around(axis, by))]
    concatenate x3 -> x0, other arithmetic: 8 us -> none  [the longest x2 6.14 us: both_cores(): return jnp.concatenate([rows, pass_on(rows, 'core', 1)], axis=0)]
  transfers between devices with their start and end apart: 28 -> 26, of which waited for: 15 -> 15; matrix products, arithmetic and copies ran while one was open for 22% -> 6% of each run, Pallas kernels for 0% -> 9%
where the time goes in v2:
time: 353 us; the launch traced here: 351 us
  starting transfers between devices  98 us (28%)
  blocking collectives  90.8 us (26%)
  waiting for transfers between devices  88.4 us (25%)
  Pallas kernels  30.1 us (9%)
  between operations  17.7 us (5%)
  local copies, waits for them, and re-layouts  11.1 us (3%)
  other arithmetic  10.5 us (3%)
  matrix products  4.53 us (1%)
    all_to_all x2, blocking collectives, exchange(): return lax.all_to_all(value, axis, split_axis=0, concat_axis=0, tiled=True)  79.1 us
    ppermute x18, starting transfers between devices, pass_on(): return lax.ppermute(value, axis, around(axis, by))  68.3 us
    ppermute x18, waiting for transfers between devices, pass_on(): return lax.ppermute(value, axis, around(axis, by))  48.7 us
    all_to_all x5, waiting for transfers between devices, exchange(): return lax.all_to_all(value, axis, split_axis=0, concat_axis=0, tiled=True)  39.6 us
    all_to_all x5, starting transfers between devices, exchange(): return lax.all_to_all(value, axis, split_axis=0, concat_axis=0, tiled=True)  29.4 us
    pallas_call x1, Pallas kernels, step_gradients(): pl.pallas_call(step_body, out_shape=(jax.ShapeDtypeStruct((size_x, size_z...  15.8 us
    pallas_call x2, Pallas kernels, serve(): pl.pallas_call(serve_body, out_shape=jax.ShapeDtypeStruct(taken.shape, jn...  14.3 us
    all_gather x1, blocking collectives, whole_step(): lax.all_gather(jnp.concatenate(arranged(b16(old_weights)), axis=1), 'x',...  11.7 us
  transfers between devices with their start and end apart: 26, of which 15 were waited for; matrix products, arithmetic and copies ran while one was open for 6% of the time, Pallas kernels for 9%

profile of v2, /device:TPU:1, one launch (start us, length us, event | category | flops | bytes accessed | tf_op | source)
XLA Modules:
  0.0 351.1 jit_solution(10105297328799298859)
XLA Ops:
  8.5 11.7 %all-gather = bf16[256,896]{1,0:T(8,128)(2,1)} all-gather(bf16[64,896]{1,0:T(8,128)(2,1)S(1)} %concatenate.18), channel_id=2, replica_groups=mesh['x'=4,'z'=8,'y'=8,'core'=2] {'x'}, dimensions={0}, use_global_device_ids=true | all-gather | bytes 573440 | tf_op jit(solution)/shard_map/all_gather | solution.py:329
  21.0 37.6 %all_to_all.35 = bf16[8,40,2048]{2,1,0:T(8,128)(2,1)S(1)} all-to-all(bf16[8,40,2048]{2,1,0:T(8,128)(2,1)S(1)} %bitcast.105), channel_id=1, replica_groups=mesh['x'=4,'z'=8,'y'=8,'core'=2] {'y'}, dimensions={0} | all-to-all | bytes 2621440 | tf_op jit(solution)/shard_map/all_to_all | solution.py:44
  58.6 7.4 %collective-permute-start = (bf16[8,40,2048]{2,1,0:T(8,128)(2,1)S(1)}, bf16[8,40,2048]{2,1,0:T(8,128)(2,1)S(1)}, u32[]{:S(2)}, u32[]{:S(2)}) collective-permute-start(bf16[8,40,2048]{2,1,0:T(8,128)(2,1)S(1)} %all_to_all.35), channel_id=1, source_target_pairs={{0,1},{1,0},{2,3},{3,2},{4,5},{5,4},{6,7},{7,6},{8,9},{9,8},{10,11... | collective-permute-start | bytes 3932168 | tf_op jit(solution)/shard_map/ppermute | solution.py:40
  66.1 2.5 collective-permute-done
  71.7 1.4 convolution_convert_fusion
  73.3 41.5 %all_to_all.36 = bf16[8,40,2048]{2,1,0:T(8,128)(2,1)S(1)} all-to-all(bf16[8,40,2048]{2,1,0:T(8,128)(2,1)S(1)} %bitcast.106), channel_id=1, replica_groups=mesh['x'=4,'z'=8,'y'=8,'core'=2] {'y'}, dimensions={0} | all-to-all | bytes 2621440 | tf_op jit(solution)/shard_map/all_to_all | solution.py:44
  114.8 2.8 collective-permute-start.1
  117.6 2.6 collective-permute-done.1
  121.4 15.8 %step_gradients.1 = (bf16[4,512,640]{2,1,0:T(8,128)(2,1)}, bf16[8,4,64,256]{3,2,1,0:T(8,128)(2,1)}) custom-call(bf16[320,2048]{1,0:T(8,128)(2,1)} %bitcast.102, bf16[320,2048]{1,0:T(8,128)(2,1)} %bitcast.114, bf16[320,2048]{1,0:T(8,128)(2,1)} %bitcast.103, bf16[320,2048]{1,0:T(8,128)(2,1)} %bitcast.115, bf16[8,4,64,896]{3,2,1,0:T(8,128)(2,1)} %bitcast.109), custom_call_target="tpu_custom_call" | custom-call | tf_op jit(solution)/shard_map/step_gradients/pallas_call | solution.py:242
  137.2 12.5 %all-to-all-start.3 = ((bf16[8,4,64,256]{3,2,1,0:T(8,128)(2,1)}), bf16[8,4,64,256]{3,2,1,0:T(8,128)(2,1)S(1)}, u32[]{:S(2)}, u32[]{:S(2)}) async-start(bf16[8,4,64,256]{3,2,1,0:T(8,128)(2,1)} %get-tuple-element.7), calls=%async_computation.3 | async-start | bytes 2097152 | tf_op jit(solution)/shard_map/all_to_all | solution.py:44
  149.7 1.4 dynamic-slice_bitcast_fusion.4
  151.1 1.9 collective-permute-start.2
  153.0 4.6 %collective-permute-start.4 = (bf16[256,640]{1,0:T(8,128)(2,1)S(1)}, bf16[256,640]{1,0:T(8,128)(2,1)S(1)}, u32[]{:S(2)}, u32[]{:S(2)}) collective-permute-start(bf16[256,640]{1,0:T(8,128)(2,1)S(1)} %get-tuple-element.12), channel_id=1, source_target_pairs={{0,384},{128,0},{256,128},{384,256},{1,385},{129,1},{257,129},{385... | collective-permute-start | bytes 983048 | tf_op jit(solution)/shard_map/ppermute | solution.py:40
  157.6 5.2 %collective-permute-done.2 = bf16[256,640]{1,0:T(8,128)(2,1)S(1)} collective-permute-done((bf16[256,640]{1,0:T(8,128)(2,1)S(1)}, bf16[256,640]{1,0:T(8,128)(2,1)S(1)}, u32[]{:S(2)}, u32[]{:S(2)}) %collective-permute-start.2) | collective-permute-done | bytes 327712 | tf_op jit(solution)/shard_map/ppermute | solution.py:40
  165.0 1.9 collective-permute-start.3
  167.0 5.3 %collective-permute-start.5 = (bf16[512,640]{1,0:T(8,128)(2,1)S(1)}, bf16[512,640]{1,0:T(8,128)(2,1)}, u32[]{:S(2)}, u32[]{:S(2)}) collective-permute-start(bf16[512,640]{1,0:T(8,128)(2,1)S(1)} %pad_maximum_fusion.1), channel_id=1, source_target_pairs={{0,384},{128,0},{256,128},{384,256},{1,385},{129,1},{257,129},{385... | collective-permute-start | bytes 1966088 | tf_op jit(solution)/shard_map/ppermute | solution.py:40
  172.3 11.3 %collective-permute-done.3 = bf16[512,640]{1,0:T(8,128)(2,1)S(1)} collective-permute-done((bf16[512,640]{1,0:T(8,128)(2,1)S(1)}, bf16[512,640]{1,0:T(8,128)(2,1)S(1)}, u32[]{:S(2)}, u32[]{:S(2)}) %collective-permute-start.3) | collective-permute-done | bytes 655392 | tf_op jit(solution)/shard_map/ppermute | solution.py:40
  184.6 2.4 fusion.2
  187.0 6.1 %all-to-all-start.2 = ((bf16[8,64,640]{2,1,0:T(8,128)(2,1)}), bf16[8,64,640]{2,1,0:T(8,128)(2,1)S(1)}, u32[]{:S(2)}, u32[]{:S(2)}) async-start(bf16[8,64,640]{2,1,0:T(8,128)(2,1)} %bitcast.29), calls=%async_computation.2 | async-start | bytes 1310720 | tf_op jit(solution)/shard_map/all_to_all | solution.py:44
  193.5 3.7 %collective-permute-start.6 = (bf16[64,256]{1,0:T(8,128)(2,1)S(1)}, bf16[64,256]{1,0:T(8,128)(2,1)S(1)}, u32[]{:S(2)}, u32[]{:S(2)}) collective-permute-start(bf16[64,256]{1,0:T(8,128)(2,1)S(1)} %get-tuple-element.25), channel_id=1, source_target_pairs={{0,128},{128,256},{256,384},{384,0},{1,129},{129,257},{257,385},{3... | collective-permute-start | bytes 98312 | tf_op jit(solution)/shard_map/ppermute | solution.py:40
  197.2 4.9 %collective-permute-start.7 = (bf16[64,256]{1,0:T(8,128)(2,1)S(1)}, bf16[64,256]{1,0:T(8,128)(2,1)S(1)}, u32[]{:S(2)}, u32[]{:S(2)}) collective-permute-start(bf16[64,256]{1,0:T(8,128)(2,1)S(1)} %get-tuple-element.27), channel_id=1, source_target_pairs={{0,256},{128,384},{256,0},{384,128},{1,257},{129,385},{257,1},{385... | collective-permute-start | bytes 98312 | tf_op jit(solution)/shard_map/ppermute | solution.py:40
  202.2 2.5 collective-permute-start.8
  204.7 2.5 collective-permute-done.8
  207.2 3.8 %all-to-all-done.2 = bf16[8,64,640]{2,1,0:T(8,128)(2,1)S(1)} async-done(((bf16[8,64,640]{2,1,0:T(8,128)(2,1)}), bf16[8,64,640]{2,1,0:T(8,128)(2,1)S(1)}, u32[]{:S(2)}, u32[]{:S(2)}) %all-to-all-start.2) | async-done | bytes 655392 | tf_op jit(solution)/shard_map/all_to_all | solution.py:44
  213.5 3.5 %all-to-all-start.4 = ((bf16[8,64,640]{2,1,0:T(8,128)(2,1)}), bf16[8,64,640]{2,1,0:T(8,128)(2,1)S(1)}, u32[]{:S(2)}, u32[]{:S(2)}) async-start(bf16[8,64,640]{2,1,0:T(8,128)(2,1)} %broadcast_in_dim.52), calls=%async_computation.4 | async-start | bytes 1310720 | tf_op jit(solution)/shard_map/all_to_all | solution.py:44
  217.1 5.4 %collective-permute-start.13 = (bf16[64,256]{1,0:T(8,128)(2,1)S(1)}, bf16[64,256]{1,0:T(8,128)(2,1)S(1)}, u32[]{:S(2)}, u32[]{:S(2)}) collective-permute-start(bf16[64,256]{1,0:T(8,128)(2,1)S(1)} %get-tuple-element.28), channel_id=1, source_target_pairs={{0,384},{128,0},{256,128},{384,256},{1,385},{129,1},{257,129},{385... | collective-permute-start | bytes 98312 | tf_op jit(solution)/shard_map/ppermute | solution.py:40
  222.5 1.9 collective-permute-start.14
  224.4 2.5 collective-permute-start.15
  227.1 1.9 collective-permute-done.14
  229.0 1.6 collective-permute-done.15
  230.6 3.7 %all-to-all-done.4 = bf16[8,64,640]{2,1,0:T(8,128)(2,1)S(1)} async-done(((bf16[8,64,640]{2,1,0:T(8,128)(2,1)}), bf16[8,64,640]{2,1,0:T(8,128)(2,1)S(1)}, u32[]{:S(2)}, u32[]{:S(2)}) %all-to-all-start.4) | async-done | bytes 655392 | tf_op jit(solution)/shard_map/all_to_all | solution.py:44
  234.3 1.3 broadcast_in_dim.58
  235.6 3.6 %all-to-all-start.5 = ((bf16[8,4,64,256]{3,2,1,0:T(8,128)(2,1)}), bf16[8,4,64,256]{3,2,1,0:T(8,128)(2,1)S(1)}, u32[]{:S(2)}, u32[]{:S(2)}) async-start(bf16[8,4,64,256]{3,2,1,0:T(8,128)(2,1)} %broadcast_in_dim.58), calls=%async_computation.5 | async-start | bytes 2097152 | tf_op jit(solution)/shard_map/all_to_all | solution.py:44
  239.2 1.4 constant_dynamic-slice_fusion
  240.6 6.6 %collective-permute-start.16 = (bf16[320,2048]{1,0:T(8,128)(2,1)S(1)}, bf16[320,2048]{1,0:T(8,128)(2,1)}, u32[]{:S(2)}, u32[]{:S(2)}) collective-permute-start(bf16[320,2048]{1,0:T(8,128)(2,1)S(1)} %bitcast.107), channel_id=1, source_target_pairs={{0,1},{1,0},{2,3},{3,2},{4,5},{5,4},{6,7},{7,6},{8,9},{9,8},{10,11... | collective-permute-start | bytes 3932168 | tf_op jit(solution)/shard_map/ppermute | solution.py:40
  247.2 3.0 collective-permute-start.10
  250.2 3.7 %collective-permute-start.9 = (bf16[512,640]{1,0:T(8,128)(2,1)S(1)}, bf16[512,640]{1,0:T(8,128)(2,1)S(1)}, u32[]{:S(2)}, u32[]{:S(2)}) collective-permute-start(bf16[512,640]{1,0:T(8,128)(2,1)S(1)} %bitcast.99), channel_id=1, source_target_pairs={{0,384},{128,0},{256,128},{384,256},{1,385},{129,1},{257,129},{385... | collective-permute-start | bytes 1966088 | tf_op jit(solution)/shard_map/ppermute | solution.py:40
  253.9 13.1 %collective-permute-done.10.left = bf16[512,640]{1,0:T(8,128)(2,1)S(1)} collective-permute-done((bf16[512,640]{1,0:T(8,128)(2,1)S(1)}, bf16[512,640]{1,0:T(8,128)(2,1)S(1)}, u32[]{:S(2)}, u32[]{:S(2)}) %collective-permute-start.10) | collective-permute-done | bytes 655392 | tf_op jit(solution)/shard_map/ppermute | solution.py:40
  267.8 1.9 collective-permute-start.11
  270.6 4.6 %collective-permute-start.12 = (bf16[256,640]{1,0:T(8,128)(2,1)S(1)}, bf16[256,640]{1,0:T(8,128)(2,1)S(1)}, u32[]{:S(2)}, u32[]{:S(2)}) collective-permute-start(bf16[256,640]{1,0:T(8,128)(2,1)S(1)} %slice.176), channel_id=1, source_target_pairs={{0,384},{128,0},{256,128},{384,256},{1,385},{129,1},{257,129},{385... | collective-permute-start | bytes 983048 | tf_op jit(solution)/shard_map/ppermute | solution.py:40
  275.2 4.7 %collective-permute-done.11.top = bf16[256,640]{1,0:T(8,128)(2,1)} collective-permute-done((bf16[256,640]{1,0:T(8,128)(2,1)}, bf16[256,640]{1,0:T(8,128)(2,1)}, u32[]{:S(2)}, u32[]{:S(2)}) %collective-permute-start.11) | collective-permute-done | bytes 327712 | tf_op jit(solution)/shard_map/ppermute | solution.py:40
  279.8 1.4 collective-permute-done.12.bottom
  282.0 7.2 %serve.3 = bf16[320,2048]{1,0:T(8,128)(2,1)} custom-call(s32[1]{0:T(128)} %bitcast.3.me, bf16[320,2048]{1,0:T(8,128)(2,1)} %collective-permute-done.16.taken, bf16[512,640]{1,0:T(8,128)(2,1)} %bitcast.100, bf16[512,640]{1,0:T(8,128)(2,1)} %copy-done.7, bf16[256,640]{1,0:T(8,128)(2,1)} %collective-permute-done.11.top, bf16[256,640]{1,0:T(8,128)(2,1)} %copy-done.8, ...), custom_call_target="tpu_custom_call" | custom-call | tf_op jit(solution)/shard_map/serve/pallas_call | solution.py:296
  289.2 3.7 %collective-permute-start.17 = (bf16[320,2048]{1,0:T(8,128)(2,1)}, bf16[320,2048]{1,0:T(8,128)(2,1)S(1)}, u32[]{:S(2)}, u32[]{:S(2)}) collective-permute-start(bf16[320,2048]{1,0:T(8,128)(2,1)} %serve.3), channel_id=1, source_target_pairs={{0,1},{1,0},{2,3},{3,2},{4,5},{5,4},{6,7},{7,6},{8,9},{9,8},{10,11... | collective-permute-start | bytes 3932168 | tf_op jit(solution)/shard_map/ppermute | solution.py:40
  292.9 7.1 %serve.2 = bf16[320,2048]{1,0:T(8,128)(2,1)} custom-call(s32[1]{0:T(128)} %bitcast.3.me, bf16[320,2048]{1,0:T(8,128)(2,1)} %bitcast.108, bf16[512,640]{1,0:T(8,128)(2,1)} %bitcast.101, bf16[512,640]{1,0:T(8,128)(2,1)} %copy-done.7, bf16[256,640]{1,0:T(8,128)(2,1)} %collective-permute-done.11.top, bf16[256,640]{1,0:T(8,128)(2,1)} %copy-done.8, ...), custom_call_target="tpu_custom_call" | custom-call | tf_op jit(solution)/shard_map/serve/pallas_call | solution.py:296
  300.0 2.9 add_convert_fusion
  302.9 3.7 %all-to-all-start.6 = ((bf16[8,40,2048]{2,1,0:T(8,128)(2,1)}), bf16[8,40,2048]{2,1,0:T(8,128)(2,1)S(1)}, u32[]{:S(2)}, u32[]{:S(2)}) async-start(bf16[8,40,2048]{2,1,0:T(8,128)(2,1)} %bitcast.40), calls=%async_computation.6 | async-start | bytes 2621440 | tf_op jit(solution)/shard_map/all_to_all | solution.py:44
  309.3 32.1 %all-to-all-done.6 = bf16[8,40,2048]{2,1,0:T(8,128)(2,1)S(1)} async-done(((bf16[8,40,2048]{2,1,0:T(8,128)(2,1)}), bf16[8,40,2048]{2,1,0:T(8,128)(2,1)S(1)}, u32[]{:S(2)}, u32[]{:S(2)}) %all-to-all-start.6) | async-done | bytes 1310752 | tf_op jit(solution)/shard_map/all_to_all | solution.py:44
  (110 shorter events, 17.7 us)
Async XLA Ops:
  7.2 13.3 %copy-start = (bf16[128,2048]{1,0:T(8,128)(2,1)S(1)}, bf16[128,2048]{1,0:T(8,128)(2,1)}, u32[]{:S(2)}) copy-start(bf16[128,2048]{1,0:T(8,128)(2,1)} %param.11) | copy-start | bytes 1572868
  7.2 13.1 %copy-start.21 = (s32[128,1]{0,1:T(1,128)S(1)}, s32[128,1]{0,1:T(1,128)}, u32[]{:S(2)}) copy-start(s32[128,1]{0,1:T(1,128)} %param.13) | copy-start | bytes 1540
  7.2 113.1 %all-gather.9.cloned.1.call-start = ((), (), s32[]{:S(2)}) async-start(), calls=%async_computation.8 | async-start | bytes 4128768 | tf_op jit(solution)/shard_map/all_gather | solution.py:332
  20.2 218.9 %all-gather.7.cloned.1.call-start = ((), (), s32[]{:S(2)}) async-start(), calls=%async_computation.7 | async-start | bytes 5898240 | tf_op jit(solution)/shard_map/all_gather | solution.py:360
  21.0 45.0 %copy-start.17 = (s32[128,1]{0,1:T(1,128)S(1)}, s32[128,1]{0,1:T(1,128)}, u32[]{:S(2)}) copy-start(s32[128,1]{0,1:T(1,128)} %param.16) | copy-start | bytes 1540
  21.0 49.5 %copy-start.12 = (bf16[128,2048]{1,0:T(8,128)(2,1)S(1)}, bf16[128,2048]{1,0:T(8,128)(2,1)}, u32[]{:S(2)}) copy-start(bf16[128,2048]{1,0:T(8,128)(2,1)} %param.15) | copy-start | bytes 1572868
  58.6 14.6 %copy-start.3 = (bf16[8,40,2048]{2,1,0:T(8,128)(2,1)}, bf16[8,40,2048]{2,1,0:T(8,128)(2,1)S(1)}, u32[]{:S(2)}) copy-start(bf16[8,40,2048]{2,1,0:T(8,128)(2,1)S(1)} %all_to_all.35) | copy-start | bytes 3932164
  58.6 13.1 %copy-start.15 = (f32[128,1]{0,1:T(1,128)S(1)}, f32[128,1]{0,1:T(1,128)}, u32[]{:S(2)}) copy-start(f32[128,1]{0,1:T(1,128)} %param.14) | copy-start | bytes 1540
  58.6 10.0 %collective-permute-start = (bf16[8,40,2048]{2,1,0:T(8,128)(2,1)S(1)}, bf16[8,40,2048]{2,1,0:T(8,128)(2,1)S(1)}, u32[]{:S(2)}, u32[]{:S(2)}) collective-permute-start(bf16[8,40,2048]{2,1,0:T(8,128)(2,1)S(1)} %all_to_all.35), channel_id=1, source_target_pairs={{0,1},{1,0},{2,3},{3,2},{4,5},{5,4},{6,7},{7,6},{8,9},{9,8},{10,11... | collective-permute-start | bytes 3932168 | tf_op jit(solution)/shard_map/ppermute | solution.py:40
  66.1 7.0 %copy-start.19 = (f32[128]{0:T(128)}, f32[128]{0:T(128)S(1)}, u32[]{:S(2)}) copy-start(f32[128]{0:T(128)S(1)} %fusion.3) | copy-start | bytes 1540
  68.6 4.6 %copy-start.9 = (bf16[8,40,2048]{2,1,0:T(8,128)(2,1)}, bf16[8,40,2048]{2,1,0:T(8,128)(2,1)S(1)}, u32[]{:S(2)}) copy-start(bf16[8,40,2048]{2,1,0:T(8,128)(2,1)S(1)} %collective-permute-done) | copy-start | bytes 3932164
  114.8 5.5 %copy-start.4 = (bf16[8,40,2048]{2,1,0:T(8,128)(2,1)}, bf16[8,40,2048]{2,1,0:T(8,128)(2,1)S(1)}, u32[]{:S(2)}) copy-start(bf16[8,40,2048]{2,1,0:T(8,128)(2,1)S(1)} %all_to_all.36) | copy-start | bytes 3932164
  114.8 5.5 %collective-permute-start.1 = (bf16[8,40,2048]{2,1,0:T(8,128)(2,1)S(1)}, bf16[8,40,2048]{2,1,0:T(8,128)(2,1)S(1)}, u32[]{:S(2)}, u32[]{:S(2)}) collective-permute-start(bf16[8,40,2048]{2,1,0:T(8,128)(2,1)S(1)} %all_to_all.36), channel_id=1, source_target_pairs={{0,1},{1,0},{2,3},{3,2},{4,5},{5,4},{6,7},{7,6},{8,9},{9,8},{10,11... | collective-permute-start | bytes 3932168 | tf_op jit(solution)/shard_map/ppermute | solution.py:40
  120.3 1.1 copy-start.10
  137.2 49.8 %all-to-all-start.3 = ((bf16[8,4,64,256]{3,2,1,0:T(8,128)(2,1)}), bf16[8,4,64,256]{3,2,1,0:T(8,128)(2,1)S(1)}, u32[]{:S(2)}, u32[]{:S(2)}) async-start(bf16[8,4,64,256]{3,2,1,0:T(8,128)(2,1)} %get-tuple-element.7), calls=%async_computation.3 | async-start | bytes 2097152 | tf_op jit(solution)/shard_map/all_to_all | solution.py:44
  151.1 11.7 %collective-permute-start.2 = (bf16[256,640]{1,0:T(8,128)(2,1)S(1)}, bf16[256,640]{1,0:T(8,128)(2,1)S(1)}, u32[]{:S(2)}, u32[]{:S(2)}) collective-permute-start(bf16[256,640]{1,0:T(8,128)(2,1)S(1)} %get-tuple-element.10), channel_id=1, source_target_pairs={{0,128},{128,256},{256,384},{384,0},{1,129},{129,257},{257,385},{3... | collective-permute-start | bytes 983048 | tf_op jit(solution)/shard_map/ppermute | solution.py:40
  153.0 10.7 %collective-permute-start.4 = (bf16[256,640]{1,0:T(8,128)(2,1)S(1)}, bf16[256,640]{1,0:T(8,128)(2,1)S(1)}, u32[]{:S(2)}, u32[]{:S(2)}) collective-permute-start(bf16[256,640]{1,0:T(8,128)(2,1)S(1)} %get-tuple-element.12), channel_id=1, source_target_pairs={{0,384},{128,0},{256,128},{384,256},{1,385},{129,1},{257,129},{385... | collective-permute-start | bytes 983048 | tf_op jit(solution)/shard_map/ppermute | solution.py:40
  165.0 18.6 %collective-permute-start.3 = (bf16[512,640]{1,0:T(8,128)(2,1)S(1)}, bf16[512,640]{1,0:T(8,128)(2,1)S(1)}, u32[]{:S(2)}, u32[]{:S(2)}) collective-permute-start(bf16[512,640]{1,0:T(8,128)(2,1)S(1)} %pad_maximum_fusion), channel_id=1, source_target_pairs={{0,128},{128,256},{256,384},{384,0},{1,129},{129,257},{257,385},{3... | collective-permute-start | bytes 1966088 | tf_op jit(solution)/shard_map/ppermute | solution.py:40
  167.0 17.6 %collective-permute-start.5 = (bf16[512,640]{1,0:T(8,128)(2,1)S(1)}, bf16[512,640]{1,0:T(8,128)(2,1)}, u32[]{:S(2)}, u32[]{:S(2)}) collective-permute-start(bf16[512,640]{1,0:T(8,128)(2,1)S(1)} %pad_maximum_fusion.1), channel_id=1, source_target_pairs={{0,384},{128,0},{256,128},{384,256},{1,385},{129,1},{257,129},{385... | collective-permute-start | bytes 1966088 | tf_op jit(solution)/shard_map/ppermute | solution.py:40
  187.0 24.0 %all-to-all-start.2 = ((bf16[8,64,640]{2,1,0:T(8,128)(2,1)}), bf16[8,64,640]{2,1,0:T(8,128)(2,1)S(1)}, u32[]{:S(2)}, u32[]{:S(2)}) async-start(bf16[8,64,640]{2,1,0:T(8,128)(2,1)} %bitcast.29), calls=%async_computation.2 | async-start | bytes 1310720 | tf_op jit(solution)/shard_map/all_to_all | solution.py:44
  193.1 149.6 %all-gather.11.cloned.1.call-start = ((), (), s32[]{:S(2)}) async-start(), calls=%async_computation.9 | async-start | bytes 5849088 | tf_op jit(solution)/shard_map/all_gather | solution.py:354
  193.4 17.9 %copy-start.11 = (f32[1,64,864]{2,1,0:T(8,128)S(1)}, f32[1,64,864]{2,1,0:T(8,128)}, u32[]{:S(2)}) copy-start(f32[1,64,864]{2,1,0:T(8,128)} %param.18) | copy-start | bytes 663556
  193.4 17.9 %copy-start.13 = (f32[1,64,864]{2,1,0:T(8,128)S(1)}, f32[1,64,864]{2,1,0:T(8,128)}, u32[]{:S(2)}) copy-start(f32[1,64,864]{2,1,0:T(8,128)} %param.19) | copy-start | bytes 663556
  193.5 17.9 %copy-start.14 = (f32[1,64,864]{2,1,0:T(8,128)S(1)}, f32[1,64,864]{2,1,0:T(8,128)}, u32[]{:S(2)}) copy-start(f32[1,64,864]{2,1,0:T(8,128)} %param.20) | copy-start | bytes 663556
  193.5 11.2 %collective-permute-start.6 = (bf16[64,256]{1,0:T(8,128)(2,1)S(1)}, bf16[64,256]{1,0:T(8,128)(2,1)S(1)}, u32[]{:S(2)}, u32[]{:S(2)}) collective-permute-start(bf16[64,256]{1,0:T(8,128)(2,1)S(1)} %get-tuple-element.25), channel_id=1, source_target_pairs={{0,128},{128,256},{256,384},{384,0},{1,129},{129,257},{257,385},{3... | collective-permute-start | bytes 98312 | tf_op jit(solution)/shard_map/ppermute | solution.py:40
  197.2 7.4 %collective-permute-start.7 = (bf16[64,256]{1,0:T(8,128)(2,1)S(1)}, bf16[64,256]{1,0:T(8,128)(2,1)S(1)}, u32[]{:S(2)}, u32[]{:S(2)}) collective-permute-start(bf16[64,256]{1,0:T(8,128)(2,1)S(1)} %get-tuple-element.27), channel_id=1, source_target_pairs={{0,256},{128,384},{256,0},{384,128},{1,257},{129,385},{257,1},{385... | collective-permute-start | bytes 98312 | tf_op jit(solution)/shard_map/ppermute | solution.py:40
  202.2 5.0 %collective-permute-start.8 = (bf16[64,256]{1,0:T(8,128)(2,1)S(1)}, bf16[64,256]{1,0:T(8,128)(2,1)S(1)}, u32[]{:S(2)}, u32[]{:S(2)}) collective-permute-start(bf16[64,256]{1,0:T(8,128)(2,1)S(1)} %get-tuple-element.26), channel_id=1, source_target_pairs={{0,384},{128,0},{256,128},{384,256},{1,385},{129,1},{257,129},{385... | collective-permute-start | bytes 98312 | tf_op jit(solution)/shard_map/ppermute | solution.py:40
  213.5 20.7 %all-to-all-start.4 = ((bf16[8,64,640]{2,1,0:T(8,128)(2,1)}), bf16[8,64,640]{2,1,0:T(8,128)(2,1)S(1)}, u32[]{:S(2)}, u32[]{:S(2)}) async-start(bf16[8,64,640]{2,1,0:T(8,128)(2,1)} %broadcast_in_dim.52), calls=%async_computation.4 | async-start | bytes 1310720 | tf_op jit(solution)/shard_map/all_to_all | solution.py:44
  217.1 10.0 %collective-permute-start.13 = (bf16[64,256]{1,0:T(8,128)(2,1)S(1)}, bf16[64,256]{1,0:T(8,128)(2,1)S(1)}, u32[]{:S(2)}, u32[]{:S(2)}) collective-permute-start(bf16[64,256]{1,0:T(8,128)(2,1)S(1)} %get-tuple-element.28), channel_id=1, source_target_pairs={{0,384},{128,0},{256,128},{384,256},{1,385},{129,1},{257,129},{385... | collective-permute-start | bytes 98312 | tf_op jit(solution)/shard_map/ppermute | solution.py:40
  222.5 6.5 %collective-permute-start.14 = (bf16[64,256]{1,0:T(8,128)(2,1)S(1)}, bf16[64,256]{1,0:T(8,128)(2,1)S(1)}, u32[]{:S(2)}, u32[]{:S(2)}) collective-permute-start(bf16[64,256]{1,0:T(8,128)(2,1)S(1)} %get-tuple-element.28), channel_id=1, source_target_pairs={{0,256},{128,384},{256,0},{384,128},{1,257},{129,385},{257,1},{385... | collective-permute-start | bytes 98312 | tf_op jit(solution)/shard_map/ppermute | solution.py:40
  224.4 6.2 %collective-permute-start.15 = (bf16[64,256]{1,0:T(8,128)(2,1)S(1)}, bf16[64,256]{1,0:T(8,128)(2,1)S(1)}, u32[]{:S(2)}, u32[]{:S(2)}) collective-permute-start(bf16[64,256]{1,0:T(8,128)(2,1)S(1)} %get-tuple-element.28), channel_id=1, source_target_pairs={{0,128},{128,256},{256,384},{384,0},{1,129},{129,257},{257,385},{3... | collective-permute-start | bytes 98312 | tf_op jit(solution)/shard_map/ppermute | solution.py:40
  234.3 15.9 %copy-start.2 = (bf16[8,64,640]{2,1,0:T(8,128)(2,1)}, bf16[8,64,640]{2,1,0:T(8,128)(2,1)S(1)}, u32[]{:S(2)}) copy-start(bf16[8,64,640]{2,1,0:T(8,128)(2,1)S(1)} %all-to-all-done.4) | copy-start | bytes 1966084
  235.6 39.6 %all-to-all-start.5 = ((bf16[8,4,64,256]{3,2,1,0:T(8,128)(2,1)}), bf16[8,4,64,256]{3,2,1,0:T(8,128)(2,1)S(1)}, u32[]{:S(2)}, u32[]{:S(2)}) async-start(bf16[8,4,64,256]{3,2,1,0:T(8,128)(2,1)} %broadcast_in_dim.58), calls=%async_computation.5 | async-start | bytes 2097152 | tf_op jit(solution)/shard_map/all_to_all | solution.py:44
  240.6 48.6 %copy-start.5 = (bf16[8,1,40,2048]{3,2,0,1:T(8,128)(2,1)}, bf16[8,1,40,2048]{3,2,0,1:T(8,128)(2,1)S(1)}, u32[]{:S(2)}) copy-start(bf16[8,1,40,2048]{3,2,0,1:T(8,128)(2,1)S(1)} %constant_dynamic-slice_fusion) | copy-start | bytes 3932164
  240.6 40.7 %collective-permute-start.16 = (bf16[320,2048]{1,0:T(8,128)(2,1)S(1)}, bf16[320,2048]{1,0:T(8,128)(2,1)}, u32[]{:S(2)}, u32[]{:S(2)}) collective-permute-start(bf16[320,2048]{1,0:T(8,128)(2,1)S(1)} %bitcast.107), channel_id=1, source_target_pairs={{0,1},{1,0},{2,3},{3,2},{4,5},{5,4},{6,7},{7,6},{8,9},{9,8},{10,11... | collective-permute-start | bytes 3932168 | tf_op jit(solution)/shard_map/ppermute | solution.py:40
  247.2 19.8 %collective-permute-start.10 = (bf16[512,640]{1,0:T(8,128)(2,1)S(1)}, bf16[512,640]{1,0:T(8,128)(2,1)S(1)}, u32[]{:S(2)}, u32[]{:S(2)}) collective-permute-start(bf16[512,640]{1,0:T(8,128)(2,1)S(1)} %bitcast.98), channel_id=1, source_target_pairs={{0,128},{128,256},{256,384},{384,0},{1,129},{129,257},{257,385},{3... | collective-permute-start | bytes 1966088 | tf_op jit(solution)/shard_map/ppermute | solution.py:40
  250.2 19.5 %collective-permute-start.9 = (bf16[512,640]{1,0:T(8,128)(2,1)S(1)}, bf16[512,640]{1,0:T(8,128)(2,1)S(1)}, u32[]{:S(2)}, u32[]{:S(2)}) collective-permute-start(bf16[512,640]{1,0:T(8,128)(2,1)S(1)} %bitcast.99), channel_id=1, source_target_pairs={{0,384},{128,0},{256,128},{384,256},{1,385},{129,1},{257,129},{385... | collective-permute-start | bytes 1966088 | tf_op jit(solution)/shard_map/ppermute | solution.py:40
  267.0 2.8 copy-start.6
  267.8 12.0 %collective-permute-start.11 = (bf16[256,640]{1,0:T(8,128)(2,1)}, bf16[256,640]{1,0:T(8,128)(2,1)}, u32[]{:S(2)}, u32[]{:S(2)}) collective-permute-start(bf16[256,640]{1,0:T(8,128)(2,1)} %slice.175), channel_id=1, source_target_pairs={{0,128},{128,256},{256,384},{384,0},{1,129},{129,257},{257,385},{3... | collective-permute-start | bytes 983048 | tf_op jit(solution)/shard_map/ppermute | solution.py:40
  269.7 0.9 copy-start.7
  270.6 10.7 %collective-permute-start.12 = (bf16[256,640]{1,0:T(8,128)(2,1)S(1)}, bf16[256,640]{1,0:T(8,128)(2,1)S(1)}, u32[]{:S(2)}, u32[]{:S(2)}) collective-permute-start(bf16[256,640]{1,0:T(8,128)(2,1)S(1)} %slice.176), channel_id=1, source_target_pairs={{0,384},{128,0},{256,128},{384,256},{1,385},{129,1},{257,129},{385... | collective-permute-start | bytes 983048 | tf_op jit(solution)/shard_map/ppermute | solution.py:40
  275.2 6.1 %copy-start.1 = (bf16[8,4,64,256]{3,2,1,0:T(8,128)(2,1)}, bf16[8,4,64,256]{3,2,1,0:T(8,128)(2,1)S(1)}, u32[]{:S(2)}) copy-start(bf16[8,4,64,256]{3,2,1,0:T(8,128)(2,1)S(1)} %all-to-all-done.5.second) | copy-start | bytes 3145732
  289.2 10.8 %collective-permute-start.17 = (bf16[320,2048]{1,0:T(8,128)(2,1)}, bf16[320,2048]{1,0:T(8,128)(2,1)S(1)}, u32[]{:S(2)}, u32[]{:S(2)}) collective-permute-start(bf16[320,2048]{1,0:T(8,128)(2,1)} %serve.3), channel_id=1, source_target_pairs={{0,1},{1,0},{2,3},{3,2},{4,5},{5,4},{6,7},{7,6},{8,9},{9,8},{10,11... | collective-permute-start | bytes 3932168 | tf_op jit(solution)/shard_map/ppermute | solution.py:40
  302.9 3.7 %copy-start.22 = (s32[16]{0:T(128)S(1)}, s32[16]{0:T(128)}, u32[]{:S(2)}) copy-start(s32[16]{0:T(128)} %param.21) | copy-start | bytes 196
  302.9 6.4 %copy-start.18 = (s32[128,1]{0,1:T(1,128)S(1)}, s32[128,1]{0,1:T(1,128)}, u32[]{:S(2)}) copy-start(s32[128,1]{0,1:T(1,128)} %param.16) | copy-start | bytes 1540
  302.9 6.4 %copy-start.20 = (f32[128]{0:T(128)S(1)}, f32[128]{0:T(128)}, u32[]{:S(2)}) copy-start(f32[128]{0:T(128)} %copy-done.19) | copy-start | bytes 1540
  302.9 38.5 %copy-start.16 = (f32[128,1]{0,1:T(1,128)S(1)}, f32[128,1]{0,1:T(1,128)}, u32[]{:S(2)}) copy-start(f32[128,1]{0,1:T(1,128)} %param.17) | copy-start | bytes 1540
  302.9 38.5 %all-to-all-start.6 = ((bf16[8,40,2048]{2,1,0:T(8,128)(2,1)}), bf16[8,40,2048]{2,1,0:T(8,128)(2,1)S(1)}, u32[]{:S(2)}, u32[]{:S(2)}) async-start(bf16[8,40,2048]{2,1,0:T(8,128)(2,1)} %bitcast.40), calls=%async_computation.6 | async-start | bytes 2621440 | tf_op jit(solution)/shard_map/all_to_all | solution.py:44
  (1 other events, 0.7 us)
Sparse Core Ops, SparseCore 0:
  20.3 60.5 all-gather.8
  83.1 74.4 all-gather.6
  212.5 42.8 all-gather.10

commit v3 on v2

v3 whole, which is shorter than its diff:
```python
import jax
import jax.numpy as jnp
from jax import lax
from jax.experimental import pallas as pl
from jax.experimental.pallas import tpu as pltpu
from jax.sharding import Mesh
from jax.sharding import PartitionSpec as P

D = 2048
HID = 1152
EXPERTS = 4
CAP = 40
SLOTS = EXPERTS * CAP
DP = ("x", "z")
EXPERT = ("y", "core")
ALL = DP + EXPERT
WIDTH = 288
MAIN = 256
TAIL = WIDTH - MAIN
LEAD = 2 * MAIN
SIDE = 128 + MAIN
COLS = LEAD + SIDE
IN_SCALE = 2048 ** (-0.5)
OUT_SCALE = HID ** (-0.5)
TEST = False


beta_one = 0.9
beta_two = 0.95
learn_rate = 0.2
decay_rate = 0.1
adam_step = 10.0
adam_eps = 1e-08


def pass_on(value, axis, by):
    size = lax.axis_size(axis)
    return lax.ppermute(value, axis, [(k, (k + by) % size) for k in range(size)])


def exchange(value, axis):
    return lax.all_to_all(value, axis, split_axis=0, concat_axis=0, tiled=True)


def f32(value):
    return value.astype(jnp.float32)


def b16(value):
    return value.astype(jnp.bfloat16)


def slot_of(routes):
    ids = routes.reshape(-1)
    one_hot = ids[:, None] == jnp.arange(EXPERTS, dtype=jnp.int32)[None, :]
    count = ids.shape[0]
    before = lax.broadcasted_iota(jnp.int32, (count, count), 1) < lax.broadcasted_iota(
        jnp.int32, (count, count), 0
    )
    earlier = jnp.dot(
        before.astype(jnp.bfloat16),
        one_hot.astype(jnp.bfloat16),
        preferred_element_type=jnp.float32,
    )
    slots = jnp.sum(jnp.where(one_hot, earlier, 0.0), axis=1).astype(jnp.int32)
    return ids * CAP + slots


def to_slots(targets, payload):
    rows = lax.broadcasted_iota(jnp.int32, (SLOTS, targets.shape[0]), 0)
    selector = (rows == targets[None, :]).astype(jnp.bfloat16)
    filled = jnp.dot(selector, payload, preferred_element_type=jnp.float32)
    return filled.astype(jnp.bfloat16).reshape(EXPERTS, CAP, payload.shape[1])


def to_chips(slots):
    chips = lax.axis_size("y")
    return exchange(jnp.repeat(slots, chips // EXPERTS, axis=0), "y").reshape(-1, D)


def arranged(value):
    gate, up, down = (value[:, k * WIDTH : (k + 1) * WIDTH] for k in range(3))
    spare = jnp.zeros((value.shape[0], 128 - 3 * TAIL), value.dtype)
    tails = [gate[:, MAIN:], up[:, MAIN:], down[:, MAIN:], spare]
    return jnp.concatenate([gate[:, :MAIN], up[:, :MAIN]] + tails + [down[:, :MAIN]], axis=1)


def in_place(value):
    parts = []
    for k, start in enumerate((0, MAIN, LEAD + 128)):
        at = LEAD + k * TAIL
        parts += [value[:, start : start + MAIN], value[:, at : at + TAIL]]
    return jnp.concatenate(parts, axis=1)


def found_along_x(value):
    half = value.shape[0] // 2
    left = pass_on(value, "x", 1)
    right = pass_on(value, "x", -1)
    top = pass_on(left[:half], "x", 1)
    bottom = pass_on(right[half:], "x", -1)
    return value, right, top, bottom, left


def found_along_z(value):
    size = lax.axis_size("z")
    me = lax.axis_index("z")
    out = jnp.zeros((size,) + value.shape, value.dtype)
    out = lax.dynamic_update_index_in_dim(out, value, me, 0)
    for by in range(1, size):
        got = pass_on(value, "z", -by)
        out = lax.dynamic_update_index_in_dim(out, got, lax.rem(me + by, size), 0)
    return out.reshape(-1, value.shape[1])


def own_rows(right, left, near, own):
    half = own.shape[0] // 2
    from_left = pass_on(right, "x", 1)
    from_right = pass_on(left, "x", -1)
    top = pass_on(b16(f32(near[0]) + f32(from_left[:half])), "x", 1)
    bottom = pass_on(b16(f32(near[1]) + f32(from_right[:half])), "x", -1)
    first = f32(own[:half]) + f32(from_right[half:]) + f32(top)
    second = f32(own[half:]) + f32(from_left[half:]) + f32(bottom)
    summed = b16(jnp.concatenate([first, second], axis=0))
    parts = exchange(summed.reshape(lax.axis_size("z"), -1, COLS), "z")
    return in_place(jnp.sum(f32(parts), axis=0))


def all_rows(value):
    size = lax.axis_size("z")
    wide = exchange(jnp.broadcast_to(value[None], (size,) + value.shape), "z")
    return found_along_x(wide.reshape(-1, COLS))


def dot(a, b, dims=((1,), (0,))):
    return lax.dot_general(a, b, (dims, ((), ())), preferred_element_type=jnp.float32)


def lanes(shape):
    return lax.broadcasted_iota(jnp.int32, shape, 1)


def start_of(me, offset, wide):
    return pl.multiple_of(lax.rem(me + offset, 4) * wide, wide)


def in_row_order(me, pieces, wn, columns):
    own, right, top, bottom, left = pieces
    wide = own.shape[0]
    half = wide // 2
    wn[pl.ds(start_of(me, 0, wide), wide), :] = own[:, columns]
    wn[pl.ds(start_of(me, 1, wide), wide), :] = right[:, columns]
    far = start_of(me, 2, wide)
    wn[pl.ds(far, half), :] = top[:, columns]
    wn[pl.ds(pl.multiple_of(far + half, half), half), :] = bottom[:, columns]
    wn[pl.ds(start_of(me, 3, wide), wide), :] = left[:, columns]


def pre_body(me, own_in, other_in, own, right, top, bottom, left, act, silu, slope, wn, pre):
    in_row_order(me[0], (own, right, top, bottom, left), wn, slice(0, LEAD + 128))
    count = own_in.shape[0]
    for half, taken in enumerate((own_in, other_in)):
        pre[half * count : (half + 1) * count, :] = dot(taken[...], wn[...]) * IN_SCALE

    def chunk(i, carry):
        at = pl.ds(pl.multiple_of(i * 64, 64), 64)
        tail = pre[at, LEAD:]
        pairs = (
            (tail, pltpu.roll(tail, 128 - TAIL, 1), slice(0, 128)),
            (pre[at, :MAIN], pre[at, MAIN:LEAD], slice(128, SIDE)),
        )
        for gate, up, cols in pairs:
            sigmoid_gate = jax.nn.sigmoid(gate)
            silu_gate = gate * sigmoid_gate
            product = silu_gate * up
            if cols.start == 0:
                lane = lanes(tail.shape)
                here = (lane >= 2 * TAIL) & (lane < 3 * TAIL)
                product = jnp.where(here, pltpu.roll(product, 2 * TAIL, 1), 0.0)
            act[at, cols] = b16(product)
            silu[at, cols] = silu_gate
            slope[at, cols] = up * sigmoid_gate * (1.0 + gate * (1.0 - sigmoid_gate))
        return carry

    lax.fori_loop(0, 2 * count // 64, chunk, 0)


def step_pre(own_in, other_in, pieces):
    me = lax.axis_index("x").astype(jnp.int32).reshape(1)
    count = 2 * own_in.shape[0]
    return pl.pallas_call(
        pre_body,
        out_shape=(
            jax.ShapeDtypeStruct((count, SIDE), jnp.bfloat16),
            jax.ShapeDtypeStruct((count, SIDE), jnp.float32),
            jax.ShapeDtypeStruct((count, SIDE), jnp.float32),
        ),
        in_specs=[pl.BlockSpec(memory_space=pltpu.SMEM)]
        + [pl.BlockSpec(memory_space=pltpu.VMEM)] * 7,
        scratch_shapes=[
            pltpu.VMEM((D, LEAD + 128), jnp.bfloat16),
            pltpu.VMEM((count, LEAD + 128), jnp.float32),
        ],
        interpret=TEST,
        name="step_pre",
    )(me, own_in, other_in, *pieces)


def terms_body(
    me, own_in, other_in, own_sc, other_sc, act, silu, slope, own, right, top, bottom, left,
    to_right, to_left, near, mine, wn, dn, g_in,
):
    in_row_order(me[0], (own, right, top, bottom, left), wn, slice(LEAD, COLS))
    count = own_in.shape[0]
    for half, scaled in enumerate((own_sc, other_sc)):
        dn[half * count : (half + 1) * count, :] = dot(scaled[...], wn[...]) * OUT_SCALE

    def chunk(i, carry):
        at = pl.ds(pl.multiple_of(i * 64, 64), 64)
        down_back = dn[at, 128:]
        g_in[at, :MAIN] = b16(down_back * slope[at, 128:])
        g_in[at, MAIN:LEAD] = b16(down_back * silu[at, 128:])
        down_tail = pltpu.roll(dn[at, :128], 128 - 2 * TAIL, 1)
        gate_t, up_t = down_tail * slope[at, :128], down_tail * silu[at, :128]
        lane = lanes(gate_t.shape)
        up_t = jnp.where(lane < 2 * TAIL, pltpu.roll(up_t, TAIL, 1), 0.0)
        g_in[at, LEAD:] = b16(jnp.where(lane < TAIL, gate_t, up_t))
        return carry

    lax.fori_loop(0, 2 * count // 64, chunk, 0)
    over_rows = ((0,), (0,))
    wide = own.shape[0]
    half = wide // 2
    for k in range(4):
        cols = pl.ds(start_of(me[0], k, wide), wide)
        a = dot(own_in[:, cols], g_in[:count, :], over_rows)
        a = (a + dot(other_in[:, cols], g_in[count:, :], over_rows)) * IN_SCALE
        b = dot(own_sc[:, cols], act[:count, :], over_rows)
        b = (b + dot(other_sc[:, cols], act[count:, :], over_rows)) * OUT_SCALE
        parts = (
            (slice(0, LEAD), b16(a[:, :LEAD])),
            (slice(LEAD, LEAD + 128), b16(a[:, LEAD:] + b[:, :128])),
            (slice(LEAD + 128, COLS), b16(b[:, 128:])),
        )
        for at, value in parts:
            if k == 0:
                mine[:, at] = value
            elif k == 1:
                near[0, :, at] = value[:half]
                to_right[half:, at] = value[half:]
            elif k == 2:
                to_right[:half, at] = value[:half]
                to_left[:half, at] = value[half:]
            else:
                to_left[half:, at] = value[:half]
                near[1, :, at] = value[half:]


def step_terms(rows, made, pieces):
    me = lax.axis_index("x").astype(jnp.int32).reshape(1)
    count = 2 * rows[0].shape[0]
    wide = pieces[0].shape[0]
    chunk = jax.ShapeDtypeStruct((wide, COLS), jnp.bfloat16)
    return pl.pallas_call(
        terms_body,
        out_shape=(
            chunk,
            chunk,
            jax.ShapeDtypeStruct((2, wide // 2, COLS), jnp.bfloat16),
            chunk,
        ),
        in_specs=[pl.BlockSpec(memory_space=pltpu.SMEM)]
        + [pl.BlockSpec(memory_space=pltpu.VMEM)] * 12,
        scratch_shapes=[
            pltpu.VMEM((D, SIDE), jnp.bfloat16),
            pltpu.VMEM((count, SIDE), jnp.float32),
            pltpu.VMEM((count, LEAD + 128), jnp.bfloat16),
        ],
        interpret=TEST,
        name="step_terms",
    )(me, *rows, *made, *pieces)


def serve_body(me, taken, own, right, top, bottom, left, out, wn, pre, act):
    in_row_order(me[0], (own, right, top, bottom, left), wn, slice(0, COLS))
    pre[...] = dot(taken[...], wn[:, : LEAD + 128]) * IN_SCALE

    def chunk(i, carry):
        at = pl.ds(pl.multiple_of(i * 64, 64), 64)
        gate, up = pre[at, :MAIN], pre[at, MAIN:LEAD]
        tail = pre[at, LEAD:]
        lane = lanes(tail.shape)
        act_t = tail * jax.nn.sigmoid(tail) * pltpu.roll(tail, 128 - TAIL, 1)
        here = (lane >= 2 * TAIL) & (lane < 3 * TAIL)
        act[at, :128] = b16(jnp.where(here, pltpu.roll(act_t, 2 * TAIL, 1), 0.0))
        act[at, 128:] = b16(gate * jax.nn.sigmoid(gate) * up)
        return carry

    lax.fori_loop(0, taken.shape[0] // 64, chunk, 0)
    wide = own.shape[0]
    for k in range(4):
        cols = slice(k * wide, (k + 1) * wide)
        total = dot(act[...], wn[cols, LEAD:], ((1,), (1,)))
        out[:, cols] = b16(total * OUT_SCALE)


def serve(taken, pieces):
    me = lax.axis_index("x").astype(jnp.int32).reshape(1)
    return pl.pallas_call(
        serve_body,
        out_shape=jax.ShapeDtypeStruct(taken.shape, jnp.bfloat16),
        in_specs=[pl.BlockSpec(memory_space=pltpu.SMEM)]
        + [pl.BlockSpec(memory_space=pltpu.VMEM)] * 6,
        scratch_shapes=[
            pltpu.VMEM((D, COLS), jnp.bfloat16),
            pltpu.VMEM((taken.shape[0], LEAD + 128), jnp.float32),
            pltpu.VMEM((taken.shape[0], SIDE), jnp.bfloat16),
        ],
        interpret=TEST,
        name="serve",
    )(me, taken, *pieces)


def migrated(stacked, owner_plan):
    groups = lax.axis_size(EXPERT)
    positions = jnp.arange(groups, dtype=jnp.int32)
    goes = owner_plan[None, :] == positions[:, None]
    holder = jnp.sum(jnp.where(goes, positions[None, :], 0), axis=1)
    pieces = stacked.reshape(groups, -1, stacked.shape[1])
    spread = exchange(pieces, EXPERT)
    ordered = jnp.take(spread, holder, axis=0)
    return exchange(ordered, EXPERT).reshape(stacked.shape)


def whole_step(
    step_inputs,
    step_cotangent,
    step_routes,
    step_gates,
    next_inputs,
    next_routes,
    next_gates,
    master_weights,
    first_moment,
    second_moment,
    owner_plan,
):
    old_weights = master_weights[0]
    step_targets = slot_of(step_routes)
    scaled = b16(f32(step_cotangent) * step_gates)
    old_wide = found_along_z(arranged(b16(old_weights)))
    old_pieces = found_along_x(old_wide)
    own_in = to_chips(to_slots(step_targets, step_inputs))
    own_sc = to_chips(to_slots(step_targets, scaled))
    other_in = pass_on(own_in, "core", 1)
    other_sc = pass_on(own_sc, "core", 1)
    made = step_pre(own_in, other_in, old_pieces)
    gradient = own_rows(*step_terms((own_in, other_in, own_sc, other_sc), made, old_pieces))
    first_new = beta_one * first_moment[0] + (1.0 - beta_one) * gradient
    second_new = beta_two * second_moment[0] + (1.0 - beta_two) * gradient * gradient
    first_hat = first_new / (1.0 - beta_one**adam_step)
    second_hat = second_new / (1.0 - beta_two**adam_step)
    new_weights = old_weights - learn_rate * (
        first_hat / (jnp.sqrt(second_hat) + adam_eps) + decay_rate * old_weights
    )
    pieces = all_rows(arranged(b16(new_weights)))
    stacked = jnp.concatenate([b16(new_weights), b16(first_new), b16(second_new)], axis=0)
    moved = f32(migrated(stacked, owner_plan)).reshape((3, 1) + old_weights.shape)

    next_targets = slot_of(next_routes)
    own_next = to_chips(to_slots(next_targets, next_inputs))
    other_next = pass_on(own_next, "core", 1)
    met = serve(other_next, pieces)
    met = pass_on(met, "core", 1)
    partials = b16(f32(serve(own_next, pieces)) + f32(met))
    returned = exchange(partials.reshape(-1, CAP, D), "y").reshape(-1, D)
    chips_each = lax.axis_size("y") // EXPERTS
    slot = lax.broadcasted_iota(jnp.int32, (next_targets.shape[0], returned.shape[0]), 1)
    expert_slot = (slot // (chips_each * CAP)) * CAP + lax.rem(slot, CAP)
    picks = (next_targets[:, None] == expert_slot).astype(jnp.bfloat16)
    pair_sums = jnp.dot(picks, returned, preferred_element_type=jnp.float32)
    layer_output = b16(pair_sums * next_gates)
    return (layer_output, moved[0], moved[1], moved[2])


def solution(mesh):
    chips = mesh.devices.reshape(4, -1, mesh.shape["expert"] // 2, 2)
    tokens = P(ALL, None)
    slabs = P(EXPERT, DP, None)
    return jax.shard_map(
        whole_step,
        mesh=Mesh(chips, ALL),
        in_specs=(tokens,) * 7 + (slabs,) * 3 + (P(),),
        out_specs=(tokens,) + (slabs,) * 3,
        check_vma=False,
    )
```

time: 353 us -> 411 us (1.16)
  waiting for transfers between devices: 88.4 us -> 201 us
  blocking collectives: 90.8 us -> 25.2 us
  starting transfers between devices: 98 us -> 120 us
  between operations: 17.7 us -> 1.35 us
  Pallas kernels: 30.1 us -> 36.4 us
    all_to_all x5 -> x7, waiting for transfers between devices: 39.6 us -> 131 us  [exchange(): return lax.all_to_all(value, axis, split_axis=0, concat_axis=0, tiled=True)]
    all_to_all x2 -> x1, blocking collectives: 79.1 us -> 25.2 us  [exchange(): return lax.all_to_all(value, axis, split_axis=0, concat_axis=0, tiled=True)]
    ppermute x18 -> x23, waiting for transfers between devices: 48.7 us -> 69.5 us  [pass_on(): lax.ppermute(value, axis, [(k, (k + by) % size) for k in range(size)])]
    ppermute x18 -> x23, starting transfers between devices: 68.3 us -> 87.1 us  [pass_on(): lax.ppermute(value, axis, [(k, (k + by) % size) for k in range(size)])]
    all_gather x1 -> x0, blocking collectives: 11.7 us -> none  [whole_step(): lax.all_gather(jnp.concatenate(arranged(b16(old_weights)), axis=1), 'x',...]
    pallas_call x1 -> x2, Pallas kernels: 15.8 us -> 21.9 us  [the longest x1 13.9 us: step_terms(): pl.pallas_call(terms_body, out_shape=(chunk, chunk, jax.ShapeDtypeStruct(...]
    all_to_all x5 -> x7, starting transfers between devices: 29.4 us -> 32.6 us  [exchange(): return lax.all_to_all(value, axis, split_axis=0, concat_axis=0, tiled=True)]
  transfers between devices with their start and end apart: 26 -> 30, of which waited for: 15 -> 18; matrix products, arithmetic and copies ran while one was open for 6% -> 3% of each run, Pallas kernels for 9% -> 4%
where the time goes in v3:
time: 411 us; the launch traced here: 409 us
  waiting for transfers between devices  201 us (49%)
  starting transfers between devices  120 us (29%)
  Pallas kernels  36.4 us (9%)
  blocking collectives  25.2 us (6%)
  local copies, waits for them, and re-layouts  15.1 us (4%)
  other arithmetic  7.55 us (2%)
    all_to_all x7, waiting for transfers between devices, exchange(): return lax.all_to_all(value, axis, split_axis=0, concat_axis=0, tiled=True)  131 us
    ppermute x23, starting transfers between devices, pass_on(): lax.ppermute(value, axis, [(k, (k + by) % size) for k in range(size)])  87.1 us
    ppermute x23, waiting for transfers between devices, pass_on(): lax.ppermute(value, axis, [(k, (k + by) % size) for k in range(size)])  69.5 us
    all_to_all x7, starting transfers between devices, exchange(): return lax.all_to_all(value, axis, split_axis=0, concat_axis=0, tiled=True)  32.6 us
    all_to_all x1, blocking collectives, exchange(): return lax.all_to_all(value, axis, split_axis=0, concat_axis=0, tiled=True)  25.2 us
    pallas_call x2, Pallas kernels, serve(): pl.pallas_call(serve_body, out_shape=jax.ShapeDtypeStruct(taken.shape, jn...  14.5 us
    pallas_call x1, Pallas kernels, step_terms(): pl.pallas_call(terms_body, out_shape=(chunk, chunk, jax.ShapeDtypeStruct(...  13.9 us
  transfers between devices with their start and end apart: 30, of which 18 were waited for; matrix products, arithmetic and copies ran while one was open for 3% of the time, Pallas kernels for 4%

profile of v3, /device:TPU:1, one launch (start us, length us, event | category | flops | bytes accessed | tf_op | source)
XLA Modules:
  0.0 409.2 jit_solution(11164700339303991822)
XLA Ops:
  3.8 7.8 %all-to-all-start.1 = ((bf16[8,40,2048]{2,1,0:T(8,128)(2,1)}), bf16[8,40,2048]{2,1,0:T(8,128)(2,1)S(1)}, u32[]{:S(2)}, u32[]{:S(2)}) async-start(bf16[8,40,2048]{2,1,0:T(8,128)(2,1)} %bitcast.11), calls=%async_computation.1 | async-start | bytes 2621440 | tf_op jit(solution)/shard_map/all_to_all | solution.py:42
  12.0 34.3 %all-to-all-done.1 = bf16[8,40,2048]{2,1,0:T(8,128)(2,1)S(1)} async-done(((bf16[8,40,2048]{2,1,0:T(8,128)(2,1)}), bf16[8,40,2048]{2,1,0:T(8,128)(2,1)S(1)}, u32[]{:S(2)}, u32[]{:S(2)}) %all-to-all-start.1) | async-done | bytes 1310752 | tf_op jit(solution)/shard_map/all_to_all | solution.py:42
  47.7 4.3 %all-to-all-start.2 = ((bf16[8,40,2048]{2,1,0:T(8,128)(2,1)}), bf16[8,40,2048]{2,1,0:T(8,128)(2,1)}, u32[]{:S(2)}, u32[]{:S(2)}) async-start(bf16[8,40,2048]{2,1,0:T(8,128)(2,1)} %bitcast.15), calls=%async_computation.2 | async-start | bytes 2621440 | tf_op jit(solution)/shard_map/all_to_all | solution.py:42
  52.3 10.8 %collective-permute-start.2 = (bf16[64,896]{1,0:T(8,128)(2,1)S(1)}, bf16[64,896]{1,0:T(8,128)(2,1)S(1)}, u32[]{:S(2)}, u32[]{:S(2)}) collective-permute-start(bf16[64,896]{1,0:T(8,128)(2,1)S(1)} %concatenate.16), channel_id=1, source_target_pairs={{0,112},{16,0},{32,16},{48,32},{64,48},{80,64},{96,80},{112,96},{1... | collective-permute-start | bytes 344072 | tf_op jit(solution)/shard_map/ppermute | solution.py:38
  63.1 2.2 collective-permute-start.3
  65.2 1.9 collective-permute-start.4
  67.2 7.3 %collective-permute-start.5 = (bf16[64,896]{1,0:T(8,128)(2,1)S(1)}, bf16[64,896]{1,0:T(8,128)(2,1)S(1)}, u32[]{:S(2)}, u32[]{:S(2)}) collective-permute-start(bf16[64,896]{1,0:T(8,128)(2,1)S(1)} %concatenate.16), channel_id=1, source_target_pairs={{0,64},{16,80},{32,96},{48,112},{64,0},{80,16},{96,32},{112,48},{1... | collective-permute-start | bytes 344072 | tf_op jit(solution)/shard_map/ppermute | solution.py:38
  74.5 1.9 collective-permute-start.6
  76.6 3.1 collective-permute-start.7
  79.7 3.3 collective-permute-start.8
  85.0 7.5 %collective-permute-done.7 = bf16[64,896]{1,0:T(8,128)(2,1)S(1)} collective-permute-done((bf16[64,896]{1,0:T(8,128)(2,1)S(1)}, bf16[64,896]{1,0:T(8,128)(2,1)S(1)}, u32[]{:S(2)}, u32[]{:S(2)}) %collective-permute-start.7) | collective-permute-done | bytes 114720 | tf_op jit(solution)/shard_map/ppermute | solution.py:38
  92.4 3.2 collective-permute-done.8
  95.7 3.1 collective-permute-start.10
  98.8 3.4 collective-permute-start.9
  102.2 3.1 collective-permute-start
  105.3 1.9 collective-permute-start.1
  107.2 13.0 %collective-permute-done.10.left = bf16[512,896]{1,0:T(8,128)(2,1)} collective-permute-done((bf16[512,896]{1,0:T(8,128)(2,1)S(1)}, bf16[512,896]{1,0:T(8,128)(2,1)}, u32[]{:S(2)}, u32[]{:S(2)}) %collective-permute-start.10) | collective-permute-done | bytes 917536 | tf_op jit(solution)/shard_map/ppermute | solution.py:38
  125.8 4.6 %collective-permute-start.12 = (bf16[256,896]{1,0:T(8,128)(2,1)}, bf16[256,896]{1,0:T(8,128)(2,1)}, u32[]{:S(2)}, u32[]{:S(2)}) collective-permute-start(bf16[256,896]{1,0:T(8,128)(2,1)} %slice.162), channel_id=1, source_target_pairs={{0,384},{128,0},{256,128},{384,256},{1,385},{129,1},{257,129},{385... | collective-permute-start | bytes 1376264 | tf_op jit(solution)/shard_map/ppermute | solution.py:38
  130.4 5.6 %collective-permute-done.11.top = bf16[256,896]{1,0:T(8,128)(2,1)S(1)} collective-permute-done((bf16[256,896]{1,0:T(8,128)(2,1)}, bf16[256,896]{1,0:T(8,128)(2,1)S(1)}, u32[]{:S(2)}, u32[]{:S(2)}) %collective-permute-start.11) | collective-permute-done | bytes 458784 | tf_op jit(solution)/shard_map/ppermute | solution.py:38
  136.0 2.9 collective-permute-done.12.bottom
  138.8 8.0 %step_pre.1 = (bf16[640,384]{1,0:T(8,128)(2,1)}, f32[640,384]{1,0:T(8,128)}, f32[640,384]{1,0:T(8,128)}) custom-call(s32[1]{0:T(128)} %bitcast.3.me, bf16[320,2048]{1,0:T(8,128)(2,1)} %bitcast.87, bf16[320,2048]{1,0:T(8,128)(2,1)} %collective-permute-done.other_in, bf16[512,896]{1,0:T(8,128)(2,1)} %bitcast.91, ...), custom_call_target="tpu_custom_call" | custom-call | tf_op jit(solution)/shard_map/step_pre/pallas_call | solution.py:191
  146.8 13.9 %step_terms.1 = (bf16[512,896]{1,0:T(8,128)(2,1)}, bf16[512,896]{1,0:T(8,128)(2,1)}, bf16[2,256,896]{2,1,0:T(8,128)(2,1)}, bf16[512,896]{1,0:T(8,128)(2,1)}) custom-call(s32[1]{0:T(128)} %bitcast.3.me, bf16[320,2048]{1,0:T(8,128)(2,1)} %bitcast.88, bf16[320,2048]{1,0:T(8,128)(2,1)} %collective-permute-done.other_in, bf16[320,2048]{1,0:T(8,128)(2,1)} %bitcast.16.own_sc, ...), custom_call_target="tpu_custom_call" | custom-call | tf_op jit(solution)/shard_map/step_terms/pallas_call | solution.py:264
  160.7 5.3 %collective-permute-start.13 = (bf16[512,896]{1,0:T(8,128)(2,1)}, bf16[512,896]{1,0:T(8,128)(2,1)S(1)}, u32[]{:S(2)}, u32[]{:S(2)}) collective-permute-start(bf16[512,896]{1,0:T(8,128)(2,1)} %get-tuple-element.15), channel_id=1, source_target_pairs={{0,384},{128,0},{256,128},{384,256},{1,385},{129,1},{257,129},{385... | collective-permute-start | bytes 2752520 | tf_op jit(solution)/shard_map/ppermute | solution.py:38
  168.0 15.5 %collective-permute-done.13 = bf16[512,896]{1,0:T(8,128)(2,1)S(1)} collective-permute-done((bf16[512,896]{1,0:T(8,128)(2,1)}, bf16[512,896]{1,0:T(8,128)(2,1)S(1)}, u32[]{:S(2)}, u32[]{:S(2)}) %collective-permute-start.13) | collective-permute-done | bytes 917536 | tf_op jit(solution)/shard_map/ppermute | solution.py:38
  183.4 4.9 %collective-permute-done.14 = bf16[512,896]{1,0:T(8,128)(2,1)S(1)} collective-permute-done((bf16[512,896]{1,0:T(8,128)(2,1)}, bf16[512,896]{1,0:T(8,128)(2,1)S(1)}, u32[]{:S(2)}, u32[]{:S(2)}) %collective-permute-start.14) | collective-permute-done | bytes 917536 | tf_op jit(solution)/shard_map/ppermute | solution.py:38
  191.8 4.8 %collective-permute-start.16 = (bf16[256,896]{1,0:T(8,128)(2,1)S(1)}, bf16[256,896]{1,0:T(8,128)(2,1)S(1)}, u32[]{:S(2)}, u32[]{:S(2)}) collective-permute-start(bf16[256,896]{1,0:T(8,128)(2,1)S(1)} %get-tuple-element.21), channel_id=1, source_target_pairs={{0,384},{128,0},{256,128},{384,256},{1,385},{129,1},{257,129},{385... | collective-permute-start | bytes 1376264 | tf_op jit(solution)/shard_map/ppermute | solution.py:38
  196.6 4.8 %collective-permute-done.15 = bf16[256,896]{1,0:T(8,128)(2,1)S(1)} collective-permute-done((bf16[256,896]{1,0:T(8,128)(2,1)S(1)}, bf16[256,896]{1,0:T(8,128)(2,1)S(1)}, u32[]{:S(2)}, u32[]{:S(2)}) %collective-permute-start.15) | collective-permute-done | bytes 458784 | tf_op jit(solution)/shard_map/ppermute | solution.py:38
  202.6 25.2 %all_to_all.40 = bf16[8,64,896]{2,1,0:T(8,128)(2,1)S(1)} all-to-all(bf16[8,64,896]{2,1,0:T(8,128)(2,1)S(1)} %bitcast.98), channel_id=1, replica_groups=mesh['x'=4,'z'=8,'y'=8,'core'=2] {'z'}, dimensions={0} | all-to-all | bytes 1835008 | tf_op jit(solution)/shard_map/all_to_all | solution.py:42
  231.2 3.6 all-to-all-start.4
  235.3 19.5 %all-to-all-done.4 = bf16[8,64,896]{2,1,0:T(8,128)(2,1)S(1)} async-done(((bf16[8,64,896]{2,1,0:T(8,128)(2,1)}), bf16[8,64,896]{2,1,0:T(8,128)(2,1)S(1)}, u32[]{:S(2)}, u32[]{:S(2)}) %all-to-all-start.4) | async-done | bytes 917536 | tf_op jit(solution)/shard_map/all_to_all | solution.py:42
  256.2 6.5 %all-to-all-start = ((bf16[8,40,2048]{2,1,0:T(8,128)(2,1)}), bf16[8,40,2048]{2,1,0:T(8,128)(2,1)}, u32[]{:S(2)}, u32[]{:S(2)}) async-start(bf16[8,40,2048]{2,1,0:T(8,128)(2,1)} %bitcast.5), calls=%async_computation | async-start | bytes 2621440 | tf_op jit(solution)/shard_map/all_to_all | solution.py:42
  262.7 3.0 collective-permute-start.18
  265.8 4.2 %collective-permute-start.17 = (bf16[512,896]{1,0:T(8,128)(2,1)S(1)}, bf16[512,896]{1,0:T(8,128)(2,1)S(1)}, u32[]{:S(2)}, u32[]{:S(2)}) collective-permute-start(bf16[512,896]{1,0:T(8,128)(2,1)S(1)} %bitcast.94), channel_id=1, source_target_pairs={{0,384},{128,0},{256,128},{384,256},{1,385},{129,1},{257,129},{385... | collective-permute-start | bytes 2752520 | tf_op jit(solution)/shard_map/ppermute | solution.py:38
  270.0 22.8 %all-to-all-done = bf16[8,40,2048]{2,1,0:T(8,128)(2,1)} async-done(((bf16[8,40,2048]{2,1,0:T(8,128)(2,1)}), bf16[8,40,2048]{2,1,0:T(8,128)(2,1)}, u32[]{:S(2)}, u32[]{:S(2)}) %all-to-all-start) | async-done | bytes 1310752 | tf_op jit(solution)/shard_map/all_to_all | solution.py:42
  292.8 7.2 %collective-permute-start.21 = (bf16[320,2048]{1,0:T(8,128)(2,1)}, bf16[320,2048]{1,0:T(8,128)(2,1)S(1)}, u32[]{:S(2)}, u32[]{:S(2)}) collective-permute-start(bf16[320,2048]{1,0:T(8,128)(2,1)} %bitcast.6.taken), channel_id=1, source_target_pairs={{0,1},{1,0},{2,3},{3,2},{4,5},{5,4},{6,7},{7,6},{8,9},{9,8},{10,11... | collective-permute-start | bytes 3932168 | tf_op jit(solution)/shard_map/ppermute | solution.py:38
  300.1 3.0 collective-permute-start.19
  303.2 4.3 %collective-permute-start.20 = (bf16[256,896]{1,0:T(8,128)(2,1)S(1)}, bf16[256,896]{1,0:T(8,128)(2,1)S(1)}, u32[]{:S(2)}, u32[]{:S(2)}) collective-permute-start(bf16[256,896]{1,0:T(8,128)(2,1)S(1)} %slice.180), channel_id=1, source_target_pairs={{0,384},{128,0},{256,128},{384,256},{1,385},{129,1},{257,129},{385... | collective-permute-start | bytes 1376264 | tf_op jit(solution)/shard_map/ppermute | solution.py:38
  308.7 7.7 %collective-permute-done.19.top = bf16[256,896]{1,0:T(8,128)(2,1)} collective-permute-done((bf16[256,896]{1,0:T(8,128)(2,1)S(1)}, bf16[256,896]{1,0:T(8,128)(2,1)}, u32[]{:S(2)}, u32[]{:S(2)}) %collective-permute-start.19) | collective-permute-done | bytes 458784 | tf_op jit(solution)/shard_map/ppermute | solution.py:38
  319.0 7.2 %serve.3 = bf16[320,2048]{1,0:T(8,128)(2,1)} custom-call(s32[1]{0:T(128)} %bitcast.3.me, bf16[320,2048]{1,0:T(8,128)(2,1)} %copy-done.8, bf16[512,896]{1,0:T(8,128)(2,1)} %bitcast.95, bf16[512,896]{1,0:T(8,128)(2,1)} %copy-done.5, bf16[256,896]{1,0:T(8,128)(2,1)} %collective-permute-done.19.top, bf16[256,896]{1,0:T(8,128)(2,1)} %copy-done.6, ...), custom_call_target="tpu_custom_call" | custom-call | tf_op jit(solution)/shard_map/serve/pallas_call | solution.py:309
  326.2 2.9 collective-permute-start.22
  330.0 3.5 all-to-all-start.6
  333.7 15.7 %all-to-all-done.6 = bf16[16,12,864]{2,1,0:T(8,128)(2,1)S(1)} async-done(((bf16[16,12,864]{2,1,0:T(8,128)(2,1)}), bf16[16,12,864]{2,1,0:T(8,128)(2,1)S(1)}, u32[]{:S(2)}, u32[]{:S(2)}) %all-to-all-start.6) | async-done | bytes 331808 | tf_op jit(solution)/shard_map/all_to_all | solution.py:42
  350.9 3.5 all-to-all-start.7
  354.4 7.2 %serve.2 = bf16[320,2048]{1,0:T(8,128)(2,1)} custom-call(s32[1]{0:T(128)} %bitcast.3.me, bf16[320,2048]{1,0:T(8,128)(2,1)} %bitcast.6.taken, bf16[512,896]{1,0:T(8,128)(2,1)} %bitcast.96, bf16[512,896]{1,0:T(8,128)(2,1)} %copy-done.5, bf16[256,896]{1,0:T(8,128)(2,1)} %collective-permute-done.19.top, bf16[256,896]{1,0:T(8,128)(2,1)} %copy-done.6, ...), custom_call_target="tpu_custom_call" | custom-call | tf_op jit(solution)/shard_map/serve/pallas_call | solution.py:309
  361.6 2.9 add_convert_fusion
  364.5 5.1 %all-to-all-done.7 = bf16[16,12,864]{2,1,0:T(8,128)(2,1)S(1)} async-done(((bf16[16,12,864]{2,1,0:T(8,128)(2,1)}), bf16[16,12,864]{2,1,0:T(8,128)(2,1)S(1)}, u32[]{:S(2)}, u32[]{:S(2)}) %all-to-all-start.7) | async-done | bytes 331808 | tf_op jit(solution)/shard_map/all_to_all | solution.py:42
  369.6 3.6 all-to-all-start.5
  374.3 33.7 %all-to-all-done.5 = bf16[8,40,2048]{2,1,0:T(8,128)(2,1)S(1)} async-done(((bf16[8,40,2048]{2,1,0:T(8,128)(2,1)}), bf16[8,40,2048]{2,1,0:T(8,128)(2,1)S(1)}, u32[]{:S(2)}, u32[]{:S(2)}) %all-to-all-start.5) | async-done | bytes 1310752 | tf_op jit(solution)/shard_map/all_to_all | solution.py:42
  (115 shorter events, 33.4 us)
Async XLA Ops:
  0.6 1.6 copy-start
  3.8 7.8 %copy-start.10 = (f32[1,64,864]{2,1,0:T(8,128)S(1)}, f32[1,64,864]{2,1,0:T(8,128)}, u32[]{:S(2)}) copy-start(f32[1,64,864]{2,1,0:T(8,128)} %param.18) | copy-start | bytes 663556
  3.8 7.8 %copy-start.13 = (bf16[128,2048]{1,0:T(8,128)(2,1)S(1)}, bf16[128,2048]{1,0:T(8,128)(2,1)}, u32[]{:S(2)}) copy-start(bf16[128,2048]{1,0:T(8,128)(2,1)} %param.12) | copy-start | bytes 1572868
  3.8 7.8 %copy-start.17 = (f32[128,1]{0,1:T(1,128)S(1)}, f32[128,1]{0,1:T(1,128)}, u32[]{:S(2)}) copy-start(f32[128,1]{0,1:T(1,128)} %param.14) | copy-start | bytes 1540
  3.8 42.6 %all-to-all-start.1 = ((bf16[8,40,2048]{2,1,0:T(8,128)(2,1)}), bf16[8,40,2048]{2,1,0:T(8,128)(2,1)S(1)}, u32[]{:S(2)}, u32[]{:S(2)}) async-start(bf16[8,40,2048]{2,1,0:T(8,128)(2,1)} %bitcast.11), calls=%async_computation.1 | async-start | bytes 2621440 | tf_op jit(solution)/shard_map/all_to_all | solution.py:42
  46.4 55.8 %copy-start.1 = (bf16[8,40,2048]{2,1,0:T(8,128)(2,1)}, bf16[8,40,2048]{2,1,0:T(8,128)(2,1)S(1)}, u32[]{:S(2)}) copy-start(bf16[8,40,2048]{2,1,0:T(8,128)(2,1)S(1)} %all-to-all-done.1) | copy-start | bytes 3932164
  47.7 57.6 %all-to-all-start.2 = ((bf16[8,40,2048]{2,1,0:T(8,128)(2,1)}), bf16[8,40,2048]{2,1,0:T(8,128)(2,1)}, u32[]{:S(2)}, u32[]{:S(2)}) async-start(bf16[8,40,2048]{2,1,0:T(8,128)(2,1)} %bitcast.15), calls=%async_computation.2 | async-start | bytes 2621440 | tf_op jit(solution)/shard_map/all_to_all | solution.py:42
  52.3 24.3 %collective-permute-start.2 = (bf16[64,896]{1,0:T(8,128)(2,1)S(1)}, bf16[64,896]{1,0:T(8,128)(2,1)S(1)}, u32[]{:S(2)}, u32[]{:S(2)}) collective-permute-start(bf16[64,896]{1,0:T(8,128)(2,1)S(1)} %concatenate.16), channel_id=1, source_target_pairs={{0,112},{16,0},{32,16},{48,32},{64,48},{80,64},{96,80},{112,96},{1... | collective-permute-start | bytes 344072 | tf_op jit(solution)/shard_map/ppermute | solution.py:38
  63.1 16.7 %collective-permute-start.3 = (bf16[64,896]{1,0:T(8,128)(2,1)S(1)}, bf16[64,896]{1,0:T(8,128)(2,1)S(1)}, u32[]{:S(2)}, u32[]{:S(2)}) collective-permute-start(bf16[64,896]{1,0:T(8,128)(2,1)S(1)} %concatenate.16), channel_id=1, source_target_pairs={{0,96},{16,112},{32,0},{48,16},{64,32},{80,48},{96,64},{112,80},{1... | collective-permute-start | bytes 344072 | tf_op jit(solution)/shard_map/ppermute | solution.py:38
  65.2 17.9 %collective-permute-start.4 = (bf16[64,896]{1,0:T(8,128)(2,1)S(1)}, bf16[64,896]{1,0:T(8,128)(2,1)S(1)}, u32[]{:S(2)}, u32[]{:S(2)}) collective-permute-start(bf16[64,896]{1,0:T(8,128)(2,1)S(1)} %concatenate.16), channel_id=1, source_target_pairs={{0,80},{16,96},{32,112},{48,0},{64,16},{80,32},{96,48},{112,64},{1... | collective-permute-start | bytes 344072 | tf_op jit(solution)/shard_map/ppermute | solution.py:38
  67.2 16.0 %collective-permute-start.5 = (bf16[64,896]{1,0:T(8,128)(2,1)S(1)}, bf16[64,896]{1,0:T(8,128)(2,1)S(1)}, u32[]{:S(2)}, u32[]{:S(2)}) collective-permute-start(bf16[64,896]{1,0:T(8,128)(2,1)S(1)} %concatenate.16), channel_id=1, source_target_pairs={{0,64},{16,80},{32,96},{48,112},{64,0},{80,16},{96,32},{112,48},{1... | collective-permute-start | bytes 344072 | tf_op jit(solution)/shard_map/ppermute | solution.py:38
  74.5 10.5 %collective-permute-start.6 = (bf16[64,896]{1,0:T(8,128)(2,1)S(1)}, bf16[64,896]{1,0:T(8,128)(2,1)S(1)}, u32[]{:S(2)}, u32[]{:S(2)}) collective-permute-start(bf16[64,896]{1,0:T(8,128)(2,1)S(1)} %concatenate.16), channel_id=1, source_target_pairs={{0,48},{16,64},{32,80},{48,96},{64,112},{80,0},{96,16},{112,32},{1... | collective-permute-start | bytes 344072 | tf_op jit(solution)/shard_map/ppermute | solution.py:38
  76.6 15.8 %collective-permute-start.7 = (bf16[64,896]{1,0:T(8,128)(2,1)S(1)}, bf16[64,896]{1,0:T(8,128)(2,1)S(1)}, u32[]{:S(2)}, u32[]{:S(2)}) collective-permute-start(bf16[64,896]{1,0:T(8,128)(2,1)S(1)} %concatenate.16), channel_id=1, source_target_pairs={{0,32},{16,48},{32,64},{48,80},{64,96},{80,112},{96,0},{112,16},{1... | collective-permute-start | bytes 344072 | tf_op jit(solution)/shard_map/ppermute | solution.py:38
  79.7 15.9 %collective-permute-start.8 = (bf16[64,896]{1,0:T(8,128)(2,1)S(1)}, bf16[64,896]{1,0:T(8,128)(2,1)S(1)}, u32[]{:S(2)}, u32[]{:S(2)}) collective-permute-start(bf16[64,896]{1,0:T(8,128)(2,1)S(1)} %concatenate.16), channel_id=1, source_target_pairs={{0,16},{16,32},{32,48},{48,64},{64,80},{80,96},{96,112},{112,0},{1... | collective-permute-start | bytes 344072 | tf_op jit(solution)/shard_map/ppermute | solution.py:38
  95.7 43.1 %copy-start.2 = (bf16[8,64,896]{2,1,0:T(8,128)(2,1)}, bf16[8,64,896]{2,1,0:T(8,128)(2,1)S(1)}, u32[]{:S(2)}) copy-start(bf16[8,64,896]{2,1,0:T(8,128)(2,1)S(1)} %bitcast_dynamic-update-slice_fusion) | copy-start | bytes 2752516
  95.7 24.5 %collective-permute-start.10 = (bf16[512,896]{1,0:T(8,128)(2,1)S(1)}, bf16[512,896]{1,0:T(8,128)(2,1)}, u32[]{:S(2)}, u32[]{:S(2)}) collective-permute-start(bf16[512,896]{1,0:T(8,128)(2,1)S(1)} %bitcast.89), channel_id=1, source_target_pairs={{0,128},{128,256},{256,384},{384,0},{1,129},{129,257},{257,385},{3... | collective-permute-start | bytes 2752520 | tf_op jit(solution)/shard_map/ppermute | solution.py:38
  98.8 25.1 %collective-permute-start.9 = (bf16[512,896]{1,0:T(8,128)(2,1)S(1)}, bf16[512,896]{1,0:T(8,128)(2,1)}, u32[]{:S(2)}, u32[]{:S(2)}) collective-permute-start(bf16[512,896]{1,0:T(8,128)(2,1)S(1)} %bitcast.90), channel_id=1, source_target_pairs={{0,384},{128,0},{256,128},{384,256},{1,385},{129,1},{257,129},{385... | collective-permute-start | bytes 2752520 | tf_op jit(solution)/shard_map/ppermute | solution.py:38
  102.2 36.6 %collective-permute-start = (bf16[320,2048]{1,0:T(8,128)(2,1)S(1)}, bf16[320,2048]{1,0:T(8,128)(2,1)}, u32[]{:S(2)}, u32[]{:S(2)}) collective-permute-start(bf16[320,2048]{1,0:T(8,128)(2,1)S(1)} %bitcast.86), channel_id=1, source_target_pairs={{0,1},{1,0},{2,3},{3,2},{4,5},{5,4},{6,7},{7,6},{8,9},{9,8},{10,11... | collective-permute-start | bytes 3932168 | tf_op jit(solution)/shard_map/ppermute | solution.py:38
  105.3 41.5 %collective-permute-start.1 = (bf16[320,2048]{1,0:T(8,128)(2,1)}, bf16[320,2048]{1,0:T(8,128)(2,1)}, u32[]{:S(2)}, u32[]{:S(2)}) collective-permute-start(bf16[320,2048]{1,0:T(8,128)(2,1)} %bitcast.16.own_sc), channel_id=1, source_target_pairs={{0,1},{1,0},{2,3},{3,2},{4,5},{5,4},{6,7},{7,6},{8,9},{9,8},{10,11... | collective-permute-start | bytes 3932168 | tf_op jit(solution)/shard_map/ppermute | solution.py:38
  122.0 13.9 %collective-permute-start.11 = (bf16[256,896]{1,0:T(8,128)(2,1)}, bf16[256,896]{1,0:T(8,128)(2,1)S(1)}, u32[]{:S(2)}, u32[]{:S(2)}) collective-permute-start(bf16[256,896]{1,0:T(8,128)(2,1)} %slice.161), channel_id=1, source_target_pairs={{0,128},{128,256},{256,384},{384,0},{1,129},{129,257},{257,385},{3... | collective-permute-start | bytes 1376264 | tf_op jit(solution)/shard_map/ppermute | solution.py:38
  125.8 13.0 %collective-permute-start.12 = (bf16[256,896]{1,0:T(8,128)(2,1)}, bf16[256,896]{1,0:T(8,128)(2,1)}, u32[]{:S(2)}, u32[]{:S(2)}) collective-permute-start(bf16[256,896]{1,0:T(8,128)(2,1)} %slice.162), channel_id=1, source_target_pairs={{0,384},{128,0},{256,128},{384,256},{1,385},{129,1},{257,129},{385... | collective-permute-start | bytes 1376264 | tf_op jit(solution)/shard_map/ppermute | solution.py:38
  136.0 2.9 copy-start.7
  160.7 22.7 %collective-permute-start.13 = (bf16[512,896]{1,0:T(8,128)(2,1)}, bf16[512,896]{1,0:T(8,128)(2,1)S(1)}, u32[]{:S(2)}, u32[]{:S(2)}) collective-permute-start(bf16[512,896]{1,0:T(8,128)(2,1)} %get-tuple-element.15), channel_id=1, source_target_pairs={{0,384},{128,0},{256,128},{384,256},{1,385},{129,1},{257,129},{385... | collective-permute-start | bytes 2752520 | tf_op jit(solution)/shard_map/ppermute | solution.py:38
  166.0 22.3 %collective-permute-start.14 = (bf16[512,896]{1,0:T(8,128)(2,1)}, bf16[512,896]{1,0:T(8,128)(2,1)S(1)}, u32[]{:S(2)}, u32[]{:S(2)}) collective-permute-start(bf16[512,896]{1,0:T(8,128)(2,1)} %get-tuple-element.17), channel_id=1, source_target_pairs={{0,128},{128,256},{256,384},{384,0},{1,129},{129,257},{257,385},{3... | collective-permute-start | bytes 2752520 | tf_op jit(solution)/shard_map/ppermute | solution.py:38
  188.4 13.8 %copy-start.9 = (bf16[512,896]{1,0:T(8,128)(2,1)S(1)}, bf16[512,896]{1,0:T(8,128)(2,1)}, u32[]{:S(2)}) copy-start(bf16[512,896]{1,0:T(8,128)(2,1)} %get-tuple-element.14) | copy-start | bytes 2752516
  189.9 11.5 %collective-permute-start.15 = (bf16[256,896]{1,0:T(8,128)(2,1)S(1)}, bf16[256,896]{1,0:T(8,128)(2,1)S(1)}, u32[]{:S(2)}, u32[]{:S(2)}) collective-permute-start(bf16[256,896]{1,0:T(8,128)(2,1)S(1)} %get-tuple-element.20), channel_id=1, source_target_pairs={{0,128},{128,256},{256,384},{384,0},{1,129},{129,257},{257,385},{3... | collective-permute-start | bytes 1376264 | tf_op jit(solution)/shard_map/ppermute | solution.py:38
  191.8 10.4 %collective-permute-start.16 = (bf16[256,896]{1,0:T(8,128)(2,1)S(1)}, bf16[256,896]{1,0:T(8,128)(2,1)S(1)}, u32[]{:S(2)}, u32[]{:S(2)}) collective-permute-start(bf16[256,896]{1,0:T(8,128)(2,1)S(1)} %get-tuple-element.21), channel_id=1, source_target_pairs={{0,384},{128,0},{256,128},{384,256},{1,385},{129,1},{257,129},{385... | collective-permute-start | bytes 1376264 | tf_op jit(solution)/shard_map/ppermute | solution.py:38
  227.9 1.2 copy-start.16
  230.1 4.7 %copy-start.20 = (s32[128,1]{0,1:T(1,128)S(1)}, s32[128,1]{0,1:T(1,128)}, u32[]{:S(2)}) copy-start(s32[128,1]{0,1:T(1,128)} %param.16) | copy-start | bytes 1540
  230.1 4.8 %copy-start.12 = (bf16[128,2048]{1,0:T(8,128)(2,1)S(1)}, bf16[128,2048]{1,0:T(8,128)(2,1)}, u32[]{:S(2)}) copy-start(bf16[128,2048]{1,0:T(8,128)(2,1)} %param.15) | copy-start | bytes 1572868
  231.2 23.6 %all-to-all-start.4 = ((bf16[8,64,896]{2,1,0:T(8,128)(2,1)}), bf16[8,64,896]{2,1,0:T(8,128)(2,1)S(1)}, u32[]{:S(2)}, u32[]{:S(2)}) async-start(bf16[8,64,896]{2,1,0:T(8,128)(2,1)} %broadcast_in_dim.92), calls=%async_computation.4 | async-start | bytes 1835008 | tf_op jit(solution)/shard_map/all_to_all | solution.py:42
  254.8 10.9 %copy-start.3 = (bf16[8,64,896]{2,1,0:T(8,128)(2,1)}, bf16[8,64,896]{2,1,0:T(8,128)(2,1)S(1)}, u32[]{:S(2)}) copy-start(bf16[8,64,896]{2,1,0:T(8,128)(2,1)S(1)} %all-to-all-done.4) | copy-start | bytes 2752516
  256.2 36.6 %all-to-all-start = ((bf16[8,40,2048]{2,1,0:T(8,128)(2,1)}), bf16[8,40,2048]{2,1,0:T(8,128)(2,1)}, u32[]{:S(2)}, u32[]{:S(2)}) async-start(bf16[8,40,2048]{2,1,0:T(8,128)(2,1)} %bitcast.5), calls=%async_computation | async-start | bytes 2621440 | tf_op jit(solution)/shard_map/all_to_all | solution.py:42
  262.7 37.3 %collective-permute-start.18 = (bf16[512,896]{1,0:T(8,128)(2,1)S(1)}, bf16[512,896]{1,0:T(8,128)(2,1)S(1)}, u32[]{:S(2)}, u32[]{:S(2)}) collective-permute-start(bf16[512,896]{1,0:T(8,128)(2,1)S(1)} %bitcast.93), channel_id=1, source_target_pairs={{0,128},{128,256},{256,384},{384,0},{1,129},{129,257},{257,385},{3... | collective-permute-start | bytes 2752520 | tf_op jit(solution)/shard_map/ppermute | solution.py:38
  265.8 37.4 %collective-permute-start.17 = (bf16[512,896]{1,0:T(8,128)(2,1)S(1)}, bf16[512,896]{1,0:T(8,128)(2,1)S(1)}, u32[]{:S(2)}, u32[]{:S(2)}) collective-permute-start(bf16[512,896]{1,0:T(8,128)(2,1)S(1)} %bitcast.94), channel_id=1, source_target_pairs={{0,384},{128,0},{256,128},{384,256},{1,385},{129,1},{257,129},{385... | collective-permute-start | bytes 2752520 | tf_op jit(solution)/shard_map/ppermute | solution.py:38
  292.8 14.8 %collective-permute-start.21 = (bf16[320,2048]{1,0:T(8,128)(2,1)}, bf16[320,2048]{1,0:T(8,128)(2,1)S(1)}, u32[]{:S(2)}, u32[]{:S(2)}) collective-permute-start(bf16[320,2048]{1,0:T(8,128)(2,1)} %bitcast.6.taken), channel_id=1, source_target_pairs={{0,1},{1,0},{2,3},{3,2},{4,5},{5,4},{6,7},{7,6},{8,9},{9,8},{10,11... | collective-permute-start | bytes 3932168 | tf_op jit(solution)/shard_map/ppermute | solution.py:38
  300.0 18.2 %copy-start.4 = (bf16[512,896]{1,0:T(8,128)(2,1)}, bf16[512,896]{1,0:T(8,128)(2,1)S(1)}, u32[]{:S(2)}) copy-start(bf16[512,896]{1,0:T(8,128)(2,1)S(1)} %collective-permute-done.18.left) | copy-start | bytes 2752516
  300.1 16.3 %collective-permute-start.19 = (bf16[256,896]{1,0:T(8,128)(2,1)S(1)}, bf16[256,896]{1,0:T(8,128)(2,1)}, u32[]{:S(2)}, u32[]{:S(2)}) collective-permute-start(bf16[256,896]{1,0:T(8,128)(2,1)S(1)} %slice.179), channel_id=1, source_target_pairs={{0,128},{128,256},{256,384},{384,0},{1,129},{129,257},{257,385},{3... | collective-permute-start | bytes 1376264 | tf_op jit(solution)/shard_map/ppermute | solution.py:38
  303.2 15.1 %copy-start.5 = (bf16[512,896]{1,0:T(8,128)(2,1)}, bf16[512,896]{1,0:T(8,128)(2,1)S(1)}, u32[]{:S(2)}) copy-start(bf16[512,896]{1,0:T(8,128)(2,1)S(1)} %collective-permute-done.17.right) | copy-start | bytes 2752516
  303.2 25.9 %copy-start.14 = (bf16[64,864]{1,0:T(8,128)(2,1)S(1)}, bf16[64,864]{1,0:T(8,128)(2,1)}, u32[]{:S(2)}) copy-start(bf16[64,864]{1,0:T(8,128)(2,1)} %get-tuple-element.27) | copy-start | bytes 331780
  303.2 15.0 %collective-permute-start.20 = (bf16[256,896]{1,0:T(8,128)(2,1)S(1)}, bf16[256,896]{1,0:T(8,128)(2,1)S(1)}, u32[]{:S(2)}, u32[]{:S(2)}) collective-permute-start(bf16[256,896]{1,0:T(8,128)(2,1)S(1)} %slice.180), channel_id=1, source_target_pairs={{0,384},{128,0},{256,128},{384,256},{1,385},{129,1},{257,129},{385... | collective-permute-start | bytes 1376264 | tf_op jit(solution)/shard_map/ppermute | solution.py:38
  307.6 1.1 copy-start.8
  326.2 7.3 %copy-start.19 = (s32[16]{0:T(128)S(1)}, s32[16]{0:T(128)}, u32[]{:S(2)}) copy-start(s32[16]{0:T(128)} %param.21) | copy-start | bytes 196
  326.2 35.4 %collective-permute-start.22 = (bf16[320,2048]{1,0:T(8,128)(2,1)}, bf16[320,2048]{1,0:T(8,128)(2,1)S(1)}, u32[]{:S(2)}, u32[]{:S(2)}) collective-permute-start(bf16[320,2048]{1,0:T(8,128)(2,1)} %serve.3), channel_id=1, source_target_pairs={{0,1},{1,0},{2,3},{3,2},{4,5},{5,4},{6,7},{7,6},{8,9},{9,8},{10,11... | collective-permute-start | bytes 3932168 | tf_op jit(solution)/shard_map/ppermute | solution.py:38
  330.0 19.3 %all-to-all-start.6 = ((bf16[16,12,864]{2,1,0:T(8,128)(2,1)}), bf16[16,12,864]{2,1,0:T(8,128)(2,1)S(1)}, u32[]{:S(2)}, u32[]{:S(2)}) async-start(bf16[16,12,864]{2,1,0:T(8,128)(2,1)} %reshape.142), calls=%async_computation.6 | async-start | bytes 917504 | tf_op jit(solution)/shard_map/all_to_all | solution.py:42
  350.9 18.7 %all-to-all-start.7 = ((bf16[16,12,864]{2,1,0:T(8,128)(2,1)}), bf16[16,12,864]{2,1,0:T(8,128)(2,1)S(1)}, u32[]{:S(2)}, u32[]{:S(2)}) async-start(bf16[16,12,864]{2,1,0:T(8,128)(2,1)} %broadcast_select_fusion), calls=%async_computation.7 | async-start | bytes 917504 | tf_op jit(solution)/shard_map/all_to_all | solution.py:42
  369.6 38.3 %all-to-all-start.5 = ((bf16[8,40,2048]{2,1,0:T(8,128)(2,1)}), bf16[8,40,2048]{2,1,0:T(8,128)(2,1)S(1)}, u32[]{:S(2)}, u32[]{:S(2)}) async-start(bf16[8,40,2048]{2,1,0:T(8,128)(2,1)} %bitcast.31), calls=%async_computation.5 | async-start | bytes 2621440 | tf_op jit(solution)/shard_map/all_to_all | solution.py:42
  373.2 34.7 %copy-start.18 = (f32[128,1]{0,1:T(1,128)S(1)}, f32[128,1]{0,1:T(1,128)}, u32[]{:S(2)}) copy-start(f32[128,1]{0,1:T(1,128)} %param.17) | copy-start | bytes 1540
  (3 other events, 2.8 us)

commit v4 on v3

--- a/solution.py
+++ b/solution.py
@@ -73,6 +73,26 @@
     return filled.astype(jnp.bfloat16).reshape(EXPERTS, CAP, payload.shape[1])
 
 
+def to_pairs(routes, targets, inputs, scaled):
+    chips = lax.axis_size("y")
+    me = lax.axis_index("y")
+    pair, odd = me // 2, lax.rem(me, 2)
+    ids = routes.reshape(-1)
+    away = lax.rem(ids - pair + EXPERTS, EXPERTS)
+    away = jnp.where(odd == 1, lax.rem(EXPERTS - away, EXPERTS), away)
+    places = targets - ids * CAP + away * CAP
+    blocks = jnp.stack([to_slots(places, inputs), to_slots(places, scaled)], axis=1)
+
+    def hop(value, step):
+        ends = [(k, (k + step if k % 2 == 0 else k - step) % chips) for k in range(chips)]
+        return lax.ppermute(value, "y", ends)
+
+    met = [blocks[0], hop(blocks[3], -1), hop(blocks[1], 2), hop(blocks[2], -3)]
+    met += [hop(block, 1) for block in met]
+    met += [pass_on(block, "core", 1) for block in met]
+    return [jnp.concatenate([block[k] for block in met], axis=0) for k in range(2)]
+
+
 def to_chips(slots):
     chips = lax.axis_size("y")
     return exchange(jnp.repeat(slots, chips // EXPERTS, axis=0), "y").reshape(-1, D)
@@ -100,17 +120,6 @@
     top = pass_on(left[:half], "x", 1)
     bottom = pass_on(right[half:], "x", -1)
     return value, right, top, bottom, left
-
-
-def found_along_z(value):
-    size = lax.axis_size("z")
-    me = lax.axis_index("z")
-    out = jnp.zeros((size,) + value.shape, value.dtype)
-    out = lax.dynamic_update_index_in_dim(out, value, me, 0)
-    for by in range(1, size):
-        got = pass_on(value, "z", -by)
-        out = lax.dynamic_update_index_in_dim(out, got, lax.rem(me + by, size), 0)
-    return out.reshape(-1, value.shape[1])
 
 
 def own_rows(right, left, near, own):
@@ -156,87 +165,50 @@
     wn[pl.ds(start_of(me, 3, wide), wide), :] = left[:, columns]
 
 
-def pre_body(me, own_in, other_in, own, right, top, bottom, left, act, silu, slope, wn, pre):
-    in_row_order(me[0], (own, right, top, bottom, left), wn, slice(0, LEAD + 128))
-    count = own_in.shape[0]
-    for half, taken in enumerate((own_in, other_in)):
-        pre[half * count : (half + 1) * count, :] = dot(taken[...], wn[...]) * IN_SCALE
+def back_terms(gate, up, down_back):
+    sigmoid_gate = jax.nn.sigmoid(gate)
+    silu_gate = gate * sigmoid_gate
+    return (
+        silu_gate * up,
+        down_back * up * sigmoid_gate * (1.0 + gate * (1.0 - sigmoid_gate)),
+        down_back * silu_gate,
+    )
+
+
+def terms_body(
+    me, taken, scaled, own, right, top, bottom, left,
+    to_right, to_left, near, mine, wn, pre, dn, g_in, g_sc,
+):
+    in_row_order(me[0], (own, right, top, bottom, left), wn, slice(0, COLS))
+    count = taken.shape[0]
+    pre[...] = dot(taken[...], wn[:, : LEAD + 128]) * IN_SCALE
+    dn[...] = dot(scaled[...], wn[:, LEAD:]) * OUT_SCALE
 
     def chunk(i, carry):
         at = pl.ds(pl.multiple_of(i * 64, 64), 64)
-        tail = pre[at, LEAD:]
-        pairs = (
-            (tail, pltpu.roll(tail, 128 - TAIL, 1), slice(0, 128)),
-            (pre[at, :MAIN], pre[at, MAIN:LEAD], slice(128, SIDE)),
+        act, gate_grad, up_grad = back_terms(pre[at, :MAIN], pre[at, MAIN:LEAD], dn[at, 128:])
+        tail, down_tail = pre[at, LEAD:], dn[at, :128]
+        lane = lanes(tail.shape)
+        act_t, gate_t, up_t = back_terms(
+            tail, pltpu.roll(tail, 128 - TAIL, 1), pltpu.roll(down_tail, 128 - 2 * TAIL, 1)
         )
-        for gate, up, cols in pairs:
-            sigmoid_gate = jax.nn.sigmoid(gate)
-            silu_gate = gate * sigmoid_gate
-            product = silu_gate * up
-            if cols.start == 0:
-                lane = lanes(tail.shape)
-                here = (lane >= 2 * TAIL) & (lane < 3 * TAIL)
-                product = jnp.where(here, pltpu.roll(product, 2 * TAIL, 1), 0.0)
-            act[at, cols] = b16(product)
-            silu[at, cols] = silu_gate
-            slope[at, cols] = up * sigmoid_gate * (1.0 + gate * (1.0 - sigmoid_gate))
+        up_t = jnp.where(lane < 2 * TAIL, pltpu.roll(up_t, TAIL, 1), 0.0)
+        here = (lane >= 2 * TAIL) & (lane < 3 * TAIL)
+        g_in[at, :MAIN] = b16(gate_grad)
+        g_in[at, MAIN:LEAD] = b16(up_grad)
+        g_in[at, LEAD:] = b16(jnp.where(lane < TAIL, gate_t, up_t))
+        g_sc[at, :128] = b16(jnp.where(here, pltpu.roll(act_t, 2 * TAIL, 1), 0.0))
+        g_sc[at, 128:] = b16(act)
         return carry
 
-    lax.fori_loop(0, 2 * count // 64, chunk, 0)
-
-
-def step_pre(own_in, other_in, pieces):
-    me = lax.axis_index("x").astype(jnp.int32).reshape(1)
-    count = 2 * own_in.shape[0]
-    return pl.pallas_call(
-        pre_body,
-        out_shape=(
-            jax.ShapeDtypeStruct((count, SIDE), jnp.bfloat16),
-            jax.ShapeDtypeStruct((count, SIDE), jnp.float32),
-            jax.ShapeDtypeStruct((count, SIDE), jnp.float32),
-        ),
-        in_specs=[pl.BlockSpec(memory_space=pltpu.SMEM)]
-        + [pl.BlockSpec(memory_space=pltpu.VMEM)] * 7,
-        scratch_shapes=[
-            pltpu.VMEM((D, LEAD + 128), jnp.bfloat16),
-            pltpu.VMEM((count, LEAD + 128), jnp.float32),
-        ],
-        interpret=TEST,
-        name="step_pre",
-    )(me, own_in, other_in, *pieces)
-
-
-def terms_body(
-    me, own_in, other_in, own_sc, other_sc, act, silu, slope, own, right, top, bottom, left,
-    to_right, to_left, near, mine, wn, dn, g_in,
-):
-    in_row_order(me[0], (own, right, top, bottom, left), wn, slice(LEAD, COLS))
-    count = own_in.shape[0]
-    for half, scaled in enumerate((own_sc, other_sc)):
-        dn[half * count : (half + 1) * count, :] = dot(scaled[...], wn[...]) * OUT_SCALE
-
-    def chunk(i, carry):
-        at = pl.ds(pl.multiple_of(i * 64, 64), 64)
-        down_back = dn[at, 128:]
-        g_in[at, :MAIN] = b16(down_back * slope[at, 128:])
-        g_in[at, MAIN:LEAD] = b16(down_back * silu[at, 128:])
-        down_tail = pltpu.roll(dn[at, :128], 128 - 2 * TAIL, 1)
-        gate_t, up_t = down_tail * slope[at, :128], down_tail * silu[at, :128]
-        lane = lanes(gate_t.shape)
-        up_t = jnp.where(lane < 2 * TAIL, pltpu.roll(up_t, TAIL, 1), 0.0)
-        g_in[at, LEAD:] = b16(jnp.where(lane < TAIL, gate_t, up_t))
-        return carry
-
-    lax.fori_loop(0, 2 * count // 64, chunk, 0)
+    lax.fori_loop(0, count // 64, chunk, 0)
     over_rows = ((0,), (0,))
     wide = own.shape[0]
     half = wide // 2
     for k in range(4):
         cols = pl.ds(start_of(me[0], k, wide), wide)
-        a = dot(own_in[:, cols], g_in[:count, :], over_rows)
-        a = (a + dot(other_in[:, cols], g_in[count:, :], over_rows)) * IN_SCALE
-        b = dot(own_sc[:, cols], act[:count, :], over_rows)
-        b = (b + dot(other_sc[:, cols], act[count:, :], over_rows)) * OUT_SCALE
+        a = dot(taken[:, cols], g_in[...], over_rows) * IN_SCALE
+        b = dot(scaled[:, cols], g_sc[...], over_rows) * OUT_SCALE
         parts = (
             (slice(0, LEAD), b16(a[:, :LEAD])),
             (slice(LEAD, LEAD + 128), b16(a[:, LEAD:] + b[:, :128])),
@@ -256,9 +228,9 @@
                 near[1, :, at] = value[half:]
 
 
-def step_terms(rows, made, pieces):
+def step_terms(taken, scaled, pieces):
     me = lax.axis_index("x").astype(jnp.int32).reshape(1)
-    count = 2 * rows[0].shape[0]
+    count = taken.shape[0]
     wide = pieces[0].shape[0]
     chunk = jax.ShapeDtypeStruct((wide, COLS), jnp.bfloat16)
     return pl.pallas_call(
@@ -270,15 +242,17 @@
             chunk,
         ),
         in_specs=[pl.BlockSpec(memory_space=pltpu.SMEM)]
-        + [pl.BlockSpec(memory_space=pltpu.VMEM)] * 12,
+        + [pl.BlockSpec(memory_space=pltpu.VMEM)] * 7,
         scratch_shapes=[
-            pltpu.VMEM((D, SIDE), jnp.bfloat16),
+            pltpu.VMEM((D, COLS), jnp.bfloat16),
+            pltpu.VMEM((count, LEAD + 128), jnp.float32),
             pltpu.VMEM((count, SIDE), jnp.float32),
             pltpu.VMEM((count, LEAD + 128), jnp.bfloat16),
+            pltpu.VMEM((count, SIDE), jnp.bfloat16),
         ],
         interpret=TEST,
         name="step_terms",
-    )(me, *rows, *made, *pieces)
+    )(me, taken, scaled, *pieces)
 
 
 def serve_body(me, taken, own, right, top, bottom, left, out, wn, pre, act):
@@ -348,14 +322,9 @@
     old_weights = master_weights[0]
     step_targets = slot_of(step_routes)
     scaled = b16(f32(step_cotangent) * step_gates)
-    old_wide = found_along_z(arranged(b16(old_weights)))
-    old_pieces = found_along_x(old_wide)
-    own_in = to_chips(to_slots(step_targets, step_inputs))
-    own_sc = to_chips(to_slots(step_targets, scaled))
-    other_in = pass_on(own_in, "core", 1)
-    other_sc = pass_on(own_sc, "core", 1)
-    made = step_pre(own_in, other_in, old_pieces)
-    gradient = own_rows(*step_terms((own_in, other_in, own_sc, other_sc), made, old_pieces))
+    old_pieces = all_rows(arranged(b16(old_weights)))
+    taken, taken_scaled = to_pairs(step_routes, step_targets, step_inputs, scaled)
+    gradient = own_rows(*step_terms(taken, taken_scaled, old_pieces))
     first_new = beta_one * first_moment[0] + (1.0 - beta_one) * gradient
     second_new = beta_two * second_moment[0] + (1.0 - beta_two) * gradient * gradient
     first_hat = first_new / (1.0 - beta_one**adam_step)

time: 411 us -> 397 us (0.966)
  waiting for transfers between devices: 201 us -> 158 us
  local copies, waits for them, and re-layouts: 15.1 us -> 32.9 us
  starting transfers between devices: 120 us -> 129 us
  Pallas kernels: 36.4 us -> 29.9 us
  blocking collectives: 25.2 us -> 30.3 us
    all_to_all x7 -> x6, waiting for transfers between devices: 131 us -> 99 us  [exchange(): return lax.all_to_all(value, axis, split_axis=0, concat_axis=0, tiled=True)]
    unnamed x42 -> x55, local copies, waits for them, and re-layouts: 2.7 us -> 24.1 us
    ppermute x0 -> x7, starting transfers between devices: none -> 20.5 us  [hop(): return lax.ppermute(value, 'y', ends)]
    ppermute x23 -> x22, waiting for transfers between devices: 69.5 us -> 56.5 us  [pass_on(): lax.ppermute(value, axis, [(k, (k + by) % size) for k in range(size)])]
    pallas_call x1 -> x0, Pallas kernels: 8 us -> none  [step_pre(): pl.pallas_call(pre_body, out_shape=(jax.ShapeDtypeStruct((count, SIDE), j...]
    ppermute x23 -> x22, starting transfers between devices: 87.1 us -> 79.5 us  [pass_on(): lax.ppermute(value, axis, [(k, (k + by) % size) for k in range(size)])]
    all_to_all x1, blocking collectives: 25.2 us -> 30.3 us  [exchange(): return lax.all_to_all(value, axis, split_axis=0, concat_axis=0, tiled=True)]
    all_to_all x7 -> x6, starting transfers between devices: 32.6 us -> 29 us  [exchange(): return lax.all_to_all(value, axis, split_axis=0, concat_axis=0, tiled=True)]
  transfers between devices with their start and end apart: 30 -> 35, of which waited for: 18 -> 17; matrix products, arithmetic and copies ran while one was open for 3% -> 8% of each run, Pallas kernels for 4% -> 2%
where the time goes in v4:
time: 397 us; the launch traced here: 395 us
  waiting for transfers between devices  158 us (40%)
  starting transfers between devices  129 us (32%)
  local copies, waits for them, and re-layouts  32.9 us (8%)
  blocking collectives  30.3 us (8%)
  Pallas kernels  29.9 us (8%)
  other arithmetic  9.39 us (2%)
  matrix products  4.41 us (1%)
    all_to_all x6, waiting for transfers between devices, exchange(): return lax.all_to_all(value, axis, split_axis=0, concat_axis=0, tiled=True)  99 us
    ppermute x22, starting transfers between devices, pass_on(): lax.ppermute(value, axis, [(k, (k + by) % size) for k in range(size)])  79.5 us
    ppermute x22, waiting for transfers between devices, pass_on(): lax.ppermute(value, axis, [(k, (k + by) % size) for k in range(size)])  56.5 us
    all_to_all x1, blocking collectives, exchange(): return lax.all_to_all(value, axis, split_axis=0, concat_axis=0, tiled=True)  30.3 us
    all_to_all x6, starting transfers between devices, exchange(): return lax.all_to_all(value, axis, split_axis=0, concat_axis=0, tiled=True)  29 us
    unnamed x55, local copies, waits for them, and re-layouts  24.1 us
    ppermute x7, starting transfers between devices, hop(): return lax.ppermute(value, 'y', ends)  20.5 us
    pallas_call x1, Pallas kernels, step_terms(): pl.pallas_call(terms_body, out_shape=(chunk, chunk, jax.ShapeDtypeStruct(...  15.4 us
  transfers between devices with their start and end apart: 35, of which 17 were waited for; matrix products, arithmetic and copies ran while one was open for 8% of the time, Pallas kernels for 2%

profile of v4, /device:TPU:1, one launch (start us, length us, event | category | flops | bytes accessed | tf_op | source)
XLA Modules:
  0.0 395.2 jit_solution(11814347947839297916)
XLA Ops:
  5.0 4.0 %collective-permute-start.3 = (bf16[2,40,2048]{2,1,0:T(8,128)(2,1)S(1)}, bf16[2,40,2048]{2,1,0:T(8,128)(2,1)}, u32[]{:S(2)}, u32[]{:S(2)}) collective-permute-start(bf16[2,40,2048]{2,1,0:T(8,128)(2,1)S(1)} %get-tuple-element.12), channel_id=1, source_target_pairs={{0,2},{2,0},{4,6},{6,4},{8,10},{10,8},{12,14},{14,12},{1,3},{3,1},... | collective-permute-start | bytes 983048 | tf_op jit(solution)/shard_map/ppermute | solution.py:88
  9.0 6.6 %collective-permute-start.7 = (bf16[2,40,2048]{2,1,0:T(8,128)(2,1)S(1)}, bf16[2,40,2048]{2,1,0:T(8,128)(2,1)}, u32[]{:S(2)}, u32[]{:S(2)}) collective-permute-start(bf16[2,40,2048]{2,1,0:T(8,128)(2,1)S(1)} %get-tuple-element.12), channel_id=1, source_target_pairs={{0,1},{1,0},{2,3},{3,2},{4,5},{5,4},{6,7},{7,6},{8,9},{9,8},{10,11... | collective-permute-start | bytes 983048 | tf_op jit(solution)/shard_map/ppermute | solution.py:38
  15.7 1.9 collective-permute-start
  17.6 4.8 %collective-permute-start.1 = (bf16[2,40,2048]{2,1,0:T(8,128)(2,1)}, bf16[2,40,2048]{2,1,0:T(8,128)(2,1)}, u32[]{:S(2)}, u32[]{:S(2)}) collective-permute-start(bf16[2,40,2048]{2,1,0:T(8,128)(2,1)} %get-tuple-element.14), channel_id=1, source_target_pairs={{0,4},{2,14},{4,8},{6,2},{8,12},{10,6},{12,0},{14,10},{1,5},{3,15}... | collective-permute-start | bytes 983048 | tf_op jit(solution)/shard_map/ppermute | solution.py:88
  22.4 2.5 collective-permute-start.2
  26.3 10.0 %all-to-all-start.1 = ((bf16[8,64,896]{2,1,0:T(8,128)(2,1)}), bf16[8,64,896]{2,1,0:T(8,128)(2,1)S(1)}, u32[]{:S(2)}, u32[]{:S(2)}) async-start(bf16[8,64,896]{2,1,0:T(8,128)(2,1)} %broadcast_in_dim.53), calls=%async_computation.1 | async-start | bytes 1835008 | tf_op jit(solution)/shard_map/all_to_all | solution.py:42
  39.9 3.4 collective-permute-start.5
  43.5 2.0 collective-permute-start.6
  50.7 8.1 %collective-permute-start.8 = (bf16[2,40,2048]{2,1,0:T(8,128)(2,1)}, bf16[2,40,2048]{2,1,0:T(8,128)(2,1)S(1)}, u32[]{:S(2)}, u32[]{:S(2)}) collective-permute-start(bf16[2,40,2048]{2,1,0:T(8,128)(2,1)} %collective-permute-done), channel_id=1, source_target_pairs={{0,1},{1,0},{2,3},{3,2},{4,5},{5,4},{6,7},{7,6},{8,9},{9,8},{10,11... | collective-permute-start | bytes 983048 | tf_op jit(solution)/shard_map/ppermute | solution.py:38
  64.3 2.4 collective-permute-start.10
  69.7 3.1 collective-permute-start.11
  74.6 1.9 collective-permute-start.12
  78.2 2.4 collective-permute-start.13
  81.4 1.9 collective-permute-start.14
  87.6 4.6 %collective-permute-start.15 = (bf16[512,896]{1,0:T(8,128)(2,1)S(1)}, bf16[512,896]{1,0:T(8,128)(2,1)S(1)}, u32[]{:S(2)}, u32[]{:S(2)}) collective-permute-start(bf16[512,896]{1,0:T(8,128)(2,1)S(1)} %bitcast.200), channel_id=1, source_target_pairs={{0,384},{128,0},{256,128},{384,256},{1,385},{129,1},{257,129},{385... | collective-permute-start | bytes 2752520 | tf_op jit(solution)/shard_map/ppermute | solution.py:38
  95.7 14.5 %collective-permute-done.16.left = bf16[512,896]{1,0:T(8,128)(2,1)S(1)} collective-permute-done((bf16[512,896]{1,0:T(8,128)(2,1)S(1)}, bf16[512,896]{1,0:T(8,128)(2,1)S(1)}, u32[]{:S(2)}, u32[]{:S(2)}) %collective-permute-start.16) | collective-permute-done | bytes 917536 | tf_op jit(solution)/shard_map/ppermute | solution.py:38
  110.2 1.9 collective-permute-start.17
  112.2 4.6 %collective-permute-start.18 = (bf16[256,896]{1,0:T(8,128)(2,1)S(1)}, bf16[256,896]{1,0:T(8,128)(2,1)S(1)}, u32[]{:S(2)}, u32[]{:S(2)}) collective-permute-start(bf16[256,896]{1,0:T(8,128)(2,1)S(1)} %slice.352), channel_id=1, source_target_pairs={{0,384},{128,0},{256,128},{384,256},{1,385},{129,1},{257,129},{385... | collective-permute-start | bytes 1376264 | tf_op jit(solution)/shard_map/ppermute | solution.py:38
  118.6 5.5 %collective-permute-done.17.top = bf16[256,896]{1,0:T(8,128)(2,1)S(1)} collective-permute-done((bf16[256,896]{1,0:T(8,128)(2,1)S(1)}, bf16[256,896]{1,0:T(8,128)(2,1)S(1)}, u32[]{:S(2)}, u32[]{:S(2)}) %collective-permute-start.17) | collective-permute-done | bytes 458784 | tf_op jit(solution)/shard_map/ppermute | solution.py:38
  125.8 15.4 %step_terms.1 = (bf16[512,896]{1,0:T(8,128)(2,1)}, bf16[512,896]{1,0:T(8,128)(2,1)}, bf16[2,256,896]{2,1,0:T(8,128)(2,1)}, bf16[512,896]{1,0:T(8,128)(2,1)}) custom-call(s32[1]{0:T(128)} %bitcast.3.me, bf16[640,2048]{1,0:T(8,128)(2,1)} %get-tuple-element.27.taken, bf16[640,2048]{1,0:T(8,128)(2,1)} %get-tuple-element.26.scaled, bf16[512,896]{1,0:T(8,128)(2,1)} %bitcast.201, ...), custom_call_target="tpu_custom_call" | custom-call | tf_op jit(solution)/shard_map/step_terms/pallas_call | solution.py:236
  141.2 5.4 %collective-permute-start.19 = (bf16[512,896]{1,0:T(8,128)(2,1)}, bf16[512,896]{1,0:T(8,128)(2,1)S(1)}, u32[]{:S(2)}, u32[]{:S(2)}) collective-permute-start(bf16[512,896]{1,0:T(8,128)(2,1)} %get-tuple-element.9), channel_id=1, source_target_pairs={{0,384},{128,0},{256,128},{384,256},{1,385},{129,1},{257,129},{385... | collective-permute-start | bytes 2752520 | tf_op jit(solution)/shard_map/ppermute | solution.py:38
  146.7 1.9 collective-permute-start.20
  148.6 15.6 %collective-permute-done.19 = bf16[512,896]{1,0:T(8,128)(2,1)S(1)} collective-permute-done((bf16[512,896]{1,0:T(8,128)(2,1)}, bf16[512,896]{1,0:T(8,128)(2,1)S(1)}, u32[]{:S(2)}, u32[]{:S(2)}) %collective-permute-start.19) | collective-permute-done | bytes 917536 | tf_op jit(solution)/shard_map/ppermute | solution.py:38
  164.2 4.9 %collective-permute-done.20 = bf16[512,896]{1,0:T(8,128)(2,1)S(1)} collective-permute-done((bf16[512,896]{1,0:T(8,128)(2,1)}, bf16[512,896]{1,0:T(8,128)(2,1)S(1)}, u32[]{:S(2)}, u32[]{:S(2)}) %collective-permute-start.20) | collective-permute-done | bytes 917536 | tf_op jit(solution)/shard_map/ppermute | solution.py:38
  170.5 1.9 collective-permute-start.21
  172.4 4.8 %collective-permute-start.22 = (bf16[256,896]{1,0:T(8,128)(2,1)S(1)}, bf16[256,896]{1,0:T(8,128)(2,1)S(1)}, u32[]{:S(2)}, u32[]{:S(2)}) collective-permute-start(bf16[256,896]{1,0:T(8,128)(2,1)S(1)} %get-tuple-element.19), channel_id=1, source_target_pairs={{0,384},{128,0},{256,128},{384,256},{1,385},{129,1},{257,129},{385... | collective-permute-start | bytes 1376264 | tf_op jit(solution)/shard_map/ppermute | solution.py:38
  177.2 4.9 %collective-permute-done.21 = bf16[256,896]{1,0:T(8,128)(2,1)S(1)} collective-permute-done((bf16[256,896]{1,0:T(8,128)(2,1)S(1)}, bf16[256,896]{1,0:T(8,128)(2,1)S(1)}, u32[]{:S(2)}, u32[]{:S(2)}) %collective-permute-start.21) | collective-permute-done | bytes 458784 | tf_op jit(solution)/shard_map/ppermute | solution.py:38
  183.4 30.3 %all_to_all.35 = bf16[8,64,896]{2,1,0:T(8,128)(2,1)S(1)} all-to-all(bf16[8,64,896]{2,1,0:T(8,128)(2,1)S(1)} %bitcast.202), channel_id=1, replica_groups=mesh['x'=4,'z'=8,'y'=8,'core'=2] {'z'}, dimensions={0} | all-to-all | bytes 1835008 | tf_op jit(solution)/shard_map/all_to_all | solution.py:42
  216.4 3.6 all-to-all-start.3
  220.4 21.3 %all-to-all-done.3 = bf16[8,64,896]{2,1,0:T(8,128)(2,1)S(1)} async-done(((bf16[8,64,896]{2,1,0:T(8,128)(2,1)}), bf16[8,64,896]{2,1,0:T(8,128)(2,1)S(1)}, u32[]{:S(2)}, u32[]{:S(2)}) %all-to-all-start.3) | async-done | bytes 917536 | tf_op jit(solution)/shard_map/all_to_all | solution.py:42
  243.2 5.0 %all-to-all-start = ((bf16[8,40,2048]{2,1,0:T(8,128)(2,1)}), bf16[8,40,2048]{2,1,0:T(8,128)(2,1)}, u32[]{:S(2)}, u32[]{:S(2)}) async-start(bf16[8,40,2048]{2,1,0:T(8,128)(2,1)} %bitcast.5), calls=%async_computation | async-start | bytes 2621440 | tf_op jit(solution)/shard_map/all_to_all | solution.py:42
  248.1 2.6 collective-permute-start.24
  250.8 4.6 %collective-permute-start.23 = (bf16[512,896]{1,0:T(8,128)(2,1)S(1)}, bf16[512,896]{1,0:T(8,128)(2,1)S(1)}, u32[]{:S(2)}, u32[]{:S(2)}) collective-permute-start(bf16[512,896]{1,0:T(8,128)(2,1)S(1)} %bitcast.195), channel_id=1, source_target_pairs={{0,384},{128,0},{256,128},{384,256},{1,385},{129,1},{257,129},{385... | collective-permute-start | bytes 2752520 | tf_op jit(solution)/shard_map/ppermute | solution.py:38
  255.4 23.3 %all-to-all-done = bf16[8,40,2048]{2,1,0:T(8,128)(2,1)} async-done(((bf16[8,40,2048]{2,1,0:T(8,128)(2,1)}), bf16[8,40,2048]{2,1,0:T(8,128)(2,1)}, u32[]{:S(2)}, u32[]{:S(2)}) %all-to-all-start) | async-done | bytes 1310752 | tf_op jit(solution)/shard_map/all_to_all | solution.py:42
  278.7 6.8 %collective-permute-start.27 = (bf16[320,2048]{1,0:T(8,128)(2,1)}, bf16[320,2048]{1,0:T(8,128)(2,1)S(1)}, u32[]{:S(2)}, u32[]{:S(2)}) collective-permute-start(bf16[320,2048]{1,0:T(8,128)(2,1)} %bitcast.6.taken), channel_id=1, source_target_pairs={{0,1},{1,0},{2,3},{3,2},{4,5},{5,4},{6,7},{7,6},{8,9},{9,8},{10,11... | collective-permute-start | bytes 3932168 | tf_op jit(solution)/shard_map/ppermute | solution.py:38
  285.5 2.6 collective-permute-start.25
  288.3 4.7 %collective-permute-start.26 = (bf16[256,896]{1,0:T(8,128)(2,1)S(1)}, bf16[256,896]{1,0:T(8,128)(2,1)S(1)}, u32[]{:S(2)}, u32[]{:S(2)}) collective-permute-start(bf16[256,896]{1,0:T(8,128)(2,1)S(1)} %slice.370), channel_id=1, source_target_pairs={{0,384},{128,0},{256,128},{384,256},{1,385},{129,1},{257,129},{385... | collective-permute-start | bytes 1376264 | tf_op jit(solution)/shard_map/ppermute | solution.py:38
  294.1 7.7 %collective-permute-done.25.top = bf16[256,896]{1,0:T(8,128)(2,1)} collective-permute-done((bf16[256,896]{1,0:T(8,128)(2,1)S(1)}, bf16[256,896]{1,0:T(8,128)(2,1)}, u32[]{:S(2)}, u32[]{:S(2)}) %collective-permute-start.25) | collective-permute-done | bytes 458784 | tf_op jit(solution)/shard_map/ppermute | solution.py:38
  304.2 7.3 %serve.3 = bf16[320,2048]{1,0:T(8,128)(2,1)} custom-call(s32[1]{0:T(128)} %bitcast.3.me, bf16[320,2048]{1,0:T(8,128)(2,1)} %copy-done.8, bf16[512,896]{1,0:T(8,128)(2,1)} %bitcast.196, bf16[512,896]{1,0:T(8,128)(2,1)} %copy-done.3, bf16[256,896]{1,0:T(8,128)(2,1)} %collective-permute-done.25.top, bf16[256,896]{1,0:T(8,128)(2,1)} %copy-done.7, ...), custom_call_target="tpu_custom_call" | custom-call | tf_op jit(solution)/shard_map/serve/pallas_call | solution.py:283
  311.5 2.8 collective-permute-start.28
  316.0 3.5 all-to-all-start.5
  319.6 15.7 %all-to-all-done.5 = bf16[16,12,864]{2,1,0:T(8,128)(2,1)S(1)} async-done(((bf16[16,12,864]{2,1,0:T(8,128)(2,1)}), bf16[16,12,864]{2,1,0:T(8,128)(2,1)S(1)}, u32[]{:S(2)}, u32[]{:S(2)}) %all-to-all-start.5) | async-done | bytes 331808 | tf_op jit(solution)/shard_map/all_to_all | solution.py:42
  336.9 3.5 all-to-all-start.6
  340.4 7.2 %serve.2 = bf16[320,2048]{1,0:T(8,128)(2,1)} custom-call(s32[1]{0:T(128)} %bitcast.3.me, bf16[320,2048]{1,0:T(8,128)(2,1)} %bitcast.6.taken, bf16[512,896]{1,0:T(8,128)(2,1)} %bitcast.197, bf16[512,896]{1,0:T(8,128)(2,1)} %copy-done.3, bf16[256,896]{1,0:T(8,128)(2,1)} %collective-permute-done.25.top, bf16[256,896]{1,0:T(8,128)(2,1)} %copy-done.7, ...), custom_call_target="tpu_custom_call" | custom-call | tf_op jit(solution)/shard_map/serve/pallas_call | solution.py:283
  347.6 2.9 add_convert_fusion
  350.6 5.1 %all-to-all-done.6 = bf16[16,12,864]{2,1,0:T(8,128)(2,1)S(1)} async-done(((bf16[16,12,864]{2,1,0:T(8,128)(2,1)}), bf16[16,12,864]{2,1,0:T(8,128)(2,1)S(1)}, u32[]{:S(2)}, u32[]{:S(2)}) %all-to-all-start.6) | async-done | bytes 331808 | tf_op jit(solution)/shard_map/all_to_all | solution.py:42
  355.6 3.6 all-to-all-start.4
  360.3 33.7 %all-to-all-done.4 = bf16[8,40,2048]{2,1,0:T(8,128)(2,1)S(1)} async-done(((bf16[8,40,2048]{2,1,0:T(8,128)(2,1)}), bf16[8,40,2048]{2,1,0:T(8,128)(2,1)S(1)}, u32[]{:S(2)}, u32[]{:S(2)}) %all-to-all-start.4) | async-done | bytes 1310752 | tf_op jit(solution)/shard_map/all_to_all | solution.py:42
  (129 shorter events, 55.3 us)
Async XLA Ops:
  0.6 24.3 %copy-start.10 = (f32[1,64,864]{2,1,0:T(8,128)S(1)}, f32[1,64,864]{2,1,0:T(8,128)}, u32[]{:S(2)}) copy-start(f32[1,64,864]{2,1,0:T(8,128)} %param.18) | copy-start | bytes 663556
  5.0 45.8 %collective-permute-start.3 = (bf16[2,40,2048]{2,1,0:T(8,128)(2,1)S(1)}, bf16[2,40,2048]{2,1,0:T(8,128)(2,1)}, u32[]{:S(2)}, u32[]{:S(2)}) collective-permute-start(bf16[2,40,2048]{2,1,0:T(8,128)(2,1)S(1)} %get-tuple-element.12), channel_id=1, source_target_pairs={{0,2},{2,0},{4,6},{6,4},{8,10},{10,8},{12,14},{14,12},{1,3},{3,1},... | collective-permute-start | bytes 983048 | tf_op jit(solution)/shard_map/ppermute | solution.py:88
  9.0 65.6 %collective-permute-start.7 = (bf16[2,40,2048]{2,1,0:T(8,128)(2,1)S(1)}, bf16[2,40,2048]{2,1,0:T(8,128)(2,1)}, u32[]{:S(2)}, u32[]{:S(2)}) collective-permute-start(bf16[2,40,2048]{2,1,0:T(8,128)(2,1)S(1)} %get-tuple-element.12), channel_id=1, source_target_pairs={{0,1},{1,0},{2,3},{3,2},{4,5},{5,4},{6,7},{7,6},{8,9},{9,8},{10,11... | collective-permute-start | bytes 983048 | tf_op jit(solution)/shard_map/ppermute | solution.py:38
  15.7 22.3 %collective-permute-start = (bf16[2,40,2048]{2,1,0:T(8,128)(2,1)}, bf16[2,40,2048]{2,1,0:T(8,128)(2,1)}, u32[]{:S(2)}, u32[]{:S(2)}) collective-permute-start(bf16[2,40,2048]{2,1,0:T(8,128)(2,1)} %get-tuple-element.13), channel_id=1, source_target_pairs={{0,14},{2,4},{4,2},{6,8},{8,6},{10,12},{12,10},{14,0},{1,15},{3,5}... | collective-permute-start | bytes 983048 | tf_op jit(solution)/shard_map/ppermute | solution.py:88
  17.6 22.3 %collective-permute-start.1 = (bf16[2,40,2048]{2,1,0:T(8,128)(2,1)}, bf16[2,40,2048]{2,1,0:T(8,128)(2,1)}, u32[]{:S(2)}, u32[]{:S(2)}) collective-permute-start(bf16[2,40,2048]{2,1,0:T(8,128)(2,1)} %get-tuple-element.14), channel_id=1, source_target_pairs={{0,4},{2,14},{4,8},{6,2},{8,12},{10,6},{12,0},{14,10},{1,5},{3,15}... | collective-permute-start | bytes 983048 | tf_op jit(solution)/shard_map/ppermute | solution.py:88
  22.4 21.1 %collective-permute-start.2 = (bf16[2,40,2048]{2,1,0:T(8,128)(2,1)S(1)}, bf16[2,40,2048]{2,1,0:T(8,128)(2,1)}, u32[]{:S(2)}, u32[]{:S(2)}) collective-permute-start(bf16[2,40,2048]{2,1,0:T(8,128)(2,1)S(1)} %get-tuple-element.15), channel_id=1, source_target_pairs={{0,10},{2,8},{4,14},{6,12},{8,2},{10,0},{12,6},{14,4},{1,11},{3,9}... | collective-permute-start | bytes 983048 | tf_op jit(solution)/shard_map/ppermute | solution.py:88
  26.3 59.3 %all-to-all-start.1 = ((bf16[8,64,896]{2,1,0:T(8,128)(2,1)}), bf16[8,64,896]{2,1,0:T(8,128)(2,1)S(1)}, u32[]{:S(2)}, u32[]{:S(2)}) async-start(bf16[8,64,896]{2,1,0:T(8,128)(2,1)} %broadcast_in_dim.53), calls=%async_computation.1 | async-start | bytes 1835008 | tf_op jit(solution)/shard_map/all_to_all | solution.py:42
  37.9 22.7 %collective-permute-start.4 = (bf16[2,40,2048]{2,1,0:T(8,128)(2,1)}, bf16[2,40,2048]{2,1,0:T(8,128)(2,1)}, u32[]{:S(2)}, u32[]{:S(2)}) collective-permute-start(bf16[2,40,2048]{2,1,0:T(8,128)(2,1)} %collective-permute-done), channel_id=1, source_target_pairs={{0,2},{2,0},{4,6},{6,4},{8,10},{10,8},{12,14},{14,12},{1,3},{3,1},... | collective-permute-start | bytes 983048 | tf_op jit(solution)/shard_map/ppermute | solution.py:88
  39.9 24.4 %collective-permute-start.5 = (bf16[2,40,2048]{2,1,0:T(8,128)(2,1)}, bf16[2,40,2048]{2,1,0:T(8,128)(2,1)}, u32[]{:S(2)}, u32[]{:S(2)}) collective-permute-start(bf16[2,40,2048]{2,1,0:T(8,128)(2,1)} %collective-permute-done.1), channel_id=1, source_target_pairs={{0,2},{2,0},{4,6},{6,4},{8,10},{10,8},{12,14},{14,12},{1,3},{3,1},... | collective-permute-start | bytes 983048 | tf_op jit(solution)/shard_map/ppermute | solution.py:88
  43.5 26.2 %collective-permute-start.6 = (bf16[2,40,2048]{2,1,0:T(8,128)(2,1)}, bf16[2,40,2048]{2,1,0:T(8,128)(2,1)}, u32[]{:S(2)}, u32[]{:S(2)}) collective-permute-start(bf16[2,40,2048]{2,1,0:T(8,128)(2,1)} %collective-permute-done.2), channel_id=1, source_target_pairs={{0,2},{2,0},{4,6},{6,4},{8,10},{10,8},{12,14},{14,12},{1,3},{3,1},... | collective-permute-start | bytes 983048 | tf_op jit(solution)/shard_map/ppermute | solution.py:88
  50.7 27.5 %collective-permute-start.8 = (bf16[2,40,2048]{2,1,0:T(8,128)(2,1)}, bf16[2,40,2048]{2,1,0:T(8,128)(2,1)S(1)}, u32[]{:S(2)}, u32[]{:S(2)}) collective-permute-start(bf16[2,40,2048]{2,1,0:T(8,128)(2,1)} %collective-permute-done), channel_id=1, source_target_pairs={{0,1},{1,0},{2,3},{3,2},{4,5},{5,4},{6,7},{7,6},{8,9},{9,8},{10,11... | collective-permute-start | bytes 983048 | tf_op jit(solution)/shard_map/ppermute | solution.py:38
  60.6 20.8 %collective-permute-start.9 = (bf16[2,40,2048]{2,1,0:T(8,128)(2,1)}, bf16[2,40,2048]{2,1,0:T(8,128)(2,1)S(1)}, u32[]{:S(2)}, u32[]{:S(2)}) collective-permute-start(bf16[2,40,2048]{2,1,0:T(8,128)(2,1)} %collective-permute-done.1), channel_id=1, source_target_pairs={{0,1},{1,0},{2,3},{3,2},{4,5},{5,4},{6,7},{7,6},{8,9},{9,8},{10,11... | collective-permute-start | bytes 983048 | tf_op jit(solution)/shard_map/ppermute | solution.py:38
  64.3 19.8 %collective-permute-start.10 = (bf16[2,40,2048]{2,1,0:T(8,128)(2,1)}, bf16[2,40,2048]{2,1,0:T(8,128)(2,1)S(1)}, u32[]{:S(2)}, u32[]{:S(2)}) collective-permute-start(bf16[2,40,2048]{2,1,0:T(8,128)(2,1)} %collective-permute-done.2), channel_id=1, source_target_pairs={{0,1},{1,0},{2,3},{3,2},{4,5},{5,4},{6,7},{7,6},{8,9},{9,8},{10,11... | collective-permute-start | bytes 983048 | tf_op jit(solution)/shard_map/ppermute | solution.py:38
  69.7 15.2 %collective-permute-start.11 = (bf16[2,40,2048]{2,1,0:T(8,128)(2,1)}, bf16[2,40,2048]{2,1,0:T(8,128)(2,1)S(1)}, u32[]{:S(2)}, u32[]{:S(2)}) collective-permute-start(bf16[2,40,2048]{2,1,0:T(8,128)(2,1)} %collective-permute-done.3), channel_id=1, source_target_pairs={{0,1},{1,0},{2,3},{3,2},{4,5},{5,4},{6,7},{7,6},{8,9},{9,8},{10,11... | collective-permute-start | bytes 983048 | tf_op jit(solution)/shard_map/ppermute | solution.py:38
  74.6 17.6 %collective-permute-start.12 = (bf16[2,40,2048]{2,1,0:T(8,128)(2,1)}, bf16[2,40,2048]{2,1,0:T(8,128)(2,1)}, u32[]{:S(2)}, u32[]{:S(2)}) collective-permute-start(bf16[2,40,2048]{2,1,0:T(8,128)(2,1)} %collective-permute-done.4), channel_id=1, source_target_pairs={{0,1},{1,0},{2,3},{3,2},{4,5},{5,4},{6,7},{7,6},{8,9},{9,8},{10,11... | collective-permute-start | bytes 983048 | tf_op jit(solution)/shard_map/ppermute | solution.py:38
  78.2 15.7 %collective-permute-start.13 = (bf16[2,40,2048]{2,1,0:T(8,128)(2,1)}, bf16[2,40,2048]{2,1,0:T(8,128)(2,1)}, u32[]{:S(2)}, u32[]{:S(2)}) collective-permute-start(bf16[2,40,2048]{2,1,0:T(8,128)(2,1)} %collective-permute-done.5), channel_id=1, source_target_pairs={{0,1},{1,0},{2,3},{3,2},{4,5},{5,4},{6,7},{7,6},{8,9},{9,8},{10,11... | collective-permute-start | bytes 983048 | tf_op jit(solution)/shard_map/ppermute | solution.py:38
  81.4 35.4 %collective-permute-start.14 = (bf16[2,40,2048]{2,1,0:T(8,128)(2,1)}, bf16[2,40,2048]{2,1,0:T(8,128)(2,1)}, u32[]{:S(2)}, u32[]{:S(2)}) collective-permute-start(bf16[2,40,2048]{2,1,0:T(8,128)(2,1)} %collective-permute-done.6), channel_id=1, source_target_pairs={{0,1},{1,0},{2,3},{3,2},{4,5},{5,4},{6,7},{7,6},{8,9},{9,8},{10,11... | collective-permute-start | bytes 983048 | tf_op jit(solution)/shard_map/ppermute | solution.py:38
  85.6 40.2 %copy-start.4 = (bf16[8,64,896]{2,1,0:T(8,128)(2,1)}, bf16[8,64,896]{2,1,0:T(8,128)(2,1)S(1)}, u32[]{:S(2)}) copy-start(bf16[8,64,896]{2,1,0:T(8,128)(2,1)S(1)} %all-to-all-done.1) | copy-start | bytes 2752516
  85.6 24.5 %collective-permute-start.16 = (bf16[512,896]{1,0:T(8,128)(2,1)S(1)}, bf16[512,896]{1,0:T(8,128)(2,1)S(1)}, u32[]{:S(2)}, u32[]{:S(2)}) collective-permute-start(bf16[512,896]{1,0:T(8,128)(2,1)S(1)} %bitcast.199), channel_id=1, source_target_pairs={{0,128},{128,256},{256,384},{384,0},{1,129},{129,257},{257,385},{3... | collective-permute-start | bytes 2752520 | tf_op jit(solution)/shard_map/ppermute | solution.py:38
  87.6 24.6 %collective-permute-start.15 = (bf16[512,896]{1,0:T(8,128)(2,1)S(1)}, bf16[512,896]{1,0:T(8,128)(2,1)S(1)}, u32[]{:S(2)}, u32[]{:S(2)}) collective-permute-start(bf16[512,896]{1,0:T(8,128)(2,1)S(1)} %bitcast.200), channel_id=1, source_target_pairs={{0,384},{128,0},{256,128},{384,256},{1,385},{129,1},{257,129},{385... | collective-permute-start | bytes 2752520 | tf_op jit(solution)/shard_map/ppermute | solution.py:38
  110.1 15.7 %copy-start.5 = (bf16[512,896]{1,0:T(8,128)(2,1)}, bf16[512,896]{1,0:T(8,128)(2,1)S(1)}, u32[]{:S(2)}) copy-start(bf16[512,896]{1,0:T(8,128)(2,1)S(1)} %collective-permute-done.16.left) | copy-start | bytes 2752516
  110.2 13.8 %collective-permute-start.17 = (bf16[256,896]{1,0:T(8,128)(2,1)S(1)}, bf16[256,896]{1,0:T(8,128)(2,1)S(1)}, u32[]{:S(2)}, u32[]{:S(2)}) collective-permute-start(bf16[256,896]{1,0:T(8,128)(2,1)S(1)} %slice.351), channel_id=1, source_target_pairs={{0,128},{128,256},{256,384},{384,0},{1,129},{129,257},{257,385},{3... | collective-permute-start | bytes 1376264 | tf_op jit(solution)/shard_map/ppermute | solution.py:38
  112.1 13.7 %copy-start.6 = (bf16[512,896]{1,0:T(8,128)(2,1)}, bf16[512,896]{1,0:T(8,128)(2,1)S(1)}, u32[]{:S(2)}) copy-start(bf16[512,896]{1,0:T(8,128)(2,1)S(1)} %collective-permute-done.15.right) | copy-start | bytes 2752516
  112.2 12.8 %collective-permute-start.18 = (bf16[256,896]{1,0:T(8,128)(2,1)S(1)}, bf16[256,896]{1,0:T(8,128)(2,1)S(1)}, u32[]{:S(2)}, u32[]{:S(2)}) collective-permute-start(bf16[256,896]{1,0:T(8,128)(2,1)S(1)} %slice.352), channel_id=1, source_target_pairs={{0,384},{128,0},{256,128},{384,256},{1,385},{129,1},{257,129},{385... | collective-permute-start | bytes 1376264 | tf_op jit(solution)/shard_map/ppermute | solution.py:38
  141.2 41.8 %copy-start.9 = (bf16[512,896]{1,0:T(8,128)(2,1)S(1)}, bf16[512,896]{1,0:T(8,128)(2,1)}, u32[]{:S(2)}) copy-start(bf16[512,896]{1,0:T(8,128)(2,1)} %get-tuple-element.8) | copy-start | bytes 2752516
  141.2 22.9 %collective-permute-start.19 = (bf16[512,896]{1,0:T(8,128)(2,1)}, bf16[512,896]{1,0:T(8,128)(2,1)S(1)}, u32[]{:S(2)}, u32[]{:S(2)}) collective-permute-start(bf16[512,896]{1,0:T(8,128)(2,1)} %get-tuple-element.9), channel_id=1, source_target_pairs={{0,384},{128,0},{256,128},{384,256},{1,385},{129,1},{257,129},{385... | collective-permute-start | bytes 2752520 | tf_op jit(solution)/shard_map/ppermute | solution.py:38
  146.7 22.4 %collective-permute-start.20 = (bf16[512,896]{1,0:T(8,128)(2,1)}, bf16[512,896]{1,0:T(8,128)(2,1)S(1)}, u32[]{:S(2)}, u32[]{:S(2)}) collective-permute-start(bf16[512,896]{1,0:T(8,128)(2,1)} %get-tuple-element.11), channel_id=1, source_target_pairs={{0,128},{128,256},{256,384},{384,0},{1,129},{129,257},{257,385},{3... | collective-permute-start | bytes 2752520 | tf_op jit(solution)/shard_map/ppermute | solution.py:38
  170.5 11.6 %collective-permute-start.21 = (bf16[256,896]{1,0:T(8,128)(2,1)S(1)}, bf16[256,896]{1,0:T(8,128)(2,1)S(1)}, u32[]{:S(2)}, u32[]{:S(2)}) collective-permute-start(bf16[256,896]{1,0:T(8,128)(2,1)S(1)} %get-tuple-element.18), channel_id=1, source_target_pairs={{0,128},{128,256},{256,384},{384,0},{1,129},{129,257},{257,385},{3... | collective-permute-start | bytes 1376264 | tf_op jit(solution)/shard_map/ppermute | solution.py:38
  172.4 10.5 %collective-permute-start.22 = (bf16[256,896]{1,0:T(8,128)(2,1)S(1)}, bf16[256,896]{1,0:T(8,128)(2,1)S(1)}, u32[]{:S(2)}, u32[]{:S(2)}) collective-permute-start(bf16[256,896]{1,0:T(8,128)(2,1)S(1)} %get-tuple-element.19), channel_id=1, source_target_pairs={{0,384},{128,0},{256,128},{384,256},{1,385},{129,1},{257,129},{385... | collective-permute-start | bytes 1376264 | tf_op jit(solution)/shard_map/ppermute | solution.py:38
  183.3 30.8 %copy-start.11 = (f32[1,64,864]{2,1,0:T(8,128)S(1)}, f32[1,64,864]{2,1,0:T(8,128)}, u32[]{:S(2)}) copy-start(f32[1,64,864]{2,1,0:T(8,128)} %param.18) | copy-start | bytes 663556
  183.3 30.8 %copy-start.15 = (f32[1,64,864]{2,1,0:T(8,128)S(1)}, f32[1,64,864]{2,1,0:T(8,128)}, u32[]{:S(2)}) copy-start(f32[1,64,864]{2,1,0:T(8,128)} %param.19) | copy-start | bytes 663556
  183.3 30.8 %copy-start.16 = (f32[1,64,864]{2,1,0:T(8,128)S(1)}, f32[1,64,864]{2,1,0:T(8,128)}, u32[]{:S(2)}) copy-start(f32[1,64,864]{2,1,0:T(8,128)} %param.20) | copy-start | bytes 663556
  216.4 25.4 %all-to-all-start.3 = ((bf16[8,64,896]{2,1,0:T(8,128)(2,1)}), bf16[8,64,896]{2,1,0:T(8,128)(2,1)S(1)}, u32[]{:S(2)}, u32[]{:S(2)}) async-start(bf16[8,64,896]{2,1,0:T(8,128)(2,1)} %broadcast_in_dim.54), calls=%async_computation.3 | async-start | bytes 1835008 | tf_op jit(solution)/shard_map/all_to_all | solution.py:42
  241.8 43.8 %copy-start.1 = (bf16[8,64,896]{2,1,0:T(8,128)(2,1)}, bf16[8,64,896]{2,1,0:T(8,128)(2,1)S(1)}, u32[]{:S(2)}) copy-start(bf16[8,64,896]{2,1,0:T(8,128)(2,1)S(1)} %all-to-all-done.3) | copy-start | bytes 2752516
  243.2 35.5 %all-to-all-start = ((bf16[8,40,2048]{2,1,0:T(8,128)(2,1)}), bf16[8,40,2048]{2,1,0:T(8,128)(2,1)}, u32[]{:S(2)}, u32[]{:S(2)}) async-start(bf16[8,40,2048]{2,1,0:T(8,128)(2,1)} %bitcast.5), calls=%async_computation | async-start | bytes 2621440 | tf_op jit(solution)/shard_map/all_to_all | solution.py:42
  248.1 37.3 %collective-permute-start.24 = (bf16[512,896]{1,0:T(8,128)(2,1)S(1)}, bf16[512,896]{1,0:T(8,128)(2,1)S(1)}, u32[]{:S(2)}, u32[]{:S(2)}) collective-permute-start(bf16[512,896]{1,0:T(8,128)(2,1)S(1)} %bitcast.194), channel_id=1, source_target_pairs={{0,128},{128,256},{256,384},{384,0},{1,129},{129,257},{257,385},{3... | collective-permute-start | bytes 2752520 | tf_op jit(solution)/shard_map/ppermute | solution.py:38
  250.8 37.4 %collective-permute-start.23 = (bf16[512,896]{1,0:T(8,128)(2,1)S(1)}, bf16[512,896]{1,0:T(8,128)(2,1)S(1)}, u32[]{:S(2)}, u32[]{:S(2)}) collective-permute-start(bf16[512,896]{1,0:T(8,128)(2,1)S(1)} %bitcast.195), channel_id=1, source_target_pairs={{0,384},{128,0},{256,128},{384,256},{1,385},{129,1},{257,129},{385... | collective-permute-start | bytes 2752520 | tf_op jit(solution)/shard_map/ppermute | solution.py:38
  278.7 14.3 %collective-permute-start.27 = (bf16[320,2048]{1,0:T(8,128)(2,1)}, bf16[320,2048]{1,0:T(8,128)(2,1)S(1)}, u32[]{:S(2)}, u32[]{:S(2)}) collective-permute-start(bf16[320,2048]{1,0:T(8,128)(2,1)} %bitcast.6.taken), channel_id=1, source_target_pairs={{0,1},{1,0},{2,3},{3,2},{4,5},{5,4},{6,7},{7,6},{8,9},{9,8},{10,11... | collective-permute-start | bytes 3932168 | tf_op jit(solution)/shard_map/ppermute | solution.py:38
  285.5 18.0 %copy-start.2 = (bf16[512,896]{1,0:T(8,128)(2,1)}, bf16[512,896]{1,0:T(8,128)(2,1)S(1)}, u32[]{:S(2)}) copy-start(bf16[512,896]{1,0:T(8,128)(2,1)S(1)} %collective-permute-done.24.left) | copy-start | bytes 2752516
  285.5 16.3 %collective-permute-start.25 = (bf16[256,896]{1,0:T(8,128)(2,1)S(1)}, bf16[256,896]{1,0:T(8,128)(2,1)}, u32[]{:S(2)}, u32[]{:S(2)}) collective-permute-start(bf16[256,896]{1,0:T(8,128)(2,1)S(1)} %slice.369), channel_id=1, source_target_pairs={{0,128},{128,256},{256,384},{384,0},{1,129},{129,257},{257,385},{3... | collective-permute-start | bytes 1376264 | tf_op jit(solution)/shard_map/ppermute | solution.py:38
  288.2 15.2 %copy-start.3 = (bf16[512,896]{1,0:T(8,128)(2,1)}, bf16[512,896]{1,0:T(8,128)(2,1)S(1)}, u32[]{:S(2)}) copy-start(bf16[512,896]{1,0:T(8,128)(2,1)S(1)} %collective-permute-done.23.right) | copy-start | bytes 2752516
  288.2 31.2 %copy-start.18 = (s32[16]{0:T(128)S(1)}, s32[16]{0:T(128)}, u32[]{:S(2)}) copy-start(s32[16]{0:T(128)} %param.21) | copy-start | bytes 196
  288.3 15.2 %collective-permute-start.26 = (bf16[256,896]{1,0:T(8,128)(2,1)S(1)}, bf16[256,896]{1,0:T(8,128)(2,1)S(1)}, u32[]{:S(2)}, u32[]{:S(2)}) collective-permute-start(bf16[256,896]{1,0:T(8,128)(2,1)S(1)} %slice.370), channel_id=1, source_target_pairs={{0,384},{128,0},{256,128},{384,256},{1,385},{129,1},{257,129},{385... | collective-permute-start | bytes 1376264 | tf_op jit(solution)/shard_map/ppermute | solution.py:38
  311.5 36.2 %collective-permute-start.28 = (bf16[320,2048]{1,0:T(8,128)(2,1)}, bf16[320,2048]{1,0:T(8,128)(2,1)S(1)}, u32[]{:S(2)}, u32[]{:S(2)}) collective-permute-start(bf16[320,2048]{1,0:T(8,128)(2,1)} %serve.3), channel_id=1, source_target_pairs={{0,1},{1,0},{2,3},{3,2},{4,5},{5,4},{6,7},{7,6},{8,9},{9,8},{10,11... | collective-permute-start | bytes 3932168 | tf_op jit(solution)/shard_map/ppermute | solution.py:38
  316.0 19.3 %all-to-all-start.5 = ((bf16[16,12,864]{2,1,0:T(8,128)(2,1)}), bf16[16,12,864]{2,1,0:T(8,128)(2,1)S(1)}, u32[]{:S(2)}, u32[]{:S(2)}) async-start(bf16[16,12,864]{2,1,0:T(8,128)(2,1)} %reshape.140), calls=%async_computation.5 | async-start | bytes 917504 | tf_op jit(solution)/shard_map/all_to_all | solution.py:42
  336.9 18.7 %all-to-all-start.6 = ((bf16[16,12,864]{2,1,0:T(8,128)(2,1)}), bf16[16,12,864]{2,1,0:T(8,128)(2,1)S(1)}, u32[]{:S(2)}, u32[]{:S(2)}) async-start(bf16[16,12,864]{2,1,0:T(8,128)(2,1)} %broadcast_select_fusion), calls=%async_computation.6 | async-start | bytes 917504 | tf_op jit(solution)/shard_map/all_to_all | solution.py:42
  350.6 43.4 %copy-start.17 = (f32[128,1]{0,1:T(1,128)S(1)}, f32[128,1]{0,1:T(1,128)}, u32[]{:S(2)}) copy-start(f32[128,1]{0,1:T(1,128)} %param.17) | copy-start | bytes 1540
  355.6 38.3 %all-to-all-start.4 = ((bf16[8,40,2048]{2,1,0:T(8,128)(2,1)}), bf16[8,40,2048]{2,1,0:T(8,128)(2,1)S(1)}, u32[]{:S(2)}, u32[]{:S(2)}) async-start(bf16[8,40,2048]{2,1,0:T(8,128)(2,1)} %bitcast.53), calls=%async_computation.4 | async-start | bytes 2621440 | tf_op jit(solution)/shard_map/all_to_all | solution.py:42
  (7 other events, 17.3 us)

commit v5 on v4

--- a/solution.py
+++ b/solution.py
@@ -73,24 +73,9 @@
     return filled.astype(jnp.bfloat16).reshape(EXPERTS, CAP, payload.shape[1])
 
 
-def to_pairs(routes, targets, inputs, scaled):
-    chips = lax.axis_size("y")
-    me = lax.axis_index("y")
-    pair, odd = me // 2, lax.rem(me, 2)
-    ids = routes.reshape(-1)
-    away = lax.rem(ids - pair + EXPERTS, EXPERTS)
-    away = jnp.where(odd == 1, lax.rem(EXPERTS - away, EXPERTS), away)
-    places = targets - ids * CAP + away * CAP
-    blocks = jnp.stack([to_slots(places, inputs), to_slots(places, scaled)], axis=1)
-
-    def hop(value, step):
-        ends = [(k, (k + step if k % 2 == 0 else k - step) % chips) for k in range(chips)]
-        return lax.ppermute(value, "y", ends)
-
-    met = [blocks[0], hop(blocks[3], -1), hop(blocks[1], 2), hop(blocks[2], -3)]
-    met += [hop(block, 1) for block in met]
-    met += [pass_on(block, "core", 1) for block in met]
-    return [jnp.concatenate([block[k] for block in met], axis=0) for k in range(2)]
+def after(value, other):
+    one = other[(0,) * other.ndim]
+    return value + (one != one).astype(value.dtype)
 
 
 def to_chips(slots):
@@ -113,32 +98,18 @@
     return jnp.concatenate(parts, axis=1)
 
 
-def found_along_x(value):
-    half = value.shape[0] // 2
-    left = pass_on(value, "x", 1)
-    right = pass_on(value, "x", -1)
-    top = pass_on(left[:half], "x", 1)
-    bottom = pass_on(right[half:], "x", -1)
-    return value, right, top, bottom, left
-
-
-def own_rows(right, left, near, own):
-    half = own.shape[0] // 2
-    from_left = pass_on(right, "x", 1)
-    from_right = pass_on(left, "x", -1)
-    top = pass_on(b16(f32(near[0]) + f32(from_left[:half])), "x", 1)
-    bottom = pass_on(b16(f32(near[1]) + f32(from_right[:half])), "x", -1)
-    first = f32(own[:half]) + f32(from_right[half:]) + f32(top)
-    second = f32(own[half:]) + f32(from_left[half:]) + f32(bottom)
-    summed = b16(jnp.concatenate([first, second], axis=0))
-    parts = exchange(summed.reshape(lax.axis_size("z"), -1, COLS), "z")
+def own_rows(terms):
+    size_z, size_x, rows, columns = terms.shape
+    flat = terms.reshape(size_z * size_x * rows, columns)
+    half = lax.psum_scatter(flat, "z", scatter_dimension=0, tiled=True)
+    parts = exchange(half.reshape(size_x, rows, columns), "x")
     return in_place(jnp.sum(f32(parts), axis=0))
 
 
 def all_rows(value):
-    size = lax.axis_size("z")
-    wide = exchange(jnp.broadcast_to(value[None], (size,) + value.shape), "z")
-    return found_along_x(wide.reshape(-1, COLS))
+    size = lax.axis_size("x")
+    wide = exchange(jnp.broadcast_to(value[None], (size,) + value.shape), "x")
+    return lax.all_gather(wide, "z", axis=0)
 
 
 def dot(a, b, dims=((1,), (0,))):
@@ -149,20 +120,12 @@
     return lax.broadcasted_iota(jnp.int32, shape, 1)
 
 
-def start_of(me, offset, wide):
-    return pl.multiple_of(lax.rem(me + offset, 4) * wide, wide)
-
-
-def in_row_order(me, pieces, wn, columns):
-    own, right, top, bottom, left = pieces
-    wide = own.shape[0]
-    half = wide // 2
-    wn[pl.ds(start_of(me, 0, wide), wide), :] = own[:, columns]
-    wn[pl.ds(start_of(me, 1, wide), wide), :] = right[:, columns]
-    far = start_of(me, 2, wide)
-    wn[pl.ds(far, half), :] = top[:, columns]
-    wn[pl.ds(pl.multiple_of(far + half, half), half), :] = bottom[:, columns]
-    wn[pl.ds(start_of(me, 3, wide), wide), :] = left[:, columns]
+def in_row_order(w, wn):
+    size_z, size_x, rows, columns = w.shape
+    wide = size_z * rows
+    for k in range(size_x):
+        wn[k * wide : (k + 1) * wide, :] = w[:, k].reshape(wide, columns)
+    return wide
 
 
 def back_terms(gate, up, down_back):
@@ -175,14 +138,13 @@
     )
 
 
-def terms_body(
-    me, taken, scaled, own, right, top, bottom, left,
-    to_right, to_left, near, mine, wn, pre, dn, g_in, g_sc,
-):
-    in_row_order(me[0], (own, right, top, bottom, left), wn, slice(0, COLS))
-    count = taken.shape[0]
-    pre[...] = dot(taken[...], wn[:, : LEAD + 128]) * IN_SCALE
-    dn[...] = dot(scaled[...], wn[:, LEAD:]) * OUT_SCALE
+def terms_body(own_in, other_in, own_sc, other_sc, w, out, wn, pre, dn, g_in, g_sc):
+    wide = in_row_order(w, wn)
+    half = own_in.shape[0]
+    count = 2 * half
+    for at, rows_in, rows_sc in ((0, own_in, own_sc), (half, other_in, other_sc)):
+        pre[at : at + half, :] = dot(rows_in[...], wn[:, : LEAD + 128]) * IN_SCALE
+        dn[at : at + half, :] = dot(rows_sc[...], wn[:, LEAD:]) * OUT_SCALE
 
     def chunk(i, carry):
         at = pl.ds(pl.multiple_of(i * 64, 64), 64)
@@ -203,46 +165,27 @@
 
     lax.fori_loop(0, count // 64, chunk, 0)
     over_rows = ((0,), (0,))
-    wide = own.shape[0]
-    half = wide // 2
-    for k in range(4):
-        cols = pl.ds(start_of(me[0], k, wide), wide)
-        a = dot(taken[:, cols], g_in[...], over_rows) * IN_SCALE
-        b = dot(scaled[:, cols], g_sc[...], over_rows) * OUT_SCALE
+    size_z, size_x, rows, _ = w.shape
+    for k in range(size_x):
+        cols = slice(k * wide, (k + 1) * wide)
+        a = dot(own_in[:, cols], g_in[:half, :], over_rows)
+        a = (a + dot(other_in[:, cols], g_in[half:, :], over_rows)) * IN_SCALE
+        b = dot(own_sc[:, cols], g_sc[:half, :], over_rows)
+        b = (b + dot(other_sc[:, cols], g_sc[half:, :], over_rows)) * OUT_SCALE
         parts = (
             (slice(0, LEAD), b16(a[:, :LEAD])),
             (slice(LEAD, LEAD + 128), b16(a[:, LEAD:] + b[:, :128])),
             (slice(LEAD + 128, COLS), b16(b[:, 128:])),
         )
         for at, value in parts:
-            if k == 0:
-                mine[:, at] = value
-            elif k == 1:
-                near[0, :, at] = value[:half]
-                to_right[half:, at] = value[half:]
-            elif k == 2:
-                to_right[:half, at] = value[:half]
-                to_left[:half, at] = value[half:]
-            else:
-                to_left[half:, at] = value[:half]
-                near[1, :, at] = value[half:]
-
-
-def step_terms(taken, scaled, pieces):
-    me = lax.axis_index("x").astype(jnp.int32).reshape(1)
-    count = taken.shape[0]
-    wide = pieces[0].shape[0]
-    chunk = jax.ShapeDtypeStruct((wide, COLS), jnp.bfloat16)
+            out[:, k, :, at] = value.reshape(size_z, rows, value.shape[1])
+
+
+def step_terms(own_in, other_in, own_sc, other_sc, w):
+    count = 2 * own_in.shape[0]
     return pl.pallas_call(
         terms_body,
-        out_shape=(
-            chunk,
-            chunk,
-            jax.ShapeDtypeStruct((2, wide // 2, COLS), jnp.bfloat16),
-            chunk,
-        ),
-        in_specs=[pl.BlockSpec(memory_space=pltpu.SMEM)]
-        + [pl.BlockSpec(memory_space=pltpu.VMEM)] * 7,
+        out_shape=jax.ShapeDtypeStruct(w.shape, jnp.bfloat16),
         scratch_shapes=[
             pltpu.VMEM((D, COLS), jnp.bfloat16),
             pltpu.VMEM((count, LEAD + 128), jnp.float32),
@@ -252,11 +195,11 @@
         ],
         interpret=TEST,
         name="step_terms",
-    )(me, taken, scaled, *pieces)
-
-
-def serve_body(me, taken, own, right, top, bottom, left, out, wn, pre, act):
-    in_row_order(me[0], (own, right, top, bottom, left), wn, slice(0, COLS))
+    )(own_in, other_in, own_sc, other_sc, w)
+
+
+def serve_body(taken, w, out, wn, pre, act):
+    wide = in_row_order(w, wn)
     pre[...] = dot(taken[...], wn[:, : LEAD + 128]) * IN_SCALE
 
     def chunk(i, carry):
@@ -271,20 +214,16 @@
         return carry
 
     lax.fori_loop(0, taken.shape[0] // 64, chunk, 0)
-    wide = own.shape[0]
-    for k in range(4):
+    for k in range(w.shape[1]):
         cols = slice(k * wide, (k + 1) * wide)
         total = dot(act[...], wn[cols, LEAD:], ((1,), (1,)))
         out[:, cols] = b16(total * OUT_SCALE)
 
 
-def serve(taken, pieces):
-    me = lax.axis_index("x").astype(jnp.int32).reshape(1)
+def serve(taken, w):
     return pl.pallas_call(
         serve_body,
         out_shape=jax.ShapeDtypeStruct(taken.shape, jnp.bfloat16),
-        in_specs=[pl.BlockSpec(memory_space=pltpu.SMEM)]
-        + [pl.BlockSpec(memory_space=pltpu.VMEM)] * 6,
         scratch_shapes=[
             pltpu.VMEM((D, COLS), jnp.bfloat16),
             pltpu.VMEM((taken.shape[0], LEAD + 128), jnp.float32),
@@ -292,7 +231,7 @@
         ],
         interpret=TEST,
         name="serve",
-    )(me, taken, *pieces)
+    )(taken, w)
 
 
 def migrated(stacked, owner_plan):
@@ -322,9 +261,13 @@
     old_weights = master_weights[0]
     step_targets = slot_of(step_routes)
     scaled = b16(f32(step_cotangent) * step_gates)
-    old_pieces = all_rows(arranged(b16(old_weights)))
-    taken, taken_scaled = to_pairs(step_routes, step_targets, step_inputs, scaled)
-    gradient = own_rows(*step_terms(taken, taken_scaled, old_pieces))
+    parts = lax.all_gather(arranged(b16(old_weights)), "x", axis=0)
+    weights = lax.all_gather(parts, "z", axis=0)
+    own_in = to_chips(to_slots(step_targets, step_inputs))
+    own_sc = to_chips(to_slots(step_targets, scaled))
+    other_in = pass_on(own_in, "core", 1)
+    other_sc = pass_on(own_sc, "core", 1)
+    gradient = own_rows(step_terms(own_in, other_in, own_sc, other_sc, weights))
     first_new = beta_one * first_moment[0] + (1.0 - beta_one) * gradient
     second_new = beta_two * second_moment[0] + (1.0 - beta_two) * gradient * gradient
     first_hat = first_new / (1.0 - beta_one**adam_step)
@@ -337,7 +280,8 @@
     moved = f32(migrated(stacked, owner_plan)).reshape((3, 1) + old_weights.shape)
 
     next_targets = slot_of(next_routes)
-    own_next = to_chips(to_slots(next_targets, next_inputs))
+    next_slots = to_slots(after(next_targets, other_in), next_inputs)
+    own_next = to_chips(next_slots)
     other_next = pass_on(own_next, "core", 1)
     met = serve(other_next, pieces)
     met = pass_on(met, "core", 1)

time: 397 us -> 352 us (0.89)
  starting transfers between devices: 129 us -> 45.7 us
  blocking collectives: 30.3 us -> 69.2 us
  local copies, waits for them, and re-layouts: 32.9 us -> 7.31 us
  waiting for transfers between devices: 158 us -> 176 us
  between operations: 1.32 us -> 15.4 us
  other arithmetic: 9.39 us -> 5.24 us
    ppermute x22 -> x4, starting transfers between devices: 79.5 us -> 20.3 us  [pass_on(): lax.ppermute(value, axis, [(k, (k + by) % size) for k in range(size)])]
    reduce_scatter x0 -> x1, waiting for transfers between devices: none -> 54.3 us  [own_rows(): half = lax.psum_scatter(flat, 'z', scatter_dimension=0, tiled=True)]
    ppermute x22 -> x4, waiting for transfers between devices: 56.5 us -> 5.22 us  [pass_on(): lax.ppermute(value, axis, [(k, (k + by) % size) for k in range(size)])]
    all_to_all x1 -> x3, blocking collectives: 30.3 us -> 57.6 us  [exchange(): return lax.all_to_all(value, axis, split_axis=0, concat_axis=0, tiled=True)]
    unnamed x55 -> x30, local copies, waits for them, and re-layouts: 24.1 us -> 0.07 us
    ppermute x7 -> x0, starting transfers between devices: 20.5 us -> none  [hop(): return lax.ppermute(value, 'y', ends)]
    all_to_all x6 -> x5, waiting for transfers between devices: 99 us -> 113 us  [exchange(): return lax.all_to_all(value, axis, split_axis=0, concat_axis=0, tiled=True)]
    all_gather x0 -> x1, blocking collectives: none -> 11.7 us  [whole_step(): parts = lax.all_gather(arranged(b16(old_weights)), 'x', axis=0)]
  transfers between devices with their start and end apart: 35 -> 12, of which waited for: 17 -> 9; matrix products, arithmetic and copies ran while one was open for 8% -> 3% of each run, Pallas kernels for 2% -> 2%
where the time goes in v5:
time: 352 us; the launch traced here: 351 us
  waiting for transfers between devices  176 us (50%)
  blocking collectives  69.2 us (20%)
  starting transfers between devices  45.7 us (13%)
  Pallas kernels  29.6 us (8%)
  between operations  15.4 us (4%)
  local copies, waits for them, and re-layouts  7.31 us (2%)
  other arithmetic  5.24 us (1%)
    all_to_all x5, waiting for transfers between devices, exchange(): return lax.all_to_all(value, axis, split_axis=0, concat_axis=0, tiled=True)  113 us
    all_to_all x3, blocking collectives, exchange(): return lax.all_to_all(value, axis, split_axis=0, concat_axis=0, tiled=True)  57.6 us
    reduce_scatter x1, waiting for transfers between devices, own_rows(): half = lax.psum_scatter(flat, 'z', scatter_dimension=0, tiled=True)  54.3 us
    all_to_all x5, starting transfers between devices, exchange(): return lax.all_to_all(value, axis, split_axis=0, concat_axis=0, tiled=True)  25.3 us
    ppermute x4, starting transfers between devices, pass_on(): lax.ppermute(value, axis, [(k, (k + by) % size) for k in range(size)])  20.3 us
    pallas_call x1, Pallas kernels, step_terms(): pl.pallas_call(terms_body, out_shape=jax.ShapeDtypeStruct(w.shape, jnp.bf...  15.6 us
    pallas_call x2, Pallas kernels, serve(): pl.pallas_call(serve_body, out_shape=jax.ShapeDtypeStruct(taken.shape, jn...  14 us
    all_gather x1, blocking collectives, whole_step(): parts = lax.all_gather(arranged(b16(old_weights)), 'x', axis=0)  11.7 us
  transfers between devices with their start and end apart: 12, of which 9 were waited for; matrix products, arithmetic and copies ran while one was open for 3% of the time, Pallas kernels for 2%

profile of v5, /device:TPU:1, one launch (start us, length us, event | category | flops | bytes accessed | tf_op | source)
XLA Modules:
  0.0 350.9 jit_solution(4963026265839020118)
XLA Ops:
  7.2 1.0 bitcast_convert_fusion
  8.2 0.1 fusion.31
  8.4 0.1 concatenate.12
  8.5 11.7 %all-gather = bf16[256,896]{1,0:T(8,128)(2,1)} all-gather(bf16[64,896]{1,0:T(8,128)(2,1)S(1)} %concatenate.12), channel_id=2, replica_groups=mesh['x'=4,'z'=8,'y'=8,'core'=2] {'x'}, dimensions={0}, use_global_device_ids=true | all-gather | bytes 573440 | tf_op jit(solution)/shard_map/all_gather | solution.py:264
  20.2 0.1 fusion.2
  20.4 0.3 convolution_convert_fusion.2
  20.7 1.2 broadcast_in_dim.52
  22.0 7.8 %all-to-all-start = ((bf16[8,40,2048]{2,1,0:T(8,128)(2,1)}), bf16[8,40,2048]{2,1,0:T(8,128)(2,1)S(1)}, u32[]{:S(2)}, u32[]{:S(2)}) async-start(bf16[8,40,2048]{2,1,0:T(8,128)(2,1)} %bitcast.5), calls=%async_computation | async-start | bytes 2621440 | tf_op jit(solution)/shard_map/all_to_all | solution.py:42
  29.8 0.4 convolution_convert_fusion
  30.2 31.3 %all-to-all-done = bf16[8,40,2048]{2,1,0:T(8,128)(2,1)S(1)} async-done(((bf16[8,40,2048]{2,1,0:T(8,128)(2,1)}), bf16[8,40,2048]{2,1,0:T(8,128)(2,1)S(1)}, u32[]{:S(2)}, u32[]{:S(2)}) %all-to-all-start) | async-done | bytes 1310752 | tf_op jit(solution)/shard_map/all_to_all | solution.py:42
  61.6 1.4 broadcast_in_dim.54
  62.9 3.6 %all-to-all-start.2 = ((bf16[8,40,2048]{2,1,0:T(8,128)(2,1)}), bf16[8,40,2048]{2,1,0:T(8,128)(2,1)S(1)}, u32[]{:S(2)}, u32[]{:S(2)}) async-start(bf16[8,40,2048]{2,1,0:T(8,128)(2,1)} %bitcast.74), calls=%async_computation.2 | async-start | bytes 2621440 | tf_op jit(solution)/shard_map/all_to_all | solution.py:42
  66.6 5.4 %collective-permute-start = (bf16[320,2048]{1,0:T(8,128)(2,1)S(1)}, bf16[320,2048]{1,0:T(8,128)(2,1)}, u32[]{:S(2)}, u32[]{:S(2)}) collective-permute-start(bf16[320,2048]{1,0:T(8,128)(2,1)S(1)} %bitcast.69), channel_id=1, source_target_pairs={{0,1},{1,0},{2,3},{3,2},{4,5},{5,4},{6,7},{7,6},{8,9},{9,8},{10,11... | collective-permute-start | bytes 3932168 | tf_op jit(solution)/shard_map/ppermute | solution.py:38
  72.0 27.0 %all-to-all-done.2 = bf16[8,40,2048]{2,1,0:T(8,128)(2,1)S(1)} async-done(((bf16[8,40,2048]{2,1,0:T(8,128)(2,1)}), bf16[8,40,2048]{2,1,0:T(8,128)(2,1)S(1)}, u32[]{:S(2)}, u32[]{:S(2)}) %all-to-all-start.2) | async-done | bytes 1310752 | tf_op jit(solution)/shard_map/all_to_all | solution.py:42
  99.0 4.6 %collective-permute-start.1 = (bf16[320,2048]{1,0:T(8,128)(2,1)S(1)}, bf16[320,2048]{1,0:T(8,128)(2,1)}, u32[]{:S(2)}, u32[]{:S(2)}) collective-permute-start(bf16[320,2048]{1,0:T(8,128)(2,1)S(1)} %bitcast.71), channel_id=1, source_target_pairs={{0,1},{1,0},{2,3},{3,2},{4,5},{5,4},{6,7},{7,6},{8,9},{9,8},{10,11... | collective-permute-start | bytes 3932168 | tf_op jit(solution)/shard_map/ppermute | solution.py:38
  103.7 2.8 collective-permute-done.1.other_sc
  106.4 15.6 %step_terms.1 = bf16[8,4,64,896]{3,2,1,0:T(8,128)(2,1)} custom-call(bf16[320,2048]{1,0:T(8,128)(2,1)} %bitcast.70, bf16[320,2048]{1,0:T(8,128)(2,1)} %collective-permute-done.other_in, bf16[320,2048]{1,0:T(8,128)(2,1)} %bitcast.72, bf16[320,2048]{1,0:T(8,128)(2,1)} %collective-permute-done.1.other_sc, bf16[8,4,64,896]{3,2,1,0:T(8,128)(2,1)} %bitcast.78), custom_call_target="tpu_custom_call" | custom-call | tf_op jit(solution)/shard_map/step_terms/pallas_call | solution.py:186
  122.1 54.3 %reduce-scatter.2.cloned.1.call-done = bf16[256,896]{1,0:T(8,128)(2,1)} async-done(((bf16[2048,896]{1,0:T(8,128)(2,1)}), bf16[256,896]{1,0:T(8,128)(2,1)}) %reduce-scatter.2.cloned.1.call-update) | async-done | bytes 458768 | tf_op jit(solution)/shard_map/reduce_scatter | solution.py:104
  176.5 11.7 %all_to_all.40 = bf16[4,64,896]{2,1,0:T(8,128)(2,1)S(1)} all-to-all(bf16[4,64,896]{2,1,0:T(8,128)(2,1)} %bitcast.83), channel_id=1, replica_groups=mesh['x'=4,'z'=8,'y'=8,'core'=2] {'x'}, dimensions={0} | all-to-all | bytes 917504 | tf_op jit(solution)/shard_map/all_to_all | solution.py:42
  188.3 0.1 concatenate.13
  188.5 0.2 fusion.14
  188.9 0.1 concatenate.14
  189.0 9.7 %all_to_all.41 = bf16[4,64,896]{2,1,0:T(8,128)(2,1)} all-to-all(bf16[4,64,896]{2,1,0:T(8,128)(2,1)S(1)} %broadcast_in_dim.55), channel_id=1, replica_groups=mesh['x'=4,'z'=8,'y'=8,'core'=2] {'x'}, dimensions={0} | all-to-all | bytes 917504 | tf_op jit(solution)/shard_map/all_to_all | solution.py:42
  198.8 0.1 fusion.1
  198.9 1.2 slice.111
  201.4 0.3 convolution_convert_fusion.1
  201.8 0.1 broadcast_in_dim.53
  201.9 36.2 %all_to_all.42 = bf16[8,40,2048]{2,1,0:T(8,128)(2,1)S(1)} all-to-all(bf16[8,40,2048]{2,1,0:T(8,128)(2,1)S(1)} %bitcast.75), channel_id=1, replica_groups=mesh['x'=4,'z'=8,'y'=8,'core'=2] {'y'}, dimensions={0} | all-to-all | bytes 2621440 | tf_op jit(solution)/shard_map/all_to_all | solution.py:42
  238.1 7.4 %collective-permute-start.2 = (bf16[320,2048]{1,0:T(8,128)(2,1)S(1)}, bf16[320,2048]{1,0:T(8,128)(2,1)S(1)}, u32[]{:S(2)}, u32[]{:S(2)}) collective-permute-start(bf16[320,2048]{1,0:T(8,128)(2,1)S(1)} %bitcast.76), channel_id=1, source_target_pairs={{0,1},{1,0},{2,3},{3,2},{4,5},{5,4},{6,7},{7,6},{8,9},{9,8},{10,11... | collective-permute-start | bytes 3932168 | tf_op jit(solution)/shard_map/ppermute | solution.py:38
  245.6 2.5 collective-permute-done.2.taken
  248.0 3.0 all-gather.8.cloned.1.call-done
  251.0 7.0 %serve.3 = bf16[320,2048]{1,0:T(8,128)(2,1)} custom-call(bf16[320,2048]{1,0:T(8,128)(2,1)} %copy-done.4, bf16[8,4,64,896]{3,2,1,0:T(8,128)(2,1)} %bitcast.67), custom_call_target="tpu_custom_call" | custom-call | tf_op jit(solution)/shard_map/serve/pallas_call | solution.py:224
  258.0 2.9 collective-permute-start.3
  260.9 0.9 reshape.132
  261.8 6.9 %all-to-all-start.6 = ((bf16[16,12,864]{2,1,0:T(8,128)(2,1)}), bf16[16,12,864]{2,1,0:T(8,128)(2,1)S(1)}, u32[]{:S(2)}, u32[]{:S(2)}) async-start(bf16[16,12,864]{2,1,0:T(8,128)(2,1)} %reshape.132), calls=%async_computation.7 | async-start | bytes 917504 | tf_op jit(solution)/shard_map/all_to_all | solution.py:42
  268.7 0.1 select_reduce_fusion
  268.8 15.7 %all-to-all-done.6 = bf16[16,12,864]{2,1,0:T(8,128)(2,1)S(1)} async-done(((bf16[16,12,864]{2,1,0:T(8,128)(2,1)}), bf16[16,12,864]{2,1,0:T(8,128)(2,1)S(1)}, u32[]{:S(2)}, u32[]{:S(2)}) %all-to-all-start.6) | async-done | bytes 331808 | tf_op jit(solution)/shard_map/all_to_all | solution.py:42
  284.5 0.6 gather_fusion
  285.1 0.9 broadcast_select_fusion
  286.0 3.5 all-to-all-start.7
  289.5 7.0 %serve.2 = bf16[320,2048]{1,0:T(8,128)(2,1)} custom-call(bf16[320,2048]{1,0:T(8,128)(2,1)} %bitcast.77, bf16[8,4,64,896]{3,2,1,0:T(8,128)(2,1)} %bitcast.68), custom_call_target="tpu_custom_call" | custom-call | tf_op jit(solution)/shard_map/serve/pallas_call | solution.py:224
  296.5 2.9 add_convert_fusion
  299.3 5.4 %all-to-all-done.7 = bf16[16,12,864]{2,1,0:T(8,128)(2,1)S(1)} async-done(((bf16[16,12,864]{2,1,0:T(8,128)(2,1)}), bf16[16,12,864]{2,1,0:T(8,128)(2,1)S(1)}, u32[]{:S(2)}, u32[]{:S(2)}) %all-to-all-start.7) | async-done | bytes 331808 | tf_op jit(solution)/shard_map/all_to_all | solution.py:42
  304.8 3.6 %all-to-all-start.5 = ((bf16[8,40,2048]{2,1,0:T(8,128)(2,1)}), bf16[8,40,2048]{2,1,0:T(8,128)(2,1)S(1)}, u32[]{:S(2)}, u32[]{:S(2)}) async-start(bf16[8,40,2048]{2,1,0:T(8,128)(2,1)} %bitcast.23), calls=%async_computation.6 | async-start | bytes 2621440 | tf_op jit(solution)/shard_map/all_to_all | solution.py:42
  308.4 0.1 reshape.134
  308.5 0.9 slice_bitcast_fusion
  309.4 33.7 %all-to-all-done.5 = bf16[8,40,2048]{2,1,0:T(8,128)(2,1)S(1)} async-done(((bf16[8,40,2048]{2,1,0:T(8,128)(2,1)}), bf16[8,40,2048]{2,1,0:T(8,128)(2,1)S(1)}, u32[]{:S(2)}, u32[]{:S(2)}) %all-to-all-start.5) | async-done | bytes 1310752 | tf_op jit(solution)/shard_map/all_to_all | solution.py:42
  343.1 1.3 fusion
  (57 shorter events, 0.8 us)
Async XLA Ops:
  7.2 13.2 %copy-start = (bf16[128,2048]{1,0:T(8,128)(2,1)S(1)}, bf16[128,2048]{1,0:T(8,128)(2,1)}, u32[]{:S(2)}) copy-start(bf16[128,2048]{1,0:T(8,128)(2,1)} %param.11) | copy-start | bytes 1572868
  7.2 13.0 %copy-start.13 = (s32[128,1]{0,1:T(1,128)S(1)}, s32[128,1]{0,1:T(1,128)}, u32[]{:S(2)}) copy-start(s32[128,1]{0,1:T(1,128)} %param.13) | copy-start | bytes 1540
  7.2 99.2 %all-gather.6.cloned.1.call-start = ((), (), s32[]{:S(2)}) async-start(), calls=%async_computation.10 | async-start | bytes 4128768 | tf_op jit(solution)/shard_map/all_gather | solution.py:265
  22.0 7.8 %copy-start.7 = (bf16[128,2048]{1,0:T(8,128)(2,1)S(1)}, bf16[128,2048]{1,0:T(8,128)(2,1)}, u32[]{:S(2)}) copy-start(bf16[128,2048]{1,0:T(8,128)(2,1)} %param.12) | copy-start | bytes 1572868
  22.0 7.8 %copy-start.10 = (f32[128,1]{0,1:T(1,128)S(1)}, f32[128,1]{0,1:T(1,128)}, u32[]{:S(2)}) copy-start(f32[128,1]{0,1:T(1,128)} %param.14) | copy-start | bytes 1540
  22.0 39.6 %all-to-all-start = ((bf16[8,40,2048]{2,1,0:T(8,128)(2,1)}), bf16[8,40,2048]{2,1,0:T(8,128)(2,1)S(1)}, u32[]{:S(2)}, u32[]{:S(2)}) async-start(bf16[8,40,2048]{2,1,0:T(8,128)(2,1)} %bitcast.5), calls=%async_computation | async-start | bytes 2621440 | tf_op jit(solution)/shard_map/all_to_all | solution.py:42
  61.6 5.0 %copy-start.1 = (bf16[8,40,2048]{2,1,0:T(8,128)(2,1)}, bf16[8,40,2048]{2,1,0:T(8,128)(2,1)S(1)}, u32[]{:S(2)}) copy-start(bf16[8,40,2048]{2,1,0:T(8,128)(2,1)S(1)} %all-to-all-done) | copy-start | bytes 3932164
  62.9 36.1 %all-to-all-start.2 = ((bf16[8,40,2048]{2,1,0:T(8,128)(2,1)}), bf16[8,40,2048]{2,1,0:T(8,128)(2,1)S(1)}, u32[]{:S(2)}, u32[]{:S(2)}) async-start(bf16[8,40,2048]{2,1,0:T(8,128)(2,1)} %bitcast.74), calls=%async_computation.2 | async-start | bytes 2621440 | tf_op jit(solution)/shard_map/all_to_all | solution.py:42
  66.5 110.0 %reduce-scatter.2.cloned.1.call-start = ((), (), s32[]{:S(2)}) async-start(), calls=%async_computation.9 | async-start | bytes 4128768 | tf_op jit(solution)/shard_map/reduce_scatter | solution.py:104
  66.6 37.1 %collective-permute-start = (bf16[320,2048]{1,0:T(8,128)(2,1)S(1)}, bf16[320,2048]{1,0:T(8,128)(2,1)}, u32[]{:S(2)}, u32[]{:S(2)}) collective-permute-start(bf16[320,2048]{1,0:T(8,128)(2,1)S(1)} %bitcast.69), channel_id=1, source_target_pairs={{0,1},{1,0},{2,3},{3,2},{4,5},{5,4},{6,7},{7,6},{8,9},{9,8},{10,11... | collective-permute-start | bytes 3932168 | tf_op jit(solution)/shard_map/ppermute | solution.py:38
  99.0 7.4 %copy-start.2 = (bf16[8,40,2048]{2,1,0:T(8,128)(2,1)}, bf16[8,40,2048]{2,1,0:T(8,128)(2,1)S(1)}, u32[]{:S(2)}) copy-start(bf16[8,40,2048]{2,1,0:T(8,128)(2,1)S(1)} %all-to-all-done.2) | copy-start | bytes 3932164
  99.0 7.4 %collective-permute-start.1 = (bf16[320,2048]{1,0:T(8,128)(2,1)S(1)}, bf16[320,2048]{1,0:T(8,128)(2,1)}, u32[]{:S(2)}, u32[]{:S(2)}) collective-permute-start(bf16[320,2048]{1,0:T(8,128)(2,1)S(1)} %bitcast.71), channel_id=1, source_target_pairs={{0,1},{1,0},{2,3},{3,2},{4,5},{5,4},{6,7},{7,6},{8,9},{9,8},{10,11... | collective-permute-start | bytes 3932168 | tf_op jit(solution)/shard_map/ppermute | solution.py:38
  122.1 128.9 %all-gather.8.cloned.1.call-start = ((), (), s32[]{:S(2)}) async-start(), calls=%async_computation.11 | async-start | bytes 4128768 | tf_op jit(solution)/shard_map/all_gather | solution.py:112
  176.5 12.0 %copy-start.5 = (f32[1,64,864]{2,1,0:T(8,128)S(1)}, f32[1,64,864]{2,1,0:T(8,128)}, u32[]{:S(2)}) copy-start(f32[1,64,864]{2,1,0:T(8,128)} %param.18) | copy-start | bytes 663556
  176.5 12.0 %copy-start.8 = (f32[1,64,864]{2,1,0:T(8,128)S(1)}, f32[1,64,864]{2,1,0:T(8,128)}, u32[]{:S(2)}) copy-start(f32[1,64,864]{2,1,0:T(8,128)} %param.19) | copy-start | bytes 663556
  176.5 12.0 %copy-start.9 = (f32[1,64,864]{2,1,0:T(8,128)S(1)}, f32[1,64,864]{2,1,0:T(8,128)}, u32[]{:S(2)}) copy-start(f32[1,64,864]{2,1,0:T(8,128)} %param.20) | copy-start | bytes 663556
  188.7 10.1 %copy-start.12 = (s32[128,1]{0,1:T(1,128)S(1)}, s32[128,1]{0,1:T(1,128)}, u32[]{:S(2)}) copy-start(s32[128,1]{0,1:T(1,128)} %param.16) | copy-start | bytes 1540
  188.7 12.7 %copy-start.6 = (bf16[128,2048]{1,0:T(8,128)(2,1)S(1)}, bf16[128,2048]{1,0:T(8,128)(2,1)}, u32[]{:S(2)}) copy-start(bf16[128,2048]{1,0:T(8,128)(2,1)} %param.15) | copy-start | bytes 1572868
  238.1 19.9 %copy-start.3 = (bf16[8,40,2048]{2,1,0:T(8,128)(2,1)}, bf16[8,40,2048]{2,1,0:T(8,128)(2,1)S(1)}, u32[]{:S(2)}) copy-start(bf16[8,40,2048]{2,1,0:T(8,128)(2,1)S(1)} %all_to_all.42) | copy-start | bytes 3932164
  238.1 9.9 %collective-permute-start.2 = (bf16[320,2048]{1,0:T(8,128)(2,1)S(1)}, bf16[320,2048]{1,0:T(8,128)(2,1)S(1)}, u32[]{:S(2)}, u32[]{:S(2)}) collective-permute-start(bf16[320,2048]{1,0:T(8,128)(2,1)S(1)} %bitcast.76), channel_id=1, source_target_pairs={{0,1},{1,0},{2,3},{3,2},{4,5},{5,4},{6,7},{7,6},{8,9},{9,8},{10,11... | collective-permute-start | bytes 3932168 | tf_op jit(solution)/shard_map/ppermute | solution.py:38
  248.0 3.0 copy-start.4
  258.0 10.6 %copy-start.14 = (s32[16]{0:T(128)S(1)}, s32[16]{0:T(128)}, u32[]{:S(2)}) copy-start(s32[16]{0:T(128)} %param.21) | copy-start | bytes 196
  258.0 38.5 %collective-permute-start.3 = (bf16[320,2048]{1,0:T(8,128)(2,1)}, bf16[320,2048]{1,0:T(8,128)(2,1)S(1)}, u32[]{:S(2)}, u32[]{:S(2)}) collective-permute-start(bf16[320,2048]{1,0:T(8,128)(2,1)} %serve.3), channel_id=1, source_target_pairs={{0,1},{1,0},{2,3},{3,2},{4,5},{5,4},{6,7},{7,6},{8,9},{9,8},{10,11... | collective-permute-start | bytes 3932168 | tf_op jit(solution)/shard_map/ppermute | solution.py:38
  261.8 22.7 %all-to-all-start.6 = ((bf16[16,12,864]{2,1,0:T(8,128)(2,1)}), bf16[16,12,864]{2,1,0:T(8,128)(2,1)S(1)}, u32[]{:S(2)}, u32[]{:S(2)}) async-start(bf16[16,12,864]{2,1,0:T(8,128)(2,1)} %reshape.132), calls=%async_computation.7 | async-start | bytes 917504 | tf_op jit(solution)/shard_map/all_to_all | solution.py:42
  286.0 18.7 %all-to-all-start.7 = ((bf16[16,12,864]{2,1,0:T(8,128)(2,1)}), bf16[16,12,864]{2,1,0:T(8,128)(2,1)S(1)}, u32[]{:S(2)}, u32[]{:S(2)}) async-start(bf16[16,12,864]{2,1,0:T(8,128)(2,1)} %broadcast_select_fusion), calls=%async_computation.8 | async-start | bytes 917504 | tf_op jit(solution)/shard_map/all_to_all | solution.py:42
  304.8 38.3 %all-to-all-start.5 = ((bf16[8,40,2048]{2,1,0:T(8,128)(2,1)}), bf16[8,40,2048]{2,1,0:T(8,128)(2,1)S(1)}, u32[]{:S(2)}, u32[]{:S(2)}) async-start(bf16[8,40,2048]{2,1,0:T(8,128)(2,1)} %bitcast.23), calls=%async_computation.6 | async-start | bytes 2621440 | tf_op jit(solution)/shard_map/all_to_all | solution.py:42
  308.3 34.7 %copy-start.11 = (f32[128,1]{0,1:T(1,128)S(1)}, f32[128,1]{0,1:T(1,128)}, u32[]{:S(2)}) copy-start(f32[128,1]{0,1:T(1,128)} %param.17) | copy-start | bytes 1540
Sparse Core Ops, SparseCore 0:
  20.3 60.5 all-gather.5
  122.2 54.2 reduce-scatter.1
  198.9 52.0 all-gather.7

commit v6 on v5

--- a/solution.py
+++ b/solution.py
@@ -186,6 +186,8 @@
     return pl.pallas_call(
         terms_body,
         out_shape=jax.ShapeDtypeStruct(w.shape, jnp.bfloat16),
+        in_specs=[pl.BlockSpec(memory_space=pltpu.VMEM), pl.BlockSpec()] * 2 + [pl.BlockSpec()],
+        compiler_params=pltpu.CompilerParams(vmem_limit_bytes=36 * 2**20),
         scratch_shapes=[
             pltpu.VMEM((D, COLS), jnp.bfloat16),
             pltpu.VMEM((count, LEAD + 128), jnp.float32),
@@ -224,6 +226,9 @@
     return pl.pallas_call(
         serve_body,
         out_shape=jax.ShapeDtypeStruct(taken.shape, jnp.bfloat16),
+        in_specs=[pl.BlockSpec(memory_space=pltpu.VMEM)] * 2,
+        out_specs=pl.BlockSpec(memory_space=pltpu.VMEM),
+        compiler_params=pltpu.CompilerParams(vmem_limit_bytes=24 * 2**20),
         scratch_shapes=[
             pltpu.VMEM((D, COLS), jnp.bfloat16),
             pltpu.VMEM((taken.shape[0], LEAD + 128), jnp.float32),

time: 352 us -> 358 us (1.017)
  local copies, waits for them, and re-layouts: 7.31 us -> 23.2 us
  Pallas kernels: 29.6 us -> 18.4 us
    unnamed x30 -> x46, local copies, waits for them, and re-layouts: 0.07 us -> 13.3 us
    pallas_call x2, Pallas kernels: 14 us -> 6.92 us  [serve(): pl.pallas_call(serve_body, out_shape=jax.ShapeDtypeStruct(taken.shape, jn...]
    pallas_call x1, Pallas kernels: 15.6 us -> 11.5 us  [step_terms(): pl.pallas_call(terms_body, out_shape=jax.ShapeDtypeStruct(w.shape, jnp.bf...]
  transfers between devices with their start and end apart: 12 -> 12, of which waited for: 9 -> 9; matrix products, arithmetic and copies ran while one was open for 3% -> 4% of each run, Pallas kernels for 2% -> 1%
where the time goes in v6:
time: 358 us; the launch traced here: 357 us
  waiting for transfers between devices  174 us (49%)
  blocking collectives  69.2 us (19%)
  starting transfers between devices  46.3 us (13%)
  local copies, waits for them, and re-layouts  23.2 us (6%)
  Pallas kernels  18.4 us (5%)
  between operations  15.4 us (4%)
  other arithmetic  6.98 us (2%)
    all_to_all x5, waiting for transfers between devices, exchange(): return lax.all_to_all(value, axis, split_axis=0, concat_axis=0, tiled=True)  113 us
    all_to_all x3, blocking collectives, exchange(): return lax.all_to_all(value, axis, split_axis=0, concat_axis=0, tiled=True)  57.6 us
    reduce_scatter x1, waiting for transfers between devices, own_rows(): half = lax.psum_scatter(flat, 'z', scatter_dimension=0, tiled=True)  54.3 us
    all_to_all x5, starting transfers between devices, exchange(): return lax.all_to_all(value, axis, split_axis=0, concat_axis=0, tiled=True)  26 us
    ppermute x4, starting transfers between devices, pass_on(): lax.ppermute(value, axis, [(k, (k + by) % size) for k in range(size)])  20.2 us
    unnamed x46, local copies, waits for them, and re-layouts  13.3 us
    all_gather x1, blocking collectives, whole_step(): parts = lax.all_gather(arranged(b16(old_weights)), 'x', axis=0)  11.7 us
    pallas_call x1, Pallas kernels, step_terms(): pl.pallas_call(terms_body, out_shape=jax.ShapeDtypeStruct(w.shape, jnp.bf...  11.5 us
  transfers between devices with their start and end apart: 12, of which 9 were waited for; matrix products, arithmetic and copies ran while one was open for 4% of the time, Pallas kernels for 1%

profile of v6, /device:TPU:1, one launch (start us, length us, event | category | flops | bytes accessed | tf_op | source)
XLA Modules:
  0.0 356.8 jit_solution(4628340176668500277)
XLA Ops:
  7.2 1.0 bitcast_convert_fusion
  8.5 11.7 %all-gather = bf16[256,896]{1,0:T(8,128)(2,1)} all-gather(bf16[64,896]{1,0:T(8,128)(2,1)S(1)} %concatenate.12), channel_id=2, replica_groups=mesh['x'=4,'z'=8,'y'=8,'core'=2] {'x'}, dimensions={0}, use_global_device_ids=true | all-gather | bytes 573440 | tf_op jit(solution)/shard_map/all_gather | solution.py:269
  20.4 0.3 convolution_convert_fusion.2
  20.7 1.3 broadcast_in_dim.52
  22.0 7.8 %all-to-all-start = ((bf16[8,40,2048]{2,1,0:T(8,128)(2,1)}), bf16[8,40,2048]{2,1,0:T(8,128)(2,1)S(1)}, u32[]{:S(2)}, u32[]{:S(2)}) async-start(bf16[8,40,2048]{2,1,0:T(8,128)(2,1)} %bitcast.5), calls=%async_computation | async-start | bytes 2621440 | tf_op jit(solution)/shard_map/all_to_all | solution.py:42
  29.8 0.4 convolution_convert_fusion
  30.3 31.3 %all-to-all-done = bf16[8,40,2048]{2,1,0:T(8,128)(2,1)S(1)} async-done(((bf16[8,40,2048]{2,1,0:T(8,128)(2,1)}), bf16[8,40,2048]{2,1,0:T(8,128)(2,1)S(1)}, u32[]{:S(2)}, u32[]{:S(2)}) %all-to-all-start) | async-done | bytes 1310752 | tf_op jit(solution)/shard_map/all_to_all | solution.py:42
  61.6 1.3 broadcast_in_dim.54
  62.9 3.6 %all-to-all-start.2 = ((bf16[8,40,2048]{2,1,0:T(8,128)(2,1)}), bf16[8,40,2048]{2,1,0:T(8,128)(2,1)S(1)}, u32[]{:S(2)}, u32[]{:S(2)}) async-start(bf16[8,40,2048]{2,1,0:T(8,128)(2,1)} %bitcast.77), calls=%async_computation.2 | async-start | bytes 2621440 | tf_op jit(solution)/shard_map/all_to_all | solution.py:42
  66.5 5.4 %collective-permute-start = (bf16[320,2048]{1,0:T(8,128)(2,1)S(1)}, bf16[320,2048]{1,0:T(8,128)(2,1)}, u32[]{:S(2)}, u32[]{:S(2)}) collective-permute-start(bf16[320,2048]{1,0:T(8,128)(2,1)S(1)} %bitcast.69), channel_id=1, source_target_pairs={{0,1},{1,0},{2,3},{3,2},{4,5},{5,4},{6,7},{7,6},{8,9},{9,8},{10,11... | collective-permute-start | bytes 3932168 | tf_op jit(solution)/shard_map/ppermute | solution.py:38
  71.9 27.0 %all-to-all-done.2 = bf16[8,40,2048]{2,1,0:T(8,128)(2,1)S(1)} async-done(((bf16[8,40,2048]{2,1,0:T(8,128)(2,1)}), bf16[8,40,2048]{2,1,0:T(8,128)(2,1)S(1)}, u32[]{:S(2)}, u32[]{:S(2)}) %all-to-all-start.2) | async-done | bytes 1310752 | tf_op jit(solution)/shard_map/all_to_all | solution.py:42
  98.9 4.6 %collective-permute-start.1 = (bf16[320,2048]{1,0:T(8,128)(2,1)S(1)}, bf16[320,2048]{1,0:T(8,128)(2,1)S(1)}, u32[]{:S(2)}, u32[]{:S(2)}) collective-permute-start(bf16[320,2048]{1,0:T(8,128)(2,1)S(1)} %bitcast.71), channel_id=1, source_target_pairs={{0,1},{1,0},{2,3},{3,2},{4,5},{5,4},{6,7},{7,6},{8,9},{9,8},{10,11... | collective-permute-start | bytes 3932168 | tf_op jit(solution)/shard_map/ppermute | solution.py:38
  103.6 2.6 collective-permute-done.1.other_sc
  106.2 1.1 copy-done.5
  107.3 2.0 copy-done.4
  109.4 1.3 copy-done.6
  110.7 11.5 %step_terms.1 = bf16[8,4,64,896]{3,2,1,0:T(8,128)(2,1)S(1)} custom-call(bf16[320,2048]{1,0:T(8,128)(2,1)S(1)} %bitcast.70, bf16[320,2048]{1,0:T(8,128)(2,1)} %collective-permute-done.other_in, bf16[320,2048]{1,0:T(8,128)(2,1)S(1)} %bitcast.72, bf16[320,2048]{1,0:T(8,128)(2,1)S(1)} %copy-done.6, bf16[8,4,64,896]{3,2,1,0:T(8,128)(2,1)S(1)} %bitcast.75), custom_call_target="tpu_custom_call" | custom-call | tf_op jit(solution)/shard_map/step_terms/pallas_call | solution.py:186
  122.2 1.8 copy-done.1
  124.0 54.3 %reduce-scatter.2.cloned.1.call-done = bf16[256,896]{1,0:T(8,128)(2,1)} async-done(((bf16[2048,896]{1,0:T(8,128)(2,1)}), bf16[256,896]{1,0:T(8,128)(2,1)}) %reduce-scatter.2.cloned.1.call-update) | async-done | bytes 458768 | tf_op jit(solution)/shard_map/reduce_scatter | solution.py:104
  178.4 11.7 %all_to_all.40 = bf16[4,64,896]{2,1,0:T(8,128)(2,1)S(1)} all-to-all(bf16[4,64,896]{2,1,0:T(8,128)(2,1)} %bitcast.83), channel_id=1, replica_groups=mesh['x'=4,'z'=8,'y'=8,'core'=2] {'x'}, dimensions={0} | all-to-all | bytes 917504 | tf_op jit(solution)/shard_map/all_to_all | solution.py:42
  190.4 0.9 fusion.14
  191.3 0.5 copy-done.9
  192.1 9.7 %all_to_all.41 = bf16[4,64,896]{2,1,0:T(8,128)(2,1)} all-to-all(bf16[4,64,896]{2,1,0:T(8,128)(2,1)S(1)} %broadcast_in_dim.55), channel_id=1, replica_groups=mesh['x'=4,'z'=8,'y'=8,'core'=2] {'x'}, dimensions={0} | all-to-all | bytes 917504 | tf_op jit(solution)/shard_map/all_to_all | solution.py:42
  202.0 1.2 slice.111
  205.0 36.2 %all_to_all.42 = bf16[8,40,2048]{2,1,0:T(8,128)(2,1)S(1)} all-to-all(bf16[8,40,2048]{2,1,0:T(8,128)(2,1)S(1)} %bitcast.78), channel_id=1, replica_groups=mesh['x'=4,'z'=8,'y'=8,'core'=2] {'y'}, dimensions={0} | all-to-all | bytes 2621440 | tf_op jit(solution)/shard_map/all_to_all | solution.py:42
  241.2 7.4 %collective-permute-start.2 = (bf16[320,2048]{1,0:T(8,128)(2,1)S(1)}, bf16[320,2048]{1,0:T(8,128)(2,1)S(1)}, u32[]{:S(2)}, u32[]{:S(2)}) collective-permute-start(bf16[320,2048]{1,0:T(8,128)(2,1)S(1)} %bitcast.73), channel_id=1, source_target_pairs={{0,1},{1,0},{2,3},{3,2},{4,5},{5,4},{6,7},{7,6},{8,9},{9,8},{10,11... | collective-permute-start | bytes 3932168 | tf_op jit(solution)/shard_map/ppermute | solution.py:38
  248.7 2.5 collective-permute-done.2.taken
  251.1 1.1 copy-done.7
  252.2 1.9 all-gather.8.cloned.1.call-done
  254.1 2.0 copy-done.2
  256.1 1.3 copy-done.8
  257.4 3.5 serve.3
  260.9 2.8 collective-permute-start.3
  263.7 0.9 reshape.132
  264.6 6.9 %all-to-all-start.6 = ((bf16[16,12,864]{2,1,0:T(8,128)(2,1)}), bf16[16,12,864]{2,1,0:T(8,128)(2,1)}, u32[]{:S(2)}, u32[]{:S(2)}) async-start(bf16[16,12,864]{2,1,0:T(8,128)(2,1)} %reshape.132), calls=%async_computation.7 | async-start | bytes 917504 | tf_op jit(solution)/shard_map/all_to_all | solution.py:42
  271.6 15.8 %all-to-all-done.6 = bf16[16,12,864]{2,1,0:T(8,128)(2,1)} async-done(((bf16[16,12,864]{2,1,0:T(8,128)(2,1)}), bf16[16,12,864]{2,1,0:T(8,128)(2,1)}, u32[]{:S(2)}, u32[]{:S(2)}) %all-to-all-start.6) | async-done | bytes 331808 | tf_op jit(solution)/shard_map/all_to_all | solution.py:42
  287.4 2.4 gather_fusion
  289.8 1.9 broadcast_select_fusion
  291.7 4.1 %all-to-all-start.7 = ((bf16[16,12,864]{2,1,0:T(8,128)(2,1)}), bf16[16,12,864]{2,1,0:T(8,128)(2,1)}, u32[]{:S(2)}, u32[]{:S(2)}) async-start(bf16[16,12,864]{2,1,0:T(8,128)(2,1)} %broadcast_select_fusion), calls=%async_computation.8 | async-start | bytes 917504 | tf_op jit(solution)/shard_map/all_to_all | solution.py:42
  295.8 2.0 copy-done.3
  297.9 3.5 serve.2
  301.4 2.9 add_convert_fusion
  304.3 6.5 %all-to-all-done.7 = bf16[16,12,864]{2,1,0:T(8,128)(2,1)} async-done(((bf16[16,12,864]{2,1,0:T(8,128)(2,1)}), bf16[16,12,864]{2,1,0:T(8,128)(2,1)}, u32[]{:S(2)}, u32[]{:S(2)}) %all-to-all-start.7) | async-done | bytes 331808 | tf_op jit(solution)/shard_map/all_to_all | solution.py:42
  310.7 3.6 %all-to-all-start.5 = ((bf16[8,40,2048]{2,1,0:T(8,128)(2,1)}), bf16[8,40,2048]{2,1,0:T(8,128)(2,1)S(1)}, u32[]{:S(2)}, u32[]{:S(2)}) async-start(bf16[8,40,2048]{2,1,0:T(8,128)(2,1)} %bitcast.23), calls=%async_computation.6 | async-start | bytes 2621440 | tf_op jit(solution)/shard_map/all_to_all | solution.py:42
  314.4 1.2 reshape.134
  315.5 0.9 slice_bitcast_fusion
  316.4 32.5 %all-to-all-done.5 = bf16[8,40,2048]{2,1,0:T(8,128)(2,1)S(1)} async-done(((bf16[8,40,2048]{2,1,0:T(8,128)(2,1)}), bf16[8,40,2048]{2,1,0:T(8,128)(2,1)S(1)}, u32[]{:S(2)}, u32[]{:S(2)}) %all-to-all-start.5) | async-done | bytes 1310752 | tf_op jit(solution)/shard_map/all_to_all | solution.py:42
  348.9 1.3 fusion
  (73 shorter events, 2.1 us)
Async XLA Ops:
  7.2 13.2 %copy-start = (bf16[128,2048]{1,0:T(8,128)(2,1)S(1)}, bf16[128,2048]{1,0:T(8,128)(2,1)}, u32[]{:S(2)}) copy-start(bf16[128,2048]{1,0:T(8,128)(2,1)} %param.11) | copy-start | bytes 1572868
  7.2 13.0 %copy-start.21 = (s32[128,1]{0,1:T(1,128)S(1)}, s32[128,1]{0,1:T(1,128)}, u32[]{:S(2)}) copy-start(s32[128,1]{0,1:T(1,128)} %param.13) | copy-start | bytes 1540
  7.2 100.1 %all-gather.6.cloned.1.call-start = ((), (), s32[]{:S(2)}) async-start(), calls=%async_computation.10 | async-start | bytes 4128768 | tf_op jit(solution)/shard_map/all_gather | solution.py:270
  22.0 7.8 %copy-start.13 = (bf16[128,2048]{1,0:T(8,128)(2,1)S(1)}, bf16[128,2048]{1,0:T(8,128)(2,1)}, u32[]{:S(2)}) copy-start(bf16[128,2048]{1,0:T(8,128)(2,1)} %param.12) | copy-start | bytes 1572868
  22.0 7.8 %copy-start.18 = (f32[128,1]{0,1:T(1,128)S(1)}, f32[128,1]{0,1:T(1,128)}, u32[]{:S(2)}) copy-start(f32[128,1]{0,1:T(1,128)} %param.14) | copy-start | bytes 1540
  22.0 39.6 %all-to-all-start = ((bf16[8,40,2048]{2,1,0:T(8,128)(2,1)}), bf16[8,40,2048]{2,1,0:T(8,128)(2,1)S(1)}, u32[]{:S(2)}, u32[]{:S(2)}) async-start(bf16[8,40,2048]{2,1,0:T(8,128)(2,1)} %bitcast.5), calls=%async_computation | async-start | bytes 2621440 | tf_op jit(solution)/shard_map/all_to_all | solution.py:42
  62.9 36.1 %all-to-all-start.2 = ((bf16[8,40,2048]{2,1,0:T(8,128)(2,1)}), bf16[8,40,2048]{2,1,0:T(8,128)(2,1)S(1)}, u32[]{:S(2)}, u32[]{:S(2)}) async-start(bf16[8,40,2048]{2,1,0:T(8,128)(2,1)} %bitcast.77), calls=%async_computation.2 | async-start | bytes 2621440 | tf_op jit(solution)/shard_map/all_to_all | solution.py:42
  66.4 111.9 %reduce-scatter.2.cloned.1.call-start = ((), (), s32[]{:S(2)}) async-start(), calls=%async_computation.9 | async-start | bytes 4128768 | tf_op jit(solution)/shard_map/reduce_scatter | solution.py:104
  66.5 37.1 %collective-permute-start = (bf16[320,2048]{1,0:T(8,128)(2,1)S(1)}, bf16[320,2048]{1,0:T(8,128)(2,1)}, u32[]{:S(2)}, u32[]{:S(2)}) collective-permute-start(bf16[320,2048]{1,0:T(8,128)(2,1)S(1)} %bitcast.69), channel_id=1, source_target_pairs={{0,1},{1,0},{2,3},{3,2},{4,5},{5,4},{6,7},{7,6},{8,9},{9,8},{10,11... | collective-permute-start | bytes 3932168 | tf_op jit(solution)/shard_map/ppermute | solution.py:38
  98.9 7.3 %collective-permute-start.1 = (bf16[320,2048]{1,0:T(8,128)(2,1)S(1)}, bf16[320,2048]{1,0:T(8,128)(2,1)S(1)}, u32[]{:S(2)}, u32[]{:S(2)}) collective-permute-start(bf16[320,2048]{1,0:T(8,128)(2,1)S(1)} %bitcast.71), channel_id=1, source_target_pairs={{0,1},{1,0},{2,3},{3,2},{4,5},{5,4},{6,7},{7,6},{8,9},{9,8},{10,11... | collective-permute-start | bytes 3932168 | tf_op jit(solution)/shard_map/ppermute | solution.py:38
  106.2 1.1 copy-start.5
  107.3 2.0 copy-start.4
  109.4 1.3 copy-start.6
  122.2 1.8 copy-start.1
  124.0 130.1 %all-gather.8.cloned.1.call-start = ((), (), s32[]{:S(2)}) async-start(), calls=%async_computation.11 | async-start | bytes 4128768 | tf_op jit(solution)/shard_map/all_gather | solution.py:112
  178.4 12.0 %copy-start.11 = (f32[1,64,864]{2,1,0:T(8,128)S(1)}, f32[1,64,864]{2,1,0:T(8,128)}, u32[]{:S(2)}) copy-start(f32[1,64,864]{2,1,0:T(8,128)} %param.18) | copy-start | bytes 663556
  178.4 12.0 %copy-start.16 = (f32[1,64,864]{2,1,0:T(8,128)S(1)}, f32[1,64,864]{2,1,0:T(8,128)}, u32[]{:S(2)}) copy-start(f32[1,64,864]{2,1,0:T(8,128)} %param.19) | copy-start | bytes 663556
  178.4 12.0 %copy-start.17 = (f32[1,64,864]{2,1,0:T(8,128)S(1)}, f32[1,64,864]{2,1,0:T(8,128)}, u32[]{:S(2)}) copy-start(f32[1,64,864]{2,1,0:T(8,128)} %param.20) | copy-start | bytes 663556
  191.2 0.6 copy-start.9
  191.3 10.6 %copy-start.20 = (s32[128,1]{0,1:T(1,128)S(1)}, s32[128,1]{0,1:T(1,128)}, u32[]{:S(2)}) copy-start(s32[128,1]{0,1:T(1,128)} %param.16) | copy-start | bytes 1540
  191.3 13.2 %copy-start.12 = (bf16[128,2048]{1,0:T(8,128)(2,1)S(1)}, bf16[128,2048]{1,0:T(8,128)(2,1)}, u32[]{:S(2)}) copy-start(bf16[128,2048]{1,0:T(8,128)(2,1)} %param.15) | copy-start | bytes 1572868
  241.2 9.9 %collective-permute-start.2 = (bf16[320,2048]{1,0:T(8,128)(2,1)S(1)}, bf16[320,2048]{1,0:T(8,128)(2,1)S(1)}, u32[]{:S(2)}, u32[]{:S(2)}) collective-permute-start(bf16[320,2048]{1,0:T(8,128)(2,1)S(1)} %bitcast.73), channel_id=1, source_target_pairs={{0,1},{1,0},{2,3},{3,2},{4,5},{5,4},{6,7},{7,6},{8,9},{9,8},{10,11... | collective-permute-start | bytes 3932168 | tf_op jit(solution)/shard_map/ppermute | solution.py:38
  251.1 1.1 copy-start.7
  254.1 2.0 copy-start.2
  256.1 1.3 copy-start.8
  257.4 6.2 %copy-start.10 = (bf16[64,864]{1,0:T(8,128)(2,1)S(1)}, bf16[64,864]{1,0:T(8,128)(2,1)}, u32[]{:S(2)}) copy-start(bf16[64,864]{1,0:T(8,128)(2,1)} %copy-done.9) | copy-start | bytes 331780
  257.4 6.3 %copy-start.14 = (bf16[64,864]{1,0:T(8,128)(2,1)S(1)}, bf16[64,864]{1,0:T(8,128)(2,1)}, u32[]{:S(2)}) copy-start(bf16[64,864]{1,0:T(8,128)(2,1)} %get-tuple-element.7) | copy-start | bytes 331780
  257.4 6.3 %copy-start.15 = (bf16[64,864]{1,0:T(8,128)(2,1)S(1)}, bf16[64,864]{1,0:T(8,128)(2,1)}, u32[]{:S(2)}) copy-start(bf16[64,864]{1,0:T(8,128)(2,1)} %get-tuple-element.9) | copy-start | bytes 331780
  260.9 10.6 %copy-start.22 = (s32[16]{0:T(128)S(1)}, s32[16]{0:T(128)}, u32[]{:S(2)}) copy-start(s32[16]{0:T(128)} %param.21) | copy-start | bytes 196
  260.9 40.4 %collective-permute-start.3 = (bf16[320,2048]{1,0:T(8,128)(2,1)S(1)}, bf16[320,2048]{1,0:T(8,128)(2,1)}, u32[]{:S(2)}, u32[]{:S(2)}) collective-permute-start(bf16[320,2048]{1,0:T(8,128)(2,1)S(1)} %serve.3), channel_id=1, source_target_pairs={{0,1},{1,0},{2,3},{3,2},{4,5},{5,4},{6,7},{7,6},{8,9},{9,8},{10,11... | collective-permute-start | bytes 3932168 | tf_op jit(solution)/shard_map/ppermute | solution.py:38
  264.6 22.8 %all-to-all-start.6 = ((bf16[16,12,864]{2,1,0:T(8,128)(2,1)}), bf16[16,12,864]{2,1,0:T(8,128)(2,1)}, u32[]{:S(2)}, u32[]{:S(2)}) async-start(bf16[16,12,864]{2,1,0:T(8,128)(2,1)} %reshape.132), calls=%async_computation.7 | async-start | bytes 917504 | tf_op jit(solution)/shard_map/all_to_all | solution.py:42
  291.7 19.0 %all-to-all-start.7 = ((bf16[16,12,864]{2,1,0:T(8,128)(2,1)}), bf16[16,12,864]{2,1,0:T(8,128)(2,1)}, u32[]{:S(2)}, u32[]{:S(2)}) async-start(bf16[16,12,864]{2,1,0:T(8,128)(2,1)} %broadcast_select_fusion), calls=%async_computation.8 | async-start | bytes 917504 | tf_op jit(solution)/shard_map/all_to_all | solution.py:42
  295.8 2.0 copy-start.3
  310.7 38.2 %all-to-all-start.5 = ((bf16[8,40,2048]{2,1,0:T(8,128)(2,1)}), bf16[8,40,2048]{2,1,0:T(8,128)(2,1)S(1)}, u32[]{:S(2)}, u32[]{:S(2)}) async-start(bf16[8,40,2048]{2,1,0:T(8,128)(2,1)} %bitcast.23), calls=%async_computation.6 | async-start | bytes 2621440 | tf_op jit(solution)/shard_map/all_to_all | solution.py:42
  314.3 34.6 %copy-start.19 = (f32[128,1]{0,1:T(1,128)S(1)}, f32[128,1]{0,1:T(1,128)}, u32[]{:S(2)}) copy-start(f32[128,1]{0,1:T(1,128)} %param.17) | copy-start | bytes 1540
Sparse Core Ops, SparseCore 0:
  20.3 60.5 all-gather.5
  124.1 54.2 reduce-scatter.1
  201.9 52.0 all-gather.7
